TPU v7x, 32 devices: a whole 2x2x4 slice. The times are simulated.
32 devices in a mesh: band: 16 (over z, y, x), lev: 2 (over core).
Axes of the slice: x: 2, y: 2, z: 4, core: 2. Of those that a mesh axis runs over, the one named last changes fastest.
Arguments:
- spectral: bfloat16 [1280, 2, 2, 3, 1280], P('band', None, 'lev'), may hold values from -0.08984375 to 0.08984375
- legendre: bfloat16 [1280, 16, 1280], P('band'), may hold values from -0.15625 to 0.15625
- level_weights: float32 [2], P('lev'), may hold values from 0.1 to 0.6
- coupling: int32 [64, 128], P('band'), may hold values from 0 to 8191
- land_sea: int32 [64, 128], P('band'), may hold values 0 or 1
- spectra: bfloat16 [36, 36, 64, 128], P('lev', None, 'band'), may hold values from 0.049804688 to 2
- courant: float32 [36], P('lev'), may hold values from 0.1 to 0.65
- growth_rate: float32 [36], P('lev'), may hold values from 0.05 to 0.5
- breaking: float32 [36], P('lev'), may hold values from 0.1 to 1
Outputs:
- grid: float32 [16, 2, 3, 512], P('band', 'lev')
- spectra_out: float32 [36, 36, 64, 128], P('lev', None, 'band')
- charnock: float32 [64, 128], P('band')
All inputs are finite; a program needn't handle non-finite values. No bound on the sum of `land_sea` on one device may be relied on, other than what follows from the above.
Results may differ from a plain program's by a relative error of at most 0.0029.
Values may be sent and summed in bfloat16 or wider, within the bound.
No kernel may reach another device: no remote copies, remote signals or barrier semaphores. Data moves between devices by JAX's collectives and lax.ppermute only.
A program may use at most 64 MiB of HBM per device.

v0:
```python
import functools
import math

import jax
import jax.numpy as jnp
from jax import lax
from jax.experimental import pallas as pl
from jax.experimental.pallas import tpu as pltpu
from jax.sharding import PartitionSpec as P


NLON = 5136
LON_W = 512
NF = 36
STEPS = 4
FIELDS = 3

VMEM = pl.BlockSpec(memory_space=pltpu.VMEM)
SMEM = pl.BlockSpec(memory_space=pltpu.SMEM)


def swapped(block, axis, apart):
    count = lax.axis_size(axis)
    return lax.ppermute(block, axis, [(i, i ^ (1 << apart)) for i in range(count)])


def bits_of(count):
    bits = count.bit_length() - 1
    return [*range(1, bits), 0] if bits else []


def angles_of(directions):
    return [2.0 * math.pi / directions * (d + 0.5) for d in range(directions)]


def halves(row_low, low, high):
    return jnp.where(row_low, low, high)


def params(mib):
    return pltpu.CompilerParams(vmem_limit_bytes=mib * 2**20)


def pack_kernel(band, spectra, low, high, buffer, sems):
    freqs, half = low.shape[:2]
    odd = band[0] % 2
    chunks = buffer.shape[1]
    span = freqs // chunks
    reads, writes = [], []
    for k, out in enumerate((low, high)):
        first = (odd if k == 0 else 1 - odd) * half
        for c in range(chunks):
            rows = pl.ds(c * span, span)
            held = buffer.at[k, c]
            reads.append(
                pltpu.make_async_copy(spectra.at[rows, pl.ds(first, half)], held, sems.at[0, k, c])
            )
            writes.append(pltpu.make_async_copy(held, out.at[rows], sems.at[1, k, c]))
    for copy in reads:
        copy.start()
    for read, write in zip(reads, writes):
        read.wait()
        write.start()
    for copy in writes:
        copy.wait()


def advect_kernel(
    directions, lev, band, courant, rate, breaking, spectra, low, high, land,
    damped, source, own, held, sems,
):
    freqs = courant.shape[0]
    pairs = directions // 2
    half = pairs // 2
    theta = angles_of(directions)
    odd = band[0] % 2
    chunks = sems.shape[1]
    span = freqs // chunks
    copies = []
    for k in range(chunks):
        whole, part = pl.ds(k * span * pairs, span * pairs), pl.ds(k * span * half, span * half)
        copies.append(
            [
                pltpu.make_async_copy(spectra.at[whole], own.at[whole], sems.at[0, k]),
                pltpu.make_async_copy(low.at[part], held.at[1 - odd, part], sems.at[1, k]),
                pltpu.make_async_copy(high.at[part], held.at[odd, part], sems.at[2, k]),
            ]
        )
        for copy in copies[-1]:
            copy.start()
    source[...] = jnp.zeros_like(source)
    row = lax.broadcasted_iota(jnp.int32, (8, 128), 0)
    row_low = row < 4
    inner_row = row % 4
    land4 = land[...].astype(jnp.float32)
    mask = jnp.concatenate([land4, land4], axis=0)

    def body(f, carry):
        speed = courant[f]
        damp = breaking[f]
        gain = (1.0 + 2.0 * (lev[0] * freqs + f).astype(jnp.float32) / (NF - 1)) * rate[f]
        for j in range(pairs):
            up = j < half
            inner = own[f * pairs + j].astype(jnp.float32)
            outer = held[0 if up else 1, f * half + j % half].astype(jnp.float32)
            cosines = [math.cos(theta[2 * j + k]) for k in range(2)]
            sines = [abs(math.sin(theta[2 * j + k])) for k in range(2)]
            b = speed * halves(row_low, abs(cosines[0]), abs(cosines[1]))
            c = speed * halves(row_low, sines[0], sines[1])
            a = 1.0 - b - c
            c2 = c * c
            weights = (4.0 * c, 6.0 * c2, 4.0 * c2 * c, c2 * c2)

            def west(tile):
                east_side = pltpu.roll(tile, 1, 1) if max(cosines) > 0 else None
                west_side = pltpu.roll(tile, 127, 1) if min(cosines) < 0 else None
                if east_side is None or west_side is None:
                    return west_side if east_side is None else east_side
                return (
                    halves(row_low, east_side, west_side)
                    if cosines[0] > 0
                    else halves(row_low, west_side, east_side)
                )

            state = inner
            for k in range(1, STEPS + 1):
                if k == 4:
                    shifted = outer
                elif up:
                    shifted = jnp.where(
                        inner_row >= k, pltpu.roll(inner, k, 0), pltpu.roll(outer, k + 4, 0)
                    )
                else:
                    shifted = jnp.where(
                        inner_row < 4 - k, pltpu.roll(inner, 8 - k, 0), pltpu.roll(outer, 4 - k, 0)
                    )
                state = a * state + b * west(state) + weights[k - 1] * shifted
            damped[f * pairs + j] = mask * state / (1.0 + damp * state)
            source[j] = source[j] + gain * state
        return carry

    for k in range(chunks):
        for copy in copies[k]:
            copy.wait()
        lax.fori_loop(k * span, (k + 1) * span, body, 0)


def build_basis(cosines, sines, cos_table, sin_table, wave_cos, wave_sin):
    waves = wave_cos.shape[0]
    blocks = cos_table.shape[0] // waves
    tens = waves // 8
    for j in range(tens):
        ca, sa = cosines[blocks + j : blocks + j + 1, :], sines[blocks + j : blocks + j + 1, :]
        cb, sb = cosines[blocks + tens :, :], sines[blocks + tens :, :]
        wave_cos[8 * j : 8 * j + 8, :] = ca * cb - sa * sb
        wave_sin[8 * j : 8 * j + 8, :] = sa * cb + ca * sb

    def body(q, carry):
        ca, sa = cosines[pl.ds(q, 1), :], sines[pl.ds(q, 1), :]
        for j in range(0, waves, 16):
            cb, sb = wave_cos[j : j + 16, :], wave_sin[j : j + 16, :]
            rows = pl.ds(pl.multiple_of(q * waves + j, 16), 16)
            cos_table[rows, :] = (ca * cb - sa * sb).astype(jnp.bfloat16)
            sin_table[rows, :] = -(sa * cb + ca * sb).astype(jnp.bfloat16)
        return carry

    lax.fori_loop(0, blocks, body, 0)


def lanes_of(cells):
    return jnp.concatenate([cells[r : r + 1, :] for r in range(cells.shape[0])], axis=1)


def one_hot(coupling, pick):
    longitude = lanes_of(coupling[...]) % LON_W
    columns = lax.broadcasted_iota(jnp.int32, pick.shape, 0)
    pick[...] = (columns == longitude).astype(jnp.float32).astype(jnp.bfloat16)


def turned(parts, hold):
    at = 0
    for part in parts:
        count = part.shape[0]
        hold[at : at + count, :] = part[...]
        at += count
    return hold[...].T


dot = functools.partial(jnp.dot, preferred_element_type=jnp.float32)


def real_sum(legs, cos_table, sin_table):
    rows = legs.shape[0] // 2
    return dot(legs[:rows], cos_table[...]) + dot(legs[rows:], sin_table[...])


def first_kernel(count, cosines, sines, coupling, *refs):
    parts = refs[:count]
    early, cos_table, sin_table, pick, legs, wave_cos, wave_sin = refs[count:]
    build_basis(cosines, sines, cos_table, sin_table, wave_cos, wave_sin)
    one_hot(coupling, pick)
    early[...] = real_sum(turned(parts, legs), cos_table, sin_table)


def sum_kernel(count, cos_table, sin_table, coupling, *refs):
    parts = refs[:count]
    early, pick, legs = refs[count:]
    one_hot(coupling, pick)
    early[...] = real_sum(turned(parts, legs), cos_table, sin_table)


def fourier_kernel(
    lats, share, band, level, early, last, phase_cos, phase_sin, cos_table, sin_table, pick, coupling,
    grid, wind, hold,
):
    legs = last[...].T
    rows = legs.shape[0] // 2
    by_cos = dot(legs, cos_table[...])
    by_sin = dot(legs, sin_table[...])
    real = by_cos[:rows] + by_sin[rows:]
    imag = by_cos[rows:] - by_sin[:rows]
    fields = early[...] + (phase_cos[...] * real - phase_sin[...] * imag)
    hold[...] = fields
    for f in range(FIELDS):
        grid[f] = hold[pl.ds(f * lats + band[0] * share, share), :]
    speed = fields[: 2 * lats] * level[0]
    top = speed.astype(jnp.bfloat16)
    low = (speed - top.astype(jnp.float32)).astype(jnp.bfloat16)
    found = dot(top, pick[...]) + dot(low, pick[...])
    latitude = lanes_of(coupling[...]) // LON_W
    here = lax.broadcasted_iota(jnp.int32, (lats, latitude.shape[1]), 0) == latitude
    for c in range(2):
        value = jnp.sum(
            jnp.where(here, found[c * lats : (c + 1) * lats], 0.0), axis=0, keepdims=True
        )
        for r in range(wind.shape[1]):
            wind[c, r : r + 1, :] = value[:, r * 128 : (r + 1) * 128]


def result_kernel(directions, parts, rate, damped, land, *refs):
    sources, winds = refs[:parts], refs[parts : 2 * parts]
    result, charnock, stage, sems = refs[2 * parts :]
    freqs = rate.shape[0]
    pairs = directions // 2
    chunks = sems.shape[0]
    span = freqs // chunks
    theta = angles_of(directions)
    row_low = lax.broadcasted_iota(jnp.int32, (8, 128), 0) < 4

    def total(parts_of, index):
        value = parts_of[0][index]
        for part in parts_of[1:]:
            value = value + part[index]
        return value

    east4 = total(winds, 0)
    north4 = total(winds, 1)
    east = jnp.concatenate([east4, east4], axis=0)
    north = jnp.concatenate([north4, north4], axis=0)
    pushes = []
    for j in range(pairs):
        cosines = halves(row_low, math.cos(theta[2 * j]), math.cos(theta[2 * j + 1]))
        sines = halves(row_low, math.sin(theta[2 * j]), math.sin(theta[2 * j + 1]))
        pushes.append(jnp.maximum(cosines * east + sines * north, 0.0))
    copies = []
    for chunk in range(chunks):
        for f in range(chunk * span, (chunk + 1) * span):
            for j in range(pairs):
                value = damped[f * pairs + j]
                stage[f * pairs + j] = value + value * (rate[f] * pushes[j])
        here = pl.ds(chunk * span * pairs, span * pairs)
        copies.append(pltpu.make_async_copy(stage.at[here], result.at[here], sems.at[chunk]))
        copies[-1].start()
    stress = jnp.zeros((8, 128), jnp.float32)
    for j in range(pairs):
        stress = stress + pushes[j] * total(sources, j)
    stress = (stress[0:4] + stress[4:8]) * (land[...].astype(jnp.float32) / (NF * directions))
    charnock[...] = 0.011 + 0.5 * stress / (
        stress + 0.05 * (1.0 + east4 * east4 + north4 * north4)
    )
    for copy in copies:
        copy.wait()


def trig(waves):
    columns = jnp.arange(LON_W, dtype=jnp.int32)
    remains = waves[:, None] * columns[None, :] % NLON
    angles = 2.0 * math.pi / NLON * remains.astype(jnp.float32)
    return jnp.cos(angles), jnp.sin(angles)


def on_device_(
    spectral, legendre, level_weights, coupling, land_sea, spectra, courant, growth_rate, breaking
):
    waves, lats, n_total = legendre.shape
    freqs, directions, tile_rows, tile_cols = spectra.shape
    bands = lax.axis_size("band")
    levs = lax.axis_size("lev")
    band = lax.axis_index("band")
    lev = lax.axis_index("lev")
    share = lats // bands
    pairs = directions // 2
    half = directions // 2

    hbm = pl.BlockSpec(memory_space=pltpu.MemorySpace.HBM)
    in_hbm = functools.partial(
        pltpu.with_memory_space_constraint, memory_space=pltpu.MemorySpace.HBM
    )
    half_shape = pltpu.MemorySpace.HBM((freqs, half, tile_rows, tile_cols), jnp.bfloat16)
    chunks = 3
    low, high = pl.pallas_call(
        pack_kernel,
        out_shape=[half_shape] * 2,
        in_specs=[SMEM, hbm],
        out_specs=[hbm] * 2,
        scratch_shapes=[
            pltpu.VMEM((2, chunks, freqs // chunks, half, tile_rows, tile_cols), jnp.bfloat16),
            pltpu.SemaphoreType.DMA((2, 2, chunks)),
        ],
        compiler_params=params(4),
        name="pack",
    )(band.reshape(1), in_hbm(spectra))
    low = lax.ppermute(low, "band", [(i, i ^ 1) for i in range(bands)])
    across = [(i, i + 1) for i in range(1, bands - 1, 2)]
    high = lax.ppermute(high, "band", across + [(j, i) for i, j in across])

    stacked = spectral.reshape(waves, 2 * FIELDS, n_total)
    legs = lax.dot_general(
        stacked, legendre, (((2,), (2,)), ((0,), (0,))), preferred_element_type=jnp.float32
    ).astype(jnp.bfloat16)
    numbers = band * waves + jnp.arange(waves, dtype=jnp.int32)
    legs = legs.reshape(waves, 2 * FIELDS * lats)
    legs = legs * jnp.where(numbers == 0, 1.0, 2.0).astype(jnp.bfloat16)[:, None]

    order = [0]
    parts = [legs]
    for bit in bits_of(bands):
        together = jnp.concatenate(parts, axis=0) if len(parts) > 1 else legs
        parts = parts + [swapped(together, "band", bit)]
        if bit:
            order = order + [q ^ (1 << bit) for q in order]
    blocks = band ^ jnp.asarray(order, dtype=jnp.int32)

    count = len(parts) - 1
    total = bands * waves // 2
    points = tile_rows * tile_cols
    columns = 2 * FIELDS * lats
    shift = waves * (1 - 2 * (band % 2))
    table = pltpu.VMEM((total, LON_W), jnp.bfloat16)
    pick_shape = jax.ShapeDtypeStruct((LON_W, points), jnp.bfloat16)
    fields_shape = jax.ShapeDtypeStruct((FIELDS * lats, LON_W), jnp.float32)
    legs_scratch = pltpu.VMEM((total, columns), jnp.bfloat16)
    size = 10 if lats <= 32 else 32
    if waves % 16 == 0:
        tens = waves // 8
        listed = [blocks * waves, 8 * jnp.arange(tens, dtype=jnp.int32)]
        cos_rows, sin_rows = trig(jnp.concatenate(listed + [jnp.arange(8, dtype=jnp.int32)]))
        early, cos_table, sin_table, pick = pl.pallas_call(
            functools.partial(first_kernel, count),
            out_shape=[fields_shape, table, table, pick_shape],
            in_specs=[VMEM] * (3 + count),
            out_specs=[VMEM] * 4,
            scratch_shapes=[legs_scratch] + [pltpu.VMEM((waves, LON_W), jnp.float32)] * 2,
            compiler_params=params(size),
            name="first",
        )(cos_rows, sin_rows, coupling, *parts[:-1])
    else:
        cos_table, sin_table = trig(
            (blocks[:, None] * waves + jnp.arange(waves, dtype=jnp.int32)).reshape(-1)
        )
        cos_table, sin_table = cos_table.astype(jnp.bfloat16), -sin_table.astype(jnp.bfloat16)
        early, pick = pl.pallas_call(
            functools.partial(sum_kernel, count),
            out_shape=[fields_shape, pick_shape],
            in_specs=[VMEM] * (3 + count),
            out_specs=[VMEM] * 2,
            scratch_shapes=[legs_scratch],
            compiler_params=params(size),
            name="first",
        )(cos_table, sin_table, coupling, *parts[:-1])
    phase_cos, phase_sin = trig(shift.reshape(1))
    grid, wind = pl.pallas_call(
        functools.partial(fourier_kernel, lats, share),
        out_shape=[
            jax.ShapeDtypeStruct((FIELDS, share, LON_W), jnp.float32),
            jax.ShapeDtypeStruct((2, tile_rows, tile_cols), jnp.float32),
        ],
        in_specs=[SMEM, SMEM] + [VMEM] * 8,
        out_specs=[VMEM] * 2,
        scratch_shapes=[pltpu.VMEM((FIELDS * lats, LON_W), jnp.float32)],
        compiler_params=params(size),
        name="fourier",
    )(
        band.reshape(1), level_weights, early, parts[-1], phase_cos, phase_sin, cos_table, sin_table,
        pick, coupling,
    )
    grid = jnp.transpose(grid, (1, 0, 2)).reshape(share, 1, FIELDS, LON_W)

    tiles = freqs * pairs
    damped, source = pl.pallas_call(
        functools.partial(advect_kernel, directions),
        out_shape=[
            pltpu.VMEM((tiles, 8, 128), jnp.float32),
            pltpu.VMEM((pairs, 8, 128), jnp.float32),
        ],
        in_specs=[SMEM] * 5 + [hbm] * 3 + [VMEM],
        out_specs=[VMEM] * 2,
        scratch_shapes=[
            pltpu.VMEM((tiles, 8, 128), jnp.bfloat16),
            pltpu.VMEM((2, tiles // 2, 8, 128), jnp.bfloat16),
            pltpu.SemaphoreType.DMA((3, chunks)),
        ],
        compiler_params=params(6),
        name="advect",
    )(
        lev.reshape(1),
        band.reshape(1),
        courant,
        growth_rate,
        breaking,
        in_hbm(spectra.reshape(tiles, 8, 128)),
        in_hbm(low.reshape(tiles // 2, 8, 128)),
        in_hbm(high.reshape(tiles // 2, 8, 128)),
        land_sea,
    )

    sources, winds = [source], [wind]
    bit = 0
    while 1 << bit < levs:
        sources = sources + [swapped(s, "lev", bit) for s in sources]
        winds = winds + [swapped(w, "lev", bit) for w in winds]
        bit += 1

    result, charnock = pl.pallas_call(
        functools.partial(result_kernel, directions, levs),
        out_shape=[
            jax.ShapeDtypeStruct((tiles, 8, 128), jnp.float32),
            jax.ShapeDtypeStruct((tile_rows, tile_cols), jnp.float32),
        ],
        in_specs=[SMEM] + [VMEM] * (2 + 2 * levs),
        out_specs=[hbm, VMEM],
        scratch_shapes=[
            pltpu.VMEM((tiles, 8, 128), jnp.float32),
            pltpu.SemaphoreType.DMA((chunks,)),
        ],
        compiler_params=params(6),
        name="result",
    )(growth_rate, damped, land_sea, *sources, *winds)
    return grid, result.reshape(freqs, directions, tile_rows, tile_cols), charnock


def solution(mesh):
    in_specs = (
        P("band", None, "lev", None, None),
        P("band", None, None),
        P("lev"),
        P("band", None),
        P("band", None),
        P("lev", None, "band", None),
        P("lev"),
        P("lev"),
        P("lev"),
    )
    out_specs = (P("band", "lev", None, None), P("lev", None, "band", None), P("band", None))
    return jax.shard_map(
        on_device_, mesh=mesh, in_specs=in_specs, out_specs=out_specs, check_vma=False
    )
```

profile of v0, /device:TPU:0, one launch (start us, length us, event | category | flops | bytes accessed | tf_op | source)
XLA Modules:
  0.0 46.3 jit_solution(3375247144421221329)
XLA Ops:
  0.6 0.0 copy-start
  0.7 1.6 %copy.14 = bf16[80,2,1,3,1280]{4,0,3,1,2:T(8,128)(2,1)S(1)} copy(bf16[80,2,1,3,1280]{4,1,3,2,0:T(2,128)(2,1)} %param.10) | data formatting | bytes 2457600 | tf_op args[0]
  2.2 0.7 %copy-done = bf16[80,16,1280]{2,1,0:T(8,128)(2,1)S(1)} copy-done((bf16[80,16,1280]{2,1,0:T(8,128)(2,1)S(1)}, bf16[80,16,1280]{2,1,0:T(8,128)(2,1)}, u32[]{:S(2)}) %copy-start) | copy-done | bytes 3276824
  2.9 1.2 %fusion.2 = bf16[80,6,16]{2,1,0:T(8,128)(2,1)S(1)} fusion(bf16[80,16,1280]{2,1,0:T(8,128)(2,1)S(1)} %copy-done, bf16[80,6,1280]{2,0,1:T(8,128)(2,1)S(1)} %bitcast.12), kind=kOutput, calls=%fused_computation.2 | convolution fusion | flops 19668480 | bytes 4520960 | tf_op jit(solution)/shard_map/dot_general | solution.py:328
  4.1 0.0 copy-start.6
  4.1 0.0 copy-start.2
  4.1 0.1 copy.16
  4.3 0.1 copy.17
  4.4 0.1 broadcast_multiply_fusion.refs_0_
  4.5 3.0 %collective-permute-start = (bf16[80,96]{1,0:T(8,128)(2,1)S(1)}, bf16[80,96]{1,0:T(8,128)(2,1)S(1)}, u32[]{:S(2)}, u32[]{:S(2)}) collective-permute-start(bf16[80,96]{1,0:T(8,128)(2,1)S(1)} %broadcast_multiply_fusion.refs_0_), channel_id=1, source_target_pairs={{0,4},{2,6},{4,0},{6,2},{8,12},{10,14},{12,8},{14,10},{16,20},{18,... | collective-permute-start | bytes 46088 | tf_op jit(solution)/shard_map/ppermute | solution.py:24
  7.5 1.9 %pack.1 = (bf16[18,18,4,128]{3,2,1,0:T(4,128)(2,1)}, bf16[18,18,4,128]{3,2,1,0:T(4,128)(2,1)}) custom-call(s32[1]{0:T(128)} %bitcast.band, bf16[18,36,4,128]{3,2,1,0:T(4,128)(2,1)} %spectra.1), custom_call_target="tpu_custom_call" | custom-call | tf_op jit(solution)/shard_map/pack/pallas_call | solution.py:311
  9.4 1.6 %collective-permute-start.4 = (bf16[18,18,4,128]{3,2,1,0:T(4,128)(2,1)}, bf16[18,18,4,128]{3,2,1,0:T(4,128)(2,1)}, u32[]{:S(2)}, u32[]{:S(2)}) collective-permute-start(bf16[18,18,4,128]{3,2,1,0:T(4,128)(2,1)} %get-tuple-element.20), channel_id=1, source_target_pairs={{0,2},{2,0},{4,6},{6,4},{8,10},{10,8},{12,14},{14,12},{16,18},{18,... | collective-permute-start | bytes 995336 | tf_op jit(solution)/shard_map/ppermute | solution.py:323
  10.9 1.4 %collective-permute-start.5 = (bf16[18,18,4,128]{3,2,1,0:T(4,128)(2,1)}, bf16[18,18,4,128]{3,2,1,0:T(4,128)(2,1)}, u32[]{:S(2)}, u32[]{:S(2)}) collective-permute-start(bf16[18,18,4,128]{3,2,1,0:T(4,128)(2,1)} %get-tuple-element.21), channel_id=1, source_target_pairs={{2,4},{6,8},{10,12},{14,16},{18,20},{22,24},{26,28},{4,2},{8,6},{1... | collective-permute-start | bytes 995336 | tf_op jit(solution)/shard_map/ppermute | solution.py:325
  12.3 0.0 collective-permute-done.refs_1_
  12.4 2.2 %collective-permute-start.1 = (bf16[160,96]{1,0:T(8,128)(2,1)S(1)}, bf16[160,96]{1,0:T(8,128)(2,1)S(1)}, u32[]{:S(2)}, u32[]{:S(2)}) collective-permute-start(bf16[160,96]{1,0:T(8,128)(2,1)S(1)} %pad_maximum_fusion.2), channel_id=1, source_target_pairs={{0,8},{2,10},{4,12},{6,14},{8,0},{10,2},{12,4},{14,6},{16,24},{18,... | collective-permute-start | bytes 92168 | tf_op jit(solution)/shard_map/ppermute | solution.py:24
  14.6 8.2 %collective-permute-done.1.refs_2_ = bf16[160,96]{1,0:T(8,128)(2,1)S(1)} collective-permute-done((bf16[160,96]{1,0:T(8,128)(2,1)S(1)}, bf16[160,96]{1,0:T(8,128)(2,1)S(1)}, u32[]{:S(2)}, u32[]{:S(2)}) %collective-permute-start.1) | collective-permute-done | bytes 30752 | tf_op jit(solution)/shard_map/ppermute | solution.py:24
  22.8 3.5 %collective-permute-start.2 = (bf16[320,96]{1,0:T(8,128)(2,1)S(1)}, bf16[320,96]{1,0:T(8,128)(2,1)S(1)}, u32[]{:S(2)}, u32[]{:S(2)}) collective-permute-start(bf16[320,96]{1,0:T(8,128)(2,1)S(1)} %pad_maximum_fusion.1), channel_id=1, source_target_pairs={{0,16},{2,18},{4,20},{6,22},{8,24},{10,26},{12,28},{14,30},{16,0},... | collective-permute-start | bytes 184328 | tf_op jit(solution)/shard_map/ppermute | solution.py:24
  26.3 0.1 pad_add_fusion
  26.4 2.3 %collective-permute-done.2.refs_3_ = bf16[320,96]{1,0:T(8,128)(2,1)S(1)} collective-permute-done((bf16[320,96]{1,0:T(8,128)(2,1)S(1)}, bf16[320,96]{1,0:T(8,128)(2,1)S(1)}, u32[]{:S(2)}, u32[]{:S(2)}) %collective-permute-start.2) | collective-permute-done | bytes 61472 | tf_op jit(solution)/shard_map/ppermute | solution.py:24
  28.8 0.7 %pad_maximum_fusion = bf16[640,96]{1,0:T(8,128)(2,1)} fusion(bf16[320,96]{1,0:T(8,128)(2,1)S(1)} %collective-permute-done.2.refs_3_, bf16[160,96]{1,0:T(8,128)(2,1)S(1)} %collective-permute-done.1.refs_2_, bf16[80,96]{1,0:T(8,128)(2,1)S(1)} %collective-permute-done.refs_1_, bf16[80,96]{1,0:T(8,128)(2,1)S(1)} %broadcast_multiply_fusion.refs_0_), kind=kLoop, calls=%fused_computation.3 | loop fusion | flops 491520 | bytes 245760 | tf_op jit(solution)/shard_map/concatenate | solution.py:338
  29.5 0.0 collective-permute-start.3
  29.5 1.0 %fusion.9 = (f32[26,512]{1,0:T(8,128)S(1)}, f32[26,512]{1,0:T(8,128)}) fusion(s32[26]{0:T(128)S(1)} %pad_add_fusion), kind=kLoop, calls=%fused_computation.11 | loop fusion | flops 119808 | bytes 106600 | tf_op jit(solution)/shard_map/sin | solution.py:289
  31.2 7.5 %advect.1 = (f32[324,8,128]{2,1,0:T(8,128)S(1)}, f32[18,8,128]{2,1,0:T(8,128)S(1)}) custom-call(s32[1]{0:T(128)} %bitcast.5.lev, s32[1]{0:T(128)} %bitcast.band, f32[18]{0:T(128)S(1)} %copy-done.5, f32[18]{0:T(128)S(1)} %copy-done.4, f32[18]{0:T(128)S(1)} %copy-done.6, bf16[324,8,128]{2,1,0:T(8,128)(2,1)} %bitcast.13, bf16[162,8,128]{2,1,0:T(8,128)(2,1)} %bitcast.7.low, ...), custom_call_target="tpu_custom_call" | custom-call | tf_op jit(solution)/shard_map/advect/pallas_call | solution.py:400
  38.6 0.1 collective-permute-start.6
  38.7 0.1 fusion.14
  38.8 0.8 %copy-done.1 = f32[26,512]{1,0:T(8,128)S(1)} copy-done((f32[26,512]{1,0:T(8,128)S(1)}, f32[26,512]{1,0:T(8,128)}, u32[]{:S(2)}) %copy-start.1) | copy-done | bytes 53272
  39.7 1.0 %first.1 = (f32[48,512]{1,0:T(8,128)S(1)}, bf16[640,512]{1,0:T(8,128)(2,1)S(1)}, bf16[640,512]{1,0:T(8,128)(2,1)S(1)}, bf16[512,512]{1,0:T(8,128)(2,1)S(1)}) custom-call(f32[26,512]{1,0:T(8,128)S(1)} %copy-done.1, f32[26,512]{1,0:T(8,128)S(1)} %get-tuple-element.33.sines, s32[4,128]{1,0:T(4,128)S(1)} %copy-done.2, ...), custom_call_target="tpu_custom_call" | custom-call | tf_op jit(solution)/shard_map/first/pallas_call | solution.py:358
  40.7 0.0 collective-permute-done.3.last
  40.7 2.0 %fourier.1 = (f32[3,1,512]{2,1,0:T(1,128)}, f32[2,4,128]{2,1,0:T(4,128)S(1)}) custom-call(s32[1]{0:T(128)} %bitcast.band, f32[1]{0:T(128)S(6)} %copy.23.level, f32[48,512]{1,0:T(8,128)S(1)} %get-tuple-element.15.early, bf16[640,96]{1,0:T(8,128)(2,1)} %collective-permute-done.3.last, f32[1,512]{1,0:T(1,128)S(1)} %get-tuple-element.36.phase_cos, ...), custom_call_target="tpu_custom_call" | custom-call | tf_op jit(solution)/shard_map/fourier/pallas_call | solution.py:382
  42.7 0.5 %collective-permute-start.7 = (f32[2,4,128]{2,1,0:T(4,128)S(1)}, f32[2,4,128]{2,1,0:T(4,128)S(1)}, u32[]{:S(2)}, u32[]{:S(2)}) collective-permute-start(f32[2,4,128]{2,1,0:T(4,128)S(1)} %get-tuple-element.24.refs_2_), channel_id=1, source_target_pairs={{0,1},{1,0},{2,3},{3,2},{4,5},{5,4},{6,7},{7,6},{8,9},{9,8},{10,11... | collective-permute-start | bytes 12296 | tf_op jit(solution)/shard_map/ppermute | solution.py:24
  43.2 0.8 %collective-permute-done.7.refs_3_ = f32[2,4,128]{2,1,0:T(4,128)S(1)} collective-permute-done((f32[2,4,128]{2,1,0:T(4,128)S(1)}, f32[2,4,128]{2,1,0:T(4,128)S(1)}, u32[]{:S(2)}, u32[]{:S(2)}) %collective-permute-start.7) | collective-permute-done | bytes 4128 | tf_op jit(solution)/shard_map/ppermute | solution.py:24
  44.0 2.3 %result.1 = (f32[324,8,128]{2,1,0:T(8,128)}, f32[4,128]{1,0:T(4,128)}) custom-call(f32[18]{0:T(128)S(1)} %copy-done.4, f32[324,8,128]{2,1,0:T(8,128)S(1)} %get-tuple-element.22.damped, s32[4,128]{1,0:T(4,128)S(1)} %copy-done.3, f32[18,8,128]{2,1,0:T(8,128)S(1)} %get-tuple-element.23.refs_0_, f32[18,8,128]{2,1,0:T(8,128)S(1)} %collective-permute-done.6.refs_1_, ...), custom_call_target="tpu_custom_call" | custom-call | tf_op jit(solution)/shard_map/result/pallas_call | solution.py:434
  (18 shorter events, 0.1 us)
Async XLA Ops:
  0.6 2.3 %copy-start = (bf16[80,16,1280]{2,1,0:T(8,128)(2,1)S(1)}, bf16[80,16,1280]{2,1,0:T(8,128)(2,1)}, u32[]{:S(2)}) copy-start(bf16[80,16,1280]{2,1,0:T(8,128)(2,1)} %param.11) | copy-start | bytes 9830404
  4.1 27.0 %copy-start.3 = (s32[4,128]{1,0:T(4,128)S(1)}, s32[4,128]{1,0:T(4,128)}, u32[]{:S(2)}) copy-start(s32[4,128]{1,0:T(4,128)} %land.3) | copy-start | bytes 6148
  4.1 27.0 %copy-start.4 = (f32[18]{0:T(128)S(1)}, f32[18]{0:T(128)}, u32[]{:S(2)}) copy-start(f32[18]{0:T(128)} %rate.3) | copy-start | bytes 220
  4.1 27.0 %copy-start.5 = (f32[18]{0:T(128)S(1)}, f32[18]{0:T(128)}, u32[]{:S(2)}) copy-start(f32[18]{0:T(128)} %courant.1) | copy-start | bytes 220
  4.1 27.1 %copy-start.6 = (f32[18]{0:T(128)S(1)}, f32[18]{0:T(128)}, u32[]{:S(2)}) copy-start(f32[18]{0:T(128)} %breaking.1) | copy-start | bytes 220
  4.1 34.7 %copy-start.2 = (s32[4,128]{1,0:T(4,128)S(1)}, s32[4,128]{1,0:T(4,128)}, u32[]{:S(2)}) copy-start(s32[4,128]{1,0:T(4,128)} %coupling.3) | copy-start | bytes 6148
  4.5 7.9 %collective-permute-start = (bf16[80,96]{1,0:T(8,128)(2,1)S(1)}, bf16[80,96]{1,0:T(8,128)(2,1)S(1)}, u32[]{:S(2)}, u32[]{:S(2)}) collective-permute-start(bf16[80,96]{1,0:T(8,128)(2,1)S(1)} %broadcast_multiply_fusion.refs_0_), channel_id=1, source_target_pairs={{0,4},{2,6},{4,0},{6,2},{8,12},{10,14},{12,8},{14,10},{16,20},{18,... | collective-permute-start | bytes 46088 | tf_op jit(solution)/shard_map/ppermute | solution.py:24
  9.4 21.7 %collective-permute-start.4 = (bf16[18,18,4,128]{3,2,1,0:T(4,128)(2,1)}, bf16[18,18,4,128]{3,2,1,0:T(4,128)(2,1)}, u32[]{:S(2)}, u32[]{:S(2)}) collective-permute-start(bf16[18,18,4,128]{3,2,1,0:T(4,128)(2,1)} %get-tuple-element.20), channel_id=1, source_target_pairs={{0,2},{2,0},{4,6},{6,4},{8,10},{10,8},{12,14},{14,12},{16,18},{18,... | collective-permute-start | bytes 995336 | tf_op jit(solution)/shard_map/ppermute | solution.py:323
  10.9 20.2 %collective-permute-start.5 = (bf16[18,18,4,128]{3,2,1,0:T(4,128)(2,1)}, bf16[18,18,4,128]{3,2,1,0:T(4,128)(2,1)}, u32[]{:S(2)}, u32[]{:S(2)}) collective-permute-start(bf16[18,18,4,128]{3,2,1,0:T(4,128)(2,1)} %get-tuple-element.21), channel_id=1, source_target_pairs={{2,4},{6,8},{10,12},{14,16},{18,20},{22,24},{26,28},{4,2},{8,6},{1... | collective-permute-start | bytes 995336 | tf_op jit(solution)/shard_map/ppermute | solution.py:325
  12.4 10.4 %collective-permute-start.1 = (bf16[160,96]{1,0:T(8,128)(2,1)S(1)}, bf16[160,96]{1,0:T(8,128)(2,1)S(1)}, u32[]{:S(2)}, u32[]{:S(2)}) collective-permute-start(bf16[160,96]{1,0:T(8,128)(2,1)S(1)} %pad_maximum_fusion.2), channel_id=1, source_target_pairs={{0,8},{2,10},{4,12},{6,14},{8,0},{10,2},{12,4},{14,6},{16,24},{18,... | collective-permute-start | bytes 92168 | tf_op jit(solution)/shard_map/ppermute | solution.py:24
  22.8 6.0 %collective-permute-start.2 = (bf16[320,96]{1,0:T(8,128)(2,1)S(1)}, bf16[320,96]{1,0:T(8,128)(2,1)S(1)}, u32[]{:S(2)}, u32[]{:S(2)}) collective-permute-start(bf16[320,96]{1,0:T(8,128)(2,1)S(1)} %pad_maximum_fusion.1), channel_id=1, source_target_pairs={{0,16},{2,18},{4,20},{6,22},{8,24},{10,26},{12,28},{14,30},{16,0},... | collective-permute-start | bytes 184328 | tf_op jit(solution)/shard_map/ppermute | solution.py:24
  29.5 11.2 %collective-permute-start.3 = (bf16[640,96]{1,0:T(8,128)(2,1)}, bf16[640,96]{1,0:T(8,128)(2,1)}, u32[]{:S(2)}, u32[]{:S(2)}) collective-permute-start(bf16[640,96]{1,0:T(8,128)(2,1)} %pad_maximum_fusion), channel_id=1, source_target_pairs={{0,2},{2,0},{4,6},{6,4},{8,10},{10,8},{12,14},{14,12},{16,18},{18,... | collective-permute-start | bytes 368648 | tf_op jit(solution)/shard_map/ppermute | solution.py:24
  38.6 5.4 %collective-permute-start.6 = (f32[18,8,128]{2,1,0:T(8,128)S(1)}, f32[18,8,128]{2,1,0:T(8,128)S(1)}, u32[]{:S(2)}, u32[]{:S(2)}) collective-permute-start(f32[18,8,128]{2,1,0:T(8,128)S(1)} %get-tuple-element.23.refs_0_), channel_id=1, source_target_pairs={{0,1},{1,0},{2,3},{3,2},{4,5},{5,4},{6,7},{7,6},{8,9},{9,8},{10,11... | collective-permute-start | bytes 221192 | tf_op jit(solution)/shard_map/ppermute | solution.py:24
  38.8 0.8 %copy-start.1 = (f32[26,512]{1,0:T(8,128)S(1)}, f32[26,512]{1,0:T(8,128)}, u32[]{:S(2)}) copy-start(f32[26,512]{1,0:T(8,128)} %get-tuple-element.34.cosines) | copy-start | bytes 159748
  42.7 1.3 %collective-permute-start.7 = (f32[2,4,128]{2,1,0:T(4,128)S(1)}, f32[2,4,128]{2,1,0:T(4,128)S(1)}, u32[]{:S(2)}, u32[]{:S(2)}) collective-permute-start(f32[2,4,128]{2,1,0:T(4,128)S(1)} %get-tuple-element.24.refs_2_), channel_id=1, source_target_pairs={{0,1},{1,0},{2,3},{3,2},{4,5},{5,4},{6,7},{7,6},{8,9},{9,8},{10,11... | collective-permute-start | bytes 12296 | tf_op jit(solution)/shard_map/ppermute | solution.py:24
where the time goes:
time: 46.6 us; the launch traced here: 46.3 us
  Pallas kernels  14.7 us (32%)
  starting transfers between devices  12.2 us (26%)
  waiting for transfers between devices  11.4 us (24%)
  local copies, waits for them, and re-layouts  3.38 us (7%)
  other arithmetic  1.98 us (4%)
  between operations  1.46 us (3%)
  matrix products  1.17 us (3%)
    ppermute x6, waiting for transfers between devices, swapped(): lax.ppermute(block, axis, [(i, i ^ 1 << apart) for i in range(count)])  11.4 us
    ppermute x6, starting transfers between devices, swapped(): lax.ppermute(block, axis, [(i, i ^ 1 << apart) for i in range(count)])  9.29 us
    pallas_call x1, Pallas kernels, on_device_(): pl.pallas_call(functools.partial(advect_kernel, directions), out_shape=[p...  7.47 us
    unnamed x15, local copies, waits for them, and re-layouts  3.15 us
    pallas_call x1, Pallas kernels, on_device_(): pl.pallas_call(functools.partial(result_kernel, directions, levs), out_sh...  2.26 us
    pallas_call x1, Pallas kernels, on_device_(): pl.pallas_call(functools.partial(fourier_kernel, lats, share), out_shape=...  1.99 us
    pallas_call x1, Pallas kernels, on_device_(): pl.pallas_call(pack_kernel, out_shape=[half_shape] * 2, in_specs=[SMEM, h...  1.91 us
    ppermute x1, starting transfers between devices, on_device_(): low = lax.ppermute(low, 'band', [(i, i ^ 1) for i in range(bands)])  1.56 us
  transfers between devices with their start and end apart: 8, of which 3 were waited for; matrix products, arithmetic and copies ran while one was open for 4% of the time, Pallas kernels for 27%

commit v1 on v0

--- a/solution.py
+++ b/solution.py
@@ -25,8 +25,7 @@
 
 
 def bits_of(count):
-    bits = count.bit_length() - 1
-    return [*range(1, bits), 0] if bits else []
+    return list(range(count.bit_length() - 1))
 
 
 def angles_of(directions):
@@ -66,44 +65,42 @@
 
 
 def advect_kernel(
-    directions, lev, band, courant, rate, breaking, spectra, low, high, land,
-    damped, source, own, held, sems,
+    directions, lev, up, courant, rate, breaking, spectra, halo, land, *refs
 ):
+    (damped, source, own, outside, sems) = refs[-5:]
     freqs = courant.shape[0]
-    pairs = directions // 2
-    half = pairs // 2
+    half = directions // 4
     theta = angles_of(directions)
-    odd = band[0] % 2
     chunks = sems.shape[1]
     span = freqs // chunks
     copies = []
     for k in range(chunks):
-        whole, part = pl.ds(k * span * pairs, span * pairs), pl.ds(k * span * half, span * half)
+        rows = pl.ds(k * span, span)
+        inside = spectra.at[rows, pl.ds((1 - up[0]) * half, half)]
         copies.append(
             [
-                pltpu.make_async_copy(spectra.at[whole], own.at[whole], sems.at[0, k]),
-                pltpu.make_async_copy(low.at[part], held.at[1 - odd, part], sems.at[1, k]),
-                pltpu.make_async_copy(high.at[part], held.at[odd, part], sems.at[2, k]),
+                pltpu.make_async_copy(inside, own.at[rows], sems.at[0, k]),
+                pltpu.make_async_copy(halo.at[rows], outside.at[rows], sems.at[1, k]),
             ]
         )
         for copy in copies[-1]:
             copy.start()
-    source[...] = jnp.zeros_like(source)
     row = lax.broadcasted_iota(jnp.int32, (8, 128), 0)
     row_low = row < 4
     inner_row = row % 4
     land4 = land[...].astype(jnp.float32)
     mask = jnp.concatenate([land4, land4], axis=0)
-
-    def body(f, carry):
+    source[...] = jnp.zeros_like(source)
+
+    def body(f, carry, rising):
         speed = courant[f]
         damp = breaking[f]
         gain = (1.0 + 2.0 * (lev[0] * freqs + f).astype(jnp.float32) / (NF - 1)) * rate[f]
-        for j in range(pairs):
-            up = j < half
-            inner = own[f * pairs + j].astype(jnp.float32)
-            outer = held[0 if up else 1, f * half + j % half].astype(jnp.float32)
-            cosines = [math.cos(theta[2 * j + k]) for k in range(2)]
+        for j in range(half):
+            inner = own[f, j].astype(jnp.float32)
+            outer = outside[f, j].astype(jnp.float32)
+            signs = [1 if rising else -1] * 2
+            cosines = [signs[k] * math.cos(theta[2 * j + k]) for k in range(2)]
             sines = [abs(math.sin(theta[2 * j + k])) for k in range(2)]
             b = speed * halves(row_low, abs(cosines[0]), abs(cosines[1]))
             c = speed * halves(row_low, sines[0], sines[1])
@@ -111,22 +108,22 @@
             c2 = c * c
             weights = (4.0 * c, 6.0 * c2, 4.0 * c2 * c, c2 * c2)
 
-            def west(tile):
-                east_side = pltpu.roll(tile, 1, 1) if max(cosines) > 0 else None
-                west_side = pltpu.roll(tile, 127, 1) if min(cosines) < 0 else None
-                if east_side is None or west_side is None:
-                    return west_side if east_side is None else east_side
+            def upwind(tile):
+                from_west = pltpu.roll(tile, 1, 1) if max(cosines) > 0 else None
+                from_east = pltpu.roll(tile, 127, 1) if min(cosines) < 0 else None
+                if from_west is None or from_east is None:
+                    return from_east if from_west is None else from_west
                 return (
-                    halves(row_low, east_side, west_side)
+                    halves(row_low, from_west, from_east)
                     if cosines[0] > 0
-                    else halves(row_low, west_side, east_side)
+                    else halves(row_low, from_east, from_west)
                 )
 
             state = inner
             for k in range(1, STEPS + 1):
                 if k == 4:
                     shifted = outer
-                elif up:
+                elif rising:
                     shifted = jnp.where(
                         inner_row >= k, pltpu.roll(inner, k, 0), pltpu.roll(outer, k + 4, 0)
                     )
@@ -134,15 +131,21 @@
                     shifted = jnp.where(
                         inner_row < 4 - k, pltpu.roll(inner, 8 - k, 0), pltpu.roll(outer, 4 - k, 0)
                     )
-                state = a * state + b * west(state) + weights[k - 1] * shifted
-            damped[f * pairs + j] = mask * state / (1.0 + damp * state)
+                state = a * state + b * upwind(state) + weights[k - 1] * shifted
+            damped[f, j] = mask * state / (1.0 + damp * state)
             source[j] = source[j] + gain * state
         return carry
 
     for k in range(chunks):
         for copy in copies[k]:
             copy.wait()
-        lax.fori_loop(k * span, (k + 1) * span, body, 0)
+        for rising in (True, False):
+
+            @pl.when(up[0] == int(rising))
+            def _(k=k, rising=rising):
+                lax.fori_loop(
+                    k * span, (k + 1) * span, functools.partial(body, rising=rising), 0
+                )
 
 
 def build_basis(cosines, sines, cos_table, sin_table, wave_cos, wave_sin):
@@ -237,49 +240,68 @@
             wind[c, r : r + 1, :] = value[:, r * 128 : (r + 1) * 128]
 
 
-def result_kernel(directions, parts, rate, damped, land, *refs):
-    sources, winds = refs[:parts], refs[parts : 2 * parts]
-    result, charnock, stage, sems = refs[2 * parts :]
-    freqs = rate.shape[0]
-    pairs = directions // 2
-    chunks = sems.shape[0]
-    span = freqs // chunks
+def total(parts, index):
+    value = parts[0][index]
+    for part in parts[1:]:
+        value = value + part[index]
+    return value
+
+
+def pushes_of(directions, winds, sign):
+    half = directions // 4
     theta = angles_of(directions)
     row_low = lax.broadcasted_iota(jnp.int32, (8, 128), 0) < 4
-
-    def total(parts_of, index):
-        value = parts_of[0][index]
-        for part in parts_of[1:]:
-            value = value + part[index]
-        return value
-
     east4 = total(winds, 0)
     north4 = total(winds, 1)
-    east = jnp.concatenate([east4, east4], axis=0)
-    north = jnp.concatenate([north4, north4], axis=0)
+    east = sign * jnp.concatenate([east4, east4], axis=0)
+    north = sign * jnp.concatenate([north4, north4], axis=0)
     pushes = []
-    for j in range(pairs):
+    for j in range(half):
         cosines = halves(row_low, math.cos(theta[2 * j]), math.cos(theta[2 * j + 1]))
         sines = halves(row_low, math.sin(theta[2 * j]), math.sin(theta[2 * j + 1]))
         pushes.append(jnp.maximum(cosines * east + sines * north, 0.0))
+    return pushes, east4, north4
+
+
+def sign_of(up):
+    return (2 * up - 1).astype(jnp.float32)
+
+
+def result_kernel(directions, parts, up, rate, damped, *refs):
+    winds = refs[:parts]
+    result, stage, sems = refs[-3:]
+    half = directions // 4
+    chunks = sems.shape[0]
+    span = rate.shape[0] // chunks
+    pushes, _, _ = pushes_of(directions, winds, sign_of(up[0]))
     copies = []
     for chunk in range(chunks):
         for f in range(chunk * span, (chunk + 1) * span):
-            for j in range(pairs):
-                value = damped[f * pairs + j]
-                stage[f * pairs + j] = value + value * (rate[f] * pushes[j])
-        here = pl.ds(chunk * span * pairs, span * pairs)
-        copies.append(pltpu.make_async_copy(stage.at[here], result.at[here], sems.at[chunk]))
+            for j in range(half):
+                value = damped[f, j]
+                stage[f, j] = value + value * (rate[f] * pushes[j])
+        rows = pl.ds(chunk * span, span)
+        there = result.at[rows, pl.ds((1 - up[0]) * half, half)]
+        copies.append(pltpu.make_async_copy(stage.at[rows], there, sems.at[chunk]))
         copies[-1].start()
+    for copy in copies:
+        copy.wait()
+
+
+def charnock_kernel(directions, parts, up, land, *refs):
+    winds, first, second, charnock = (
+        refs[:parts], refs[parts : 2 * parts], refs[2 * parts : 3 * parts], refs[3 * parts],
+    )
+    sign = sign_of(up[0])
     stress = jnp.zeros((8, 128), jnp.float32)
-    for j in range(pairs):
-        stress = stress + pushes[j] * total(sources, j)
+    for sources, way in ((first, sign), (second, -sign)):
+        pushes, east, north = pushes_of(directions, winds, way)
+        for j, push in enumerate(pushes):
+            stress = stress + push * total(sources, j)
     stress = (stress[0:4] + stress[4:8]) * (land[...].astype(jnp.float32) / (NF * directions))
     charnock[...] = 0.011 + 0.5 * stress / (
-        stress + 0.05 * (1.0 + east4 * east4 + north4 * north4)
+        stress + 0.05 * (1.0 + east * east + north * north)
     )
-    for copy in copies:
-        copy.wait()
 
 
 def trig(waves):
@@ -337,7 +359,7 @@
     for bit in bits_of(bands):
         together = jnp.concatenate(parts, axis=0) if len(parts) > 1 else legs
         parts = parts + [swapped(together, "band", bit)]
-        if bit:
+        if 2 << bit < bands:
             order = order + [q ^ (1 << bit) for q in order]
     blocks = band ^ jnp.asarray(order, dtype=jnp.int32)
 
@@ -345,7 +367,7 @@
     total = bands * waves // 2
     points = tile_rows * tile_cols
     columns = 2 * FIELDS * lats
-    shift = waves * (1 - 2 * (band % 2))
+    shift = total * (1 - 2 * (band // (bands // 2)))
     table = pltpu.VMEM((total, LON_W), jnp.bfloat16)
     pick_shape = jax.ShapeDtypeStruct((LON_W, points), jnp.bfloat16)
     fields_shape = jax.ShapeDtypeStruct((FIELDS * lats, LON_W), jnp.float32)
@@ -396,56 +418,67 @@
     )
     grid = jnp.transpose(grid, (1, 0, 2)).reshape(share, 1, FIELDS, LON_W)
 
-    tiles = freqs * pairs
-    damped, source = pl.pallas_call(
-        functools.partial(advect_kernel, directions),
-        out_shape=[
-            pltpu.VMEM((tiles, 8, 128), jnp.float32),
-            pltpu.VMEM((pairs, 8, 128), jnp.float32),
-        ],
-        in_specs=[SMEM] * 5 + [hbm] * 3 + [VMEM],
-        out_specs=[VMEM] * 2,
-        scratch_shapes=[
-            pltpu.VMEM((tiles, 8, 128), jnp.bfloat16),
-            pltpu.VMEM((2, tiles // 2, 8, 128), jnp.bfloat16),
-            pltpu.SemaphoreType.DMA((3, chunks)),
-        ],
-        compiler_params=params(6),
-        name="advect",
-    )(
-        lev.reshape(1),
-        band.reshape(1),
-        courant,
-        growth_rate,
-        breaking,
-        in_hbm(spectra.reshape(tiles, 8, 128)),
-        in_hbm(low.reshape(tiles // 2, 8, 128)),
-        in_hbm(high.reshape(tiles // 2, 8, 128)),
-        land_sea,
-    )
-
-    sources, winds = [source], [wind]
-    bit = 0
-    while 1 << bit < levs:
-        sources = sources + [swapped(s, "lev", bit) for s in sources]
-        winds = winds + [swapped(w, "lev", bit) for w in winds]
-        bit += 1
-
-    result, charnock = pl.pallas_call(
-        functools.partial(result_kernel, directions, levs),
-        out_shape=[
-            jax.ShapeDtypeStruct((tiles, 8, 128), jnp.float32),
-            jax.ShapeDtypeStruct((tile_rows, tile_cols), jnp.float32),
-        ],
-        in_specs=[SMEM] + [VMEM] * (2 + 2 * levs),
-        out_specs=[hbm, VMEM],
-        scratch_shapes=[
-            pltpu.VMEM((tiles, 8, 128), jnp.float32),
-            pltpu.SemaphoreType.DMA((chunks,)),
-        ],
-        compiler_params=params(6),
-        name="result",
-    )(growth_rate, damped, land_sea, *sources, *winds)
+    quarter = pairs // 2
+    odd = band % 2
+    levels = lev.reshape(1)
+    own = in_hbm(spectra.reshape(freqs, pairs, 8, 128))
+    half_state = pltpu.VMEM((freqs, quarter, 8, 128), jnp.float32)
+
+    def advected(halo, up):
+        return pl.pallas_call(
+            functools.partial(advect_kernel, directions),
+            out_shape=[half_state, pltpu.VMEM((quarter, 8, 128), jnp.float32)],
+            in_specs=[SMEM] * 5 + [hbm] * 2 + [VMEM],
+            out_specs=[VMEM] * 2,
+            scratch_shapes=[
+                pltpu.VMEM((freqs, quarter, 8, 128), jnp.bfloat16),
+                pltpu.VMEM((freqs, quarter, 8, 128), jnp.bfloat16),
+                pltpu.SemaphoreType.DMA((2, chunks)),
+            ],
+            compiler_params=params(4),
+        )(
+            levels, up, courant, growth_rate, breaking, own,
+            in_hbm(halo.reshape(freqs, quarter, 8, 128)), land_sea,
+        )
+
+    def over_lev(value):
+        parts = [value]
+        bit = 0
+        while 1 << bit < levs:
+            parts = parts + [swapped(part, "lev", bit) for part in parts]
+            bit += 1
+        return parts
+
+    def forced(damped, up, *earlier):
+        return pl.pallas_call(
+            functools.partial(result_kernel, directions, levs),
+            out_shape=pltpu.MemorySpace.HBM((freqs, pairs, 8, 128), jnp.float32),
+            in_specs=[SMEM] * 2 + [VMEM] * (1 + levs) + [hbm] * len(earlier),
+            out_specs=hbm,
+            scratch_shapes=[
+                pltpu.VMEM((freqs, quarter, 8, 128), jnp.float32),
+                pltpu.SemaphoreType.DMA((chunks,)),
+            ],
+            input_output_aliases={3 + levs: 0} if earlier else {},
+            compiler_params=params(4),
+        )(up, growth_rate, damped, *winds, *earlier)
+
+    near_up, far_up = odd.reshape(1), (1 - odd).reshape(1)
+    winds = over_lev(wind)
+    damped, source = advected(low, near_up)
+    near_sources = over_lev(source)
+    result = forced(damped, near_up)
+    damped, source = advected(high, far_up)
+    far_sources = over_lev(source)
+    result = forced(damped, far_up, result)
+    charnock = pl.pallas_call(
+        functools.partial(charnock_kernel, directions, levs),
+        out_shape=jax.ShapeDtypeStruct((tile_rows, tile_cols), jnp.float32),
+        in_specs=[SMEM] + [VMEM] * (1 + 3 * levs),
+        out_specs=VMEM,
+        compiler_params=params(2),
+        name="charnock",
+    )(near_up, land_sea, *winds, *near_sources, *far_sources)
     return grid, result.reshape(freqs, directions, tile_rows, tile_cols), charnock
 
 

time: 46.6 us -> 56 us (1.20)
  Pallas kernels: 14.7 us -> 22.7 us
  starting transfers between devices: 12.2 us -> 17.2 us
  waiting for transfers between devices: 11.4 us -> 8.67 us
  local copies, waits for them, and re-layouts: 3.38 us -> 2.54 us
    pallas_call x2 -> x5, Pallas kernels: 9.73 us -> 17.8 us  [the longest x2 14.3 us: advected(): pl.pallas_call(functools.partial(advect_kernel, directions), out_shape=[h...]
    ppermute x6 -> x7, starting transfers between devices: 9.29 us -> 12.2 us  [swapped(): lax.ppermute(block, axis, [(i, i ^ 1 << apart) for i in range(count)])]
    ppermute x6 -> x7, waiting for transfers between devices: 11.4 us -> 8.67 us  [swapped(): lax.ppermute(block, axis, [(i, i ^ 1 << apart) for i in range(count)])]
    ppermute x1, starting transfers between devices: 1.56 us -> 3.56 us  [on_device_(): low = lax.ppermute(low, 'band', [(i, i ^ 1) for i in range(bands)])]
    unnamed x15, local copies, waits for them, and re-layouts: 3.15 us -> 2.3 us
  transfers between devices with their start and end apart: 8 -> 9, of which waited for: 3 -> 3; matrix products, arithmetic and copies ran while one was open for 4% -> 3% of each run, Pallas kernels for 27% -> 40%
where the time goes in v1:
time: 56 us; the launch traced here: 55.7 us
  Pallas kernels  22.7 us (41%)
  starting transfers between devices  17.2 us (31%)
  waiting for transfers between devices  8.67 us (15%)
  local copies, waits for them, and re-layouts  2.54 us (5%)
  other arithmetic  1.96 us (4%)
  between operations  1.47 us (3%)
  matrix products  1.17 us (2%)
    pallas_call x2, Pallas kernels, advected(): pl.pallas_call(functools.partial(advect_kernel, directions), out_shape=[h...  14.3 us
    ppermute x7, starting transfers between devices, swapped(): lax.ppermute(block, axis, [(i, i ^ 1 << apart) for i in range(count)])  12.2 us
    ppermute x7, waiting for transfers between devices, swapped(): lax.ppermute(block, axis, [(i, i ^ 1 << apart) for i in range(count)])  8.67 us
    ppermute x1, starting transfers between devices, on_device_(): low = lax.ppermute(low, 'band', [(i, i ^ 1) for i in range(bands)])  3.56 us
    pallas_call x2, Pallas kernels, forced(): pl.pallas_call(functools.partial(result_kernel, directions, levs), out_sh...  2.87 us
    unnamed x15, local copies, waits for them, and re-layouts  2.3 us
    pallas_call x1, Pallas kernels, on_device_(): pl.pallas_call(functools.partial(fourier_kernel, lats, share), out_shape=...  1.99 us
    pallas_call x1, Pallas kernels, on_device_(): pl.pallas_call(pack_kernel, out_shape=[half_shape] * 2, in_specs=[SMEM, h...  1.92 us
  transfers between devices with their start and end apart: 9, of which 3 were waited for; matrix products, arithmetic and copies ran while one was open for 3% of the time, Pallas kernels for 40%

profile of v1, /device:TPU:0, one launch (start us, length us, event | category | flops | bytes accessed | tf_op | source)
XLA Modules:
  0.0 55.7 jit_solution(6595711264400518864)
XLA Ops:
  0.6 0.0 copy-start
  0.7 1.6 %copy.15 = bf16[80,2,1,3,1280]{4,0,3,1,2:T(8,128)(2,1)S(1)} copy(bf16[80,2,1,3,1280]{4,1,3,2,0:T(2,128)(2,1)} %param.10) | data formatting | bytes 2457600 | tf_op args[0]
  2.2 0.7 %copy-done = bf16[80,16,1280]{2,1,0:T(8,128)(2,1)S(1)} copy-done((bf16[80,16,1280]{2,1,0:T(8,128)(2,1)S(1)}, bf16[80,16,1280]{2,1,0:T(8,128)(2,1)}, u32[]{:S(2)}) %copy-start) | copy-done | bytes 3276824
  2.9 1.2 %fusion.2 = bf16[80,6,16]{2,1,0:T(8,128)(2,1)S(1)} fusion(bf16[80,16,1280]{2,1,0:T(8,128)(2,1)S(1)} %copy-done, bf16[80,6,1280]{2,0,1:T(8,128)(2,1)S(1)} %bitcast.14), kind=kOutput, calls=%fused_computation.2 | convolution fusion | flops 19668480 | bytes 4520960 | tf_op jit(solution)/shard_map/dot_general | solution.py:350
  4.1 0.0 copy-start.6
  4.1 0.1 copy.17
  4.3 0.1 copy.18
  4.4 0.1 broadcast_multiply_fusion.refs_0_
  4.4 3.0 %collective-permute-start = (bf16[80,96]{1,0:T(8,128)(2,1)S(1)}, bf16[80,96]{1,0:T(8,128)(2,1)S(1)}, u32[]{:S(2)}, u32[]{:S(2)}) collective-permute-start(bf16[80,96]{1,0:T(8,128)(2,1)S(1)} %broadcast_multiply_fusion.refs_0_), channel_id=1, source_target_pairs={{0,2},{2,0},{4,6},{6,4},{8,10},{10,8},{12,14},{14,12},{16,18},{18,... | collective-permute-start | bytes 46088 | tf_op jit(solution)/shard_map/ppermute | solution.py:24
  7.4 1.9 %pack.1 = (bf16[18,18,4,128]{3,2,1,0:T(4,128)(2,1)}, bf16[18,18,4,128]{3,2,1,0:T(4,128)(2,1)}) custom-call(s32[1]{0:T(128)} %bitcast.band, bf16[18,36,4,128]{3,2,1,0:T(4,128)(2,1)} %spectra.1), custom_call_target="tpu_custom_call" | custom-call | tf_op jit(solution)/shard_map/pack/pallas_call | solution.py:333
  9.3 1.4 %collective-permute-start.4 = (bf16[18,18,4,128]{3,2,1,0:T(4,128)(2,1)}, bf16[18,18,4,128]{3,2,1,0:T(4,128)(2,1)}, u32[]{:S(2)}, u32[]{:S(2)}) collective-permute-start(bf16[18,18,4,128]{3,2,1,0:T(4,128)(2,1)} %get-tuple-element.20), channel_id=1, source_target_pairs={{2,4},{6,8},{10,12},{14,16},{18,20},{22,24},{26,28},{4,2},{8,6},{1... | collective-permute-start | bytes 995336 | tf_op jit(solution)/shard_map/ppermute | solution.py:347
  10.8 3.6 %collective-permute-start.6 = (bf16[18,18,4,128]{3,2,1,0:T(4,128)(2,1)}, bf16[18,18,4,128]{3,2,1,0:T(4,128)(2,1)}, u32[]{:S(2)}, u32[]{:S(2)}) collective-permute-start(bf16[18,18,4,128]{3,2,1,0:T(4,128)(2,1)} %get-tuple-element.23), channel_id=1, source_target_pairs={{0,2},{2,0},{4,6},{6,4},{8,10},{10,8},{12,14},{14,12},{16,18},{18,... | collective-permute-start | bytes 995336 | tf_op jit(solution)/shard_map/ppermute | solution.py:345
  14.3 1.6 %collective-permute-start.1 = (bf16[160,96]{1,0:T(8,128)(2,1)S(1)}, bf16[160,96]{1,0:T(8,128)(2,1)S(1)}, u32[]{:S(2)}, u32[]{:S(2)}) collective-permute-start(bf16[160,96]{1,0:T(8,128)(2,1)S(1)} %pad_maximum_fusion.2), channel_id=1, source_target_pairs={{0,4},{2,6},{4,0},{6,2},{8,12},{10,14},{12,8},{14,10},{16,20},{18,... | collective-permute-start | bytes 92168 | tf_op jit(solution)/shard_map/ppermute | solution.py:24
  15.9 4.9 %collective-permute-done.1.refs_2_ = bf16[160,96]{1,0:T(8,128)(2,1)S(1)} collective-permute-done((bf16[160,96]{1,0:T(8,128)(2,1)S(1)}, bf16[160,96]{1,0:T(8,128)(2,1)S(1)}, u32[]{:S(2)}, u32[]{:S(2)}) %collective-permute-start.1) | collective-permute-done | bytes 30752 | tf_op jit(solution)/shard_map/ppermute | solution.py:24
  20.8 4.3 %collective-permute-start.2 = (bf16[320,96]{1,0:T(8,128)(2,1)S(1)}, bf16[320,96]{1,0:T(8,128)(2,1)S(1)}, u32[]{:S(2)}, u32[]{:S(2)}) collective-permute-start(bf16[320,96]{1,0:T(8,128)(2,1)S(1)} %pad_maximum_fusion.1), channel_id=1, source_target_pairs={{0,8},{2,10},{4,12},{6,14},{8,0},{10,2},{12,4},{14,6},{16,24},{18,... | collective-permute-start | bytes 184328 | tf_op jit(solution)/shard_map/ppermute | solution.py:24
  25.1 0.1 pad_add_fusion
  25.2 2.6 %collective-permute-done.2.refs_3_ = bf16[320,96]{1,0:T(8,128)(2,1)S(1)} collective-permute-done((bf16[320,96]{1,0:T(8,128)(2,1)S(1)}, bf16[320,96]{1,0:T(8,128)(2,1)S(1)}, u32[]{:S(2)}, u32[]{:S(2)}) %collective-permute-start.2) | collective-permute-done | bytes 61472 | tf_op jit(solution)/shard_map/ppermute | solution.py:24
  27.8 0.7 %pad_maximum_fusion = bf16[640,96]{1,0:T(8,128)(2,1)} fusion(bf16[320,96]{1,0:T(8,128)(2,1)S(1)} %collective-permute-done.2.refs_3_, bf16[160,96]{1,0:T(8,128)(2,1)S(1)} %collective-permute-done.1.refs_2_, bf16[80,96]{1,0:T(8,128)(2,1)S(1)} %collective-permute-done.refs_1_, bf16[80,96]{1,0:T(8,128)(2,1)S(1)} %broadcast_multiply_fusion.refs_0_), kind=kLoop, calls=%fused_computation.3 | loop fusion | flops 491520 | bytes 245760 | tf_op jit(solution)/shard_map/concatenate | solution.py:360
  28.5 2.8 %collective-permute-start.3 = (bf16[640,96]{1,0:T(8,128)(2,1)}, bf16[640,96]{1,0:T(8,128)(2,1)}, u32[]{:S(2)}, u32[]{:S(2)}) collective-permute-start(bf16[640,96]{1,0:T(8,128)(2,1)} %pad_maximum_fusion), channel_id=1, source_target_pairs={{0,16},{2,18},{4,20},{6,22},{8,24},{10,26},{12,28},{14,30},{16,0},... | collective-permute-start | bytes 368648 | tf_op jit(solution)/shard_map/ppermute | solution.py:24
  31.3 1.0 %fusion.9 = (f32[26,512]{1,0:T(8,128)S(1)}, f32[26,512]{1,0:T(8,128)}) fusion(s32[26]{0:T(128)S(1)} %pad_add_fusion), kind=kLoop, calls=%fused_computation.11 | loop fusion | flops 119808 | bytes 106600 | tf_op jit(solution)/shard_map/sin | solution.py:311
  32.3 7.1 %shard_map.121 = (f32[18,9,8,128]{3,2,1,0:T(8,128)S(1)}, f32[9,8,128]{2,1,0:T(8,128)S(1)}) custom-call(s32[1]{0:T(128)} %bitcast.6.lev, s32[1]{0:T(128)} %bitcast.5.up, f32[18]{0:T(128)S(1)} %copy-done.5, f32[18]{0:T(128)S(1)} %copy-done.3, f32[18]{0:T(128)S(1)} %copy-done.6, bf16[18,18,8,128]{3,2,1,0:T(8,128)(2,1)} %bitcast.15, ...), custom_call_target="tpu_custom_call" | custom-call | tf_op jit(solution)/shard_map/pallas_call | solution.py:428
  39.4 0.1 collective-permute-start.8
  39.5 7.2 %shard_map.122 = (f32[18,9,8,128]{3,2,1,0:T(8,128)S(1)}, f32[9,8,128]{2,1,0:T(8,128)S(1)}) custom-call(s32[1]{0:T(128)} %bitcast.6.lev, s32[1]{0:T(128)} %bitcast.9.up, f32[18]{0:T(128)S(1)} %copy-done.5, f32[18]{0:T(128)S(1)} %copy-done.3, f32[18]{0:T(128)S(1)} %copy-done.6, bf16[18,18,8,128]{3,2,1,0:T(8,128)(2,1)} %bitcast.16, ...), custom_call_target="tpu_custom_call" | custom-call | tf_op jit(solution)/shard_map/pallas_call | solution.py:428
  46.6 0.5 collective-permute-start.7
  47.2 0.1 fusion.14
  48.0 1.0 %first.1 = (f32[48,512]{1,0:T(8,128)S(1)}, bf16[640,512]{1,0:T(8,128)(2,1)S(1)}, bf16[640,512]{1,0:T(8,128)(2,1)S(1)}, bf16[512,512]{1,0:T(8,128)(2,1)S(1)}) custom-call(f32[26,512]{1,0:T(8,128)S(1)} %copy-done.1, f32[26,512]{1,0:T(8,128)S(1)} %get-tuple-element.33.sines, s32[4,128]{1,0:T(4,128)S(1)} %copy-done.4, ...), custom_call_target="tpu_custom_call" | custom-call | tf_op jit(solution)/shard_map/first/pallas_call | solution.py:380
  49.0 2.0 %fourier.1 = (f32[3,1,512]{2,1,0:T(1,128)}, f32[2,4,128]{2,1,0:T(4,128)S(1)}) custom-call(s32[1]{0:T(128)} %bitcast.band, f32[1]{0:T(128)S(6)} %copy.25.level, f32[48,512]{1,0:T(8,128)S(1)} %get-tuple-element.15.early, bf16[640,96]{1,0:T(8,128)(2,1)} %collective-permute-done.3.last, f32[1,512]{1,0:T(1,128)S(1)} %get-tuple-element.36.phase_cos, ...), custom_call_target="tpu_custom_call" | custom-call | tf_op jit(solution)/shard_map/fourier/pallas_call | solution.py:404
  51.0 0.0 collective-permute-start.5
  51.0 1.1 %collective-permute-done.5.refs_1_ = f32[2,4,128]{2,1,0:T(4,128)S(1)} collective-permute-done((f32[2,4,128]{2,1,0:T(4,128)S(1)}, f32[2,4,128]{2,1,0:T(4,128)S(1)}, u32[]{:S(2)}, u32[]{:S(2)}) %collective-permute-start.5) | collective-permute-done | bytes 4128 | tf_op jit(solution)/shard_map/ppermute | solution.py:24
  52.2 1.4 %shard_map.123.refs_2_ = f32[18,18,8,128]{3,2,1,0:T(8,128)} custom-call(s32[1]{0:T(128)} %bitcast.9.up, f32[18]{0:T(128)S(1)} %copy-done.3, f32[18,9,8,128]{3,2,1,0:T(8,128)S(1)} %get-tuple-element.24.damped, f32[2,4,128]{2,1,0:T(4,128)S(1)} %get-tuple-element.22.refs_0_, f32[2,4,128]{2,1,0:T(4,128)S(1)} %collective-permute-done.5.refs_1_), custom_call_target="tpu_custom_call" | custom-call | tf_op jit(solution)/shard_map/pallas_call | solution.py:453
  53.6 1.4 %shard_map.124 = f32[18,18,8,128]{3,2,1,0:T(8,128)} custom-call(s32[1]{0:T(128)} %bitcast.5.up, f32[18]{0:T(128)S(1)} %copy-done.3, f32[18,9,8,128]{3,2,1,0:T(8,128)S(1)} %get-tuple-element.21.damped, f32[2,4,128]{2,1,0:T(4,128)S(1)} %get-tuple-element.22.refs_0_, f32[2,4,128]{2,1,0:T(4,128)S(1)} %collective-permute-done.5.refs_1_, ...), custom_call_target="tpu_custom_call", output_to_operand_aliasing={{}: (5, {})} | custom-call | tf_op jit(solution)/shard_map/pallas_call | solution.py:453
  55.1 0.6 %charnock.1 = f32[4,128]{1,0:T(4,128)} custom-call(s32[1]{0:T(128)} %bitcast.9.up, s32[4,128]{1,0:T(4,128)S(1)} %copy-done.2, f32[2,4,128]{2,1,0:T(4,128)S(1)} %get-tuple-element.22.refs_0_, f32[2,4,128]{2,1,0:T(4,128)S(1)} %collective-permute-done.5.refs_1_, f32[9,8,128]{2,1,0:T(8,128)S(1)} %get-tuple-element.25.refs_2_, ...), custom_call_target="tpu_custom_call" | custom-call | tf_op jit(solution)/shard_map/charnock/pallas_call | solution.py:474
  (23 shorter events, 0.1 us)
Async XLA Ops:
  0.6 2.3 %copy-start = (bf16[80,16,1280]{2,1,0:T(8,128)(2,1)S(1)}, bf16[80,16,1280]{2,1,0:T(8,128)(2,1)}, u32[]{:S(2)}) copy-start(bf16[80,16,1280]{2,1,0:T(8,128)(2,1)} %param.11) | copy-start | bytes 9830404
  4.1 28.1 %copy-start.2 = (s32[4,128]{1,0:T(4,128)S(1)}, s32[4,128]{1,0:T(4,128)}, u32[]{:S(2)}) copy-start(s32[4,128]{1,0:T(4,128)} %land.5) | copy-start | bytes 6148
  4.1 28.1 %copy-start.3 = (f32[18]{0:T(128)S(1)}, f32[18]{0:T(128)}, u32[]{:S(2)}) copy-start(f32[18]{0:T(128)} %rate.7) | copy-start | bytes 220
  4.1 28.2 %copy-start.5 = (f32[18]{0:T(128)S(1)}, f32[18]{0:T(128)}, u32[]{:S(2)}) copy-start(f32[18]{0:T(128)} %courant.3) | copy-start | bytes 220
  4.1 28.2 %copy-start.6 = (f32[18]{0:T(128)S(1)}, f32[18]{0:T(128)}, u32[]{:S(2)}) copy-start(f32[18]{0:T(128)} %breaking.3) | copy-start | bytes 220
  4.4 9.9 %collective-permute-start = (bf16[80,96]{1,0:T(8,128)(2,1)S(1)}, bf16[80,96]{1,0:T(8,128)(2,1)S(1)}, u32[]{:S(2)}, u32[]{:S(2)}) collective-permute-start(bf16[80,96]{1,0:T(8,128)(2,1)S(1)} %broadcast_multiply_fusion.refs_0_), channel_id=1, source_target_pairs={{0,2},{2,0},{4,6},{6,4},{8,10},{10,8},{12,14},{14,12},{16,18},{18,... | collective-permute-start | bytes 46088 | tf_op jit(solution)/shard_map/ppermute | solution.py:24
  7.4 40.5 %copy-start.4 = (s32[4,128]{1,0:T(4,128)S(1)}, s32[4,128]{1,0:T(4,128)}, u32[]{:S(2)}) copy-start(s32[4,128]{1,0:T(4,128)} %coupling.3) | copy-start | bytes 6148
  9.3 22.9 %collective-permute-start.4 = (bf16[18,18,4,128]{3,2,1,0:T(4,128)(2,1)}, bf16[18,18,4,128]{3,2,1,0:T(4,128)(2,1)}, u32[]{:S(2)}, u32[]{:S(2)}) collective-permute-start(bf16[18,18,4,128]{3,2,1,0:T(4,128)(2,1)} %get-tuple-element.20), channel_id=1, source_target_pairs={{2,4},{6,8},{10,12},{14,16},{18,20},{22,24},{26,28},{4,2},{8,6},{1... | collective-permute-start | bytes 995336 | tf_op jit(solution)/shard_map/ppermute | solution.py:347
  10.8 28.7 %collective-permute-start.6 = (bf16[18,18,4,128]{3,2,1,0:T(4,128)(2,1)}, bf16[18,18,4,128]{3,2,1,0:T(4,128)(2,1)}, u32[]{:S(2)}, u32[]{:S(2)}) collective-permute-start(bf16[18,18,4,128]{3,2,1,0:T(4,128)(2,1)} %get-tuple-element.23), channel_id=1, source_target_pairs={{0,2},{2,0},{4,6},{6,4},{8,10},{10,8},{12,14},{14,12},{16,18},{18,... | collective-permute-start | bytes 995336 | tf_op jit(solution)/shard_map/ppermute | solution.py:345
  14.3 6.5 %collective-permute-start.1 = (bf16[160,96]{1,0:T(8,128)(2,1)S(1)}, bf16[160,96]{1,0:T(8,128)(2,1)S(1)}, u32[]{:S(2)}, u32[]{:S(2)}) collective-permute-start(bf16[160,96]{1,0:T(8,128)(2,1)S(1)} %pad_maximum_fusion.2), channel_id=1, source_target_pairs={{0,4},{2,6},{4,0},{6,2},{8,12},{10,14},{12,8},{14,10},{16,20},{18,... | collective-permute-start | bytes 92168 | tf_op jit(solution)/shard_map/ppermute | solution.py:24
  20.8 7.0 %collective-permute-start.2 = (bf16[320,96]{1,0:T(8,128)(2,1)S(1)}, bf16[320,96]{1,0:T(8,128)(2,1)S(1)}, u32[]{:S(2)}, u32[]{:S(2)}) collective-permute-start(bf16[320,96]{1,0:T(8,128)(2,1)S(1)} %pad_maximum_fusion.1), channel_id=1, source_target_pairs={{0,8},{2,10},{4,12},{6,14},{8,0},{10,2},{12,4},{14,6},{16,24},{18,... | collective-permute-start | bytes 184328 | tf_op jit(solution)/shard_map/ppermute | solution.py:24
  28.5 20.5 %collective-permute-start.3 = (bf16[640,96]{1,0:T(8,128)(2,1)}, bf16[640,96]{1,0:T(8,128)(2,1)}, u32[]{:S(2)}, u32[]{:S(2)}) collective-permute-start(bf16[640,96]{1,0:T(8,128)(2,1)} %pad_maximum_fusion), channel_id=1, source_target_pairs={{0,16},{2,18},{4,20},{6,22},{8,24},{10,26},{12,28},{14,30},{16,0},... | collective-permute-start | bytes 368648 | tf_op jit(solution)/shard_map/ppermute | solution.py:24
  32.2 15.7 %copy-start.1 = (f32[26,512]{1,0:T(8,128)S(1)}, f32[26,512]{1,0:T(8,128)}, u32[]{:S(2)}) copy-start(f32[26,512]{1,0:T(8,128)} %get-tuple-element.34.cosines) | copy-start | bytes 159748
  39.4 15.7 %collective-permute-start.8 = (f32[9,8,128]{2,1,0:T(8,128)S(1)}, f32[9,8,128]{2,1,0:T(8,128)S(1)}, u32[]{:S(2)}, u32[]{:S(2)}) collective-permute-start(f32[9,8,128]{2,1,0:T(8,128)S(1)} %get-tuple-element.26.refs_4_), channel_id=1, source_target_pairs={{0,1},{1,0},{2,3},{3,2},{4,5},{5,4},{6,7},{7,6},{8,9},{9,8},{10,11... | collective-permute-start | bytes 110600 | tf_op jit(solution)/shard_map/ppermute | solution.py:24
  46.6 8.4 %collective-permute-start.7 = (f32[9,8,128]{2,1,0:T(8,128)S(1)}, f32[9,8,128]{2,1,0:T(8,128)S(1)}, u32[]{:S(2)}, u32[]{:S(2)}) collective-permute-start(f32[9,8,128]{2,1,0:T(8,128)S(1)} %get-tuple-element.25.refs_2_), channel_id=1, source_target_pairs={{0,1},{1,0},{2,3},{3,2},{4,5},{5,4},{6,7},{7,6},{8,9},{9,8},{10,11... | collective-permute-start | bytes 110600 | tf_op jit(solution)/shard_map/ppermute | solution.py:24
  51.0 1.2 %collective-permute-start.5 = (f32[2,4,128]{2,1,0:T(4,128)S(1)}, f32[2,4,128]{2,1,0:T(4,128)S(1)}, u32[]{:S(2)}, u32[]{:S(2)}) collective-permute-start(f32[2,4,128]{2,1,0:T(4,128)S(1)} %get-tuple-element.22.refs_0_), channel_id=1, source_target_pairs={{0,1},{1,0},{2,3},{3,2},{4,5},{5,4},{6,7},{7,6},{8,9},{9,8},{10,11... | collective-permute-start | bytes 12296 | tf_op jit(solution)/shard_map/ppermute | solution.py:24

commit v2 on v1

--- a/solution.py
+++ b/solution.py
@@ -25,11 +25,15 @@
 
 
 def bits_of(count):
-    return list(range(count.bit_length() - 1))
+    bits = count.bit_length() - 1
+    return [0, *range(bits - 1, 0, -1)][:bits]
 
 
 def angles_of(directions):
     return [2.0 * math.pi / directions * (d + 0.5) for d in range(directions)]
+
+
+dot = functools.partial(jnp.dot, preferred_element_type=jnp.float32)
 
 
 def halves(row_low, low, high):
@@ -64,88 +68,115 @@
         copy.wait()
 
 
-def advect_kernel(
-    directions, lev, up, courant, rate, breaking, spectra, halo, land, *refs
-):
-    (damped, source, own, outside, sems) = refs[-5:]
+def advect_kernel(directions, lev, up, courant, rate, breaking, spectra, halo, land, *refs):
+    whole = spectra.shape[1] > halo.shape[1]
+    if whole:
+        damped, source, other, own, terms, moved, kept, shifts, sems = refs
+    else:
+        damped, source, terms, moved, kept, shifts = refs
+        own = spectra
     freqs = courant.shape[0]
     half = directions // 4
+    tiles = -(-half // 2)
     theta = angles_of(directions)
-    chunks = sems.shape[1]
-    span = freqs // chunks
-    copies = []
-    for k in range(chunks):
-        rows = pl.ds(k * span, span)
-        inside = spectra.at[rows, pl.ds((1 - up[0]) * half, half)]
-        copies.append(
-            [
-                pltpu.make_async_copy(inside, own.at[rows], sems.at[0, k]),
-                pltpu.make_async_copy(halo.at[rows], outside.at[rows], sems.at[1, k]),
-            ]
-        )
-        for copy in copies[-1]:
-            copy.start()
+    if whole:
+        copies = []
+        for k, (first, dst) in enumerate((((1 - up[0]) * half, own), (up[0] * half, other))):
+            copies.append(pltpu.make_async_copy(spectra.at[:, pl.ds(first, half)], dst, sems.at[k]))
+            copies[-1].start()
+
+    sign = 2 * up[0] - 1
+    row = lax.broadcasted_iota(jnp.int32, (128, 128), 0)
+    column = lax.broadcasted_iota(jnp.int32, (128, 128), 1)
+    for i in range(STEPS):
+        for k in range(2):
+            move = (1 - 2 * k) * sign * (i + 1)
+            hit = (row - column + move + 256) % 128 == 0
+            shifts[128 * i : 128 * i + 128, 128 * k : 128 * k + 128] = hit.astype(
+                jnp.float32
+            ).astype(jnp.bfloat16)
+
     row = lax.broadcasted_iota(jnp.int32, (8, 128), 0)
     row_low = row < 4
     inner_row = row % 4
     land4 = land[...].astype(jnp.float32)
     mask = jnp.concatenate([land4, land4], axis=0)
     source[...] = jnp.zeros_like(source)
-
-    def body(f, carry, rising):
+    if whole:
+        for copy in copies:
+            copy.wait()
+
+    def powers(f, carry, rising):
         speed = courant[f]
+        inside = inner_row >= 1 if rising else inner_row <= 2
+        step = 1 if rising else 7
+        held = []
+        for j in range(half):
+            cosines = [abs(math.cos(theta[2 * j + k])) for k in range(2)]
+            sines = [abs(math.sin(theta[2 * j + k])) for k in range(2)]
+
+            def both(power):
+                return halves(row_low, power(cosines[0], sines[0]), power(cosines[1], sines[1]))
+
+            def swapped_both(power):
+                return halves(row_low, power(cosines[1], sines[1]), power(cosines[0], sines[0]))
+
+            c = speed * both(lambda x, y: y)
+            a = 1.0 - speed * both(lambda x, y: x + y)
+            c_outer = speed * swapped_both(lambda x, y: y)
+            a_outer = 1.0 - speed * swapped_both(lambda x, y: x + y)
+            inner = own[f, j].astype(jnp.float32)
+            outer = pltpu.roll(halo[f, j].astype(jnp.float32), 4, 0)
+            states = [inner]
+            for k in range(STEPS):
+                from_outer = pltpu.roll(outer, step, 0)
+                inner = a * inner + c * jnp.where(inside, pltpu.roll(inner, step, 0), from_outer)
+                states.append(inner)
+                if k < STEPS - 1:
+                    outer = a_outer * outer + c_outer * from_outer
+            kept[f, j] = states[STEPS]
+            factors = (
+                4.0 * speed, 6.0 * speed * speed, 4.0 * speed * speed * speed,
+                speed * speed * speed * speed,
+            )
+            held.append(
+                [
+                    (factors[i] * both(lambda x, y, i=i: x ** (i + 1))) * states[STEPS - 1 - i]
+                    for i in range(STEPS)
+                ]
+            )
+            if j % 2 or j == half - 1:
+                first = held[-2] if j % 2 else held[-1]
+                at = pl.ds(pl.multiple_of(f * (16 * tiles) + 16 * (j // 2), 16), 16)
+                for i in range(STEPS):
+                    tile = jnp.concatenate([first[i], held[-1][i]], axis=0)
+                    terms[at, 128 * i : 128 * i + 128] = tile.astype(jnp.bfloat16)
+        return carry
+
+    for rising in (True, False):
+
+        @pl.when(up[0] == int(rising))
+        def _(rising=rising):
+            lax.fori_loop(0, freqs, functools.partial(powers, rising=rising), 0)
+
+    moved[...] = dot(terms[...], shifts[...])
+
+    def finish(f, carry):
         damp = breaking[f]
         gain = (1.0 + 2.0 * (lev[0] * freqs + f).astype(jnp.float32) / (NF - 1)) * rate[f]
         for j in range(half):
-            inner = own[f, j].astype(jnp.float32)
-            outer = outside[f, j].astype(jnp.float32)
-            signs = [1 if rising else -1] * 2
-            cosines = [signs[k] * math.cos(theta[2 * j + k]) for k in range(2)]
-            sines = [abs(math.sin(theta[2 * j + k])) for k in range(2)]
-            b = speed * halves(row_low, abs(cosines[0]), abs(cosines[1]))
-            c = speed * halves(row_low, sines[0], sines[1])
-            a = 1.0 - b - c
-            c2 = c * c
-            weights = (4.0 * c, 6.0 * c2, 4.0 * c2 * c, c2 * c2)
-
-            def upwind(tile):
-                from_west = pltpu.roll(tile, 1, 1) if max(cosines) > 0 else None
-                from_east = pltpu.roll(tile, 127, 1) if min(cosines) < 0 else None
-                if from_west is None or from_east is None:
-                    return from_east if from_west is None else from_west
-                return (
-                    halves(row_low, from_west, from_east)
-                    if cosines[0] > 0
-                    else halves(row_low, from_east, from_west)
-                )
-
-            state = inner
-            for k in range(1, STEPS + 1):
-                if k == 4:
-                    shifted = outer
-                elif rising:
-                    shifted = jnp.where(
-                        inner_row >= k, pltpu.roll(inner, k, 0), pltpu.roll(outer, k + 4, 0)
-                    )
-                else:
-                    shifted = jnp.where(
-                        inner_row < 4 - k, pltpu.roll(inner, 8 - k, 0), pltpu.roll(outer, 4 - k, 0)
-                    )
-                state = a * state + b * upwind(state) + weights[k - 1] * shifted
+            at = pl.ds(pl.multiple_of(f * (16 * tiles) + 8 * j, 8), 8)
+            east = [math.cos(theta[2 * j + k]) > 0 for k in range(2)]
+            if east[0] == east[1]:
+                shifted = moved[at, 0:128] if east[0] else moved[at, 128:256]
+            else:
+                shifted = halves(row_low, moved[at, 0:128], moved[at, 128:256])
+            state = kept[f, j] + shifted
             damped[f, j] = mask * state / (1.0 + damp * state)
             source[j] = source[j] + gain * state
         return carry
 
-    for k in range(chunks):
-        for copy in copies[k]:
-            copy.wait()
-        for rising in (True, False):
-
-            @pl.when(up[0] == int(rising))
-            def _(k=k, rising=rising):
-                lax.fori_loop(
-                    k * span, (k + 1) * span, functools.partial(body, rising=rising), 0
-                )
+    lax.fori_loop(0, freqs, finish, 0)
 
 
 def build_basis(cosines, sines, cos_table, sin_table, wave_cos, wave_sin):
@@ -187,9 +218,6 @@
         hold[at : at + count, :] = part[...]
         at += count
     return hold[...].T
-
-
-dot = functools.partial(jnp.dot, preferred_element_type=jnp.float32)
 
 
 def real_sum(legs, cos_table, sin_table):
@@ -328,6 +356,9 @@
     in_hbm = functools.partial(
         pltpu.with_memory_space_constraint, memory_space=pltpu.MemorySpace.HBM
     )
+    in_vmem = functools.partial(
+        pltpu.with_memory_space_constraint, memory_space=pltpu.MemorySpace.VMEM
+    )
     half_shape = pltpu.MemorySpace.HBM((freqs, half, tile_rows, tile_cols), jnp.bfloat16)
     chunks = 3
     low, high = pl.pallas_call(
@@ -359,7 +390,7 @@
     for bit in bits_of(bands):
         together = jnp.concatenate(parts, axis=0) if len(parts) > 1 else legs
         parts = parts + [swapped(together, "band", bit)]
-        if 2 << bit < bands:
+        if len(parts) <= bands.bit_length() - 1:
             order = order + [q ^ (1 << bit) for q in order]
     blocks = band ^ jnp.asarray(order, dtype=jnp.int32)
 
@@ -367,7 +398,8 @@
     total = bands * waves // 2
     points = tile_rows * tile_cols
     columns = 2 * FIELDS * lats
-    shift = total * (1 - 2 * (band // (bands // 2)))
+    last = bits_of(bands)[-1]
+    shift = (waves << last) * (1 - 2 * (jnp.right_shift(band, last) % 2))
     table = pltpu.VMEM((total, LON_W), jnp.bfloat16)
     pick_shape = jax.ShapeDtypeStruct((LON_W, points), jnp.bfloat16)
     fields_shape = jax.ShapeDtypeStruct((FIELDS * lats, LON_W), jnp.float32)
@@ -424,21 +456,27 @@
     own = in_hbm(spectra.reshape(freqs, pairs, 8, 128))
     half_state = pltpu.VMEM((freqs, quarter, 8, 128), jnp.float32)
 
-    def advected(halo, up):
+    def advected(spectra_of, halo, up):
+        whole = spectra_of.shape[1] == pairs
+        part = pltpu.VMEM((freqs, quarter, 8, 128), jnp.bfloat16)
+        tall = 16 * -(-quarter // 2) * freqs
         return pl.pallas_call(
             functools.partial(advect_kernel, directions),
-            out_shape=[half_state, pltpu.VMEM((quarter, 8, 128), jnp.float32)],
-            in_specs=[SMEM] * 5 + [hbm] * 2 + [VMEM],
-            out_specs=[VMEM] * 2,
-            scratch_shapes=[
-                pltpu.VMEM((freqs, quarter, 8, 128), jnp.bfloat16),
-                pltpu.VMEM((freqs, quarter, 8, 128), jnp.bfloat16),
-                pltpu.SemaphoreType.DMA((2, chunks)),
-            ],
-            compiler_params=params(4),
+            out_shape=[half_state, pltpu.VMEM((quarter, 8, 128), jnp.float32)] + [part] * whole,
+            in_specs=[SMEM] * 5 + [hbm if whole else VMEM, VMEM, VMEM],
+            out_specs=[VMEM] * (2 + whole),
+            scratch_shapes=[part] * whole
+            + [
+                pltpu.VMEM((tall, STEPS * 128), jnp.bfloat16),
+                pltpu.VMEM((tall, 256), jnp.float32),
+                pltpu.VMEM((freqs, quarter, 8, 128), jnp.float32),
+                pltpu.VMEM((STEPS * 128, 256), jnp.bfloat16),
+            ]
+            + [pltpu.SemaphoreType.DMA((2,))] * whole,
+            compiler_params=params(12),
         )(
-            levels, up, courant, growth_rate, breaking, own,
-            in_hbm(halo.reshape(freqs, quarter, 8, 128)), land_sea,
+            levels, up, courant, growth_rate, breaking, spectra_of,
+            in_vmem(halo.reshape(freqs, quarter, 8, 128)), land_sea,
         )
 
     def over_lev(value):
@@ -465,10 +503,10 @@
 
     near_up, far_up = odd.reshape(1), (1 - odd).reshape(1)
     winds = over_lev(wind)
-    damped, source = advected(low, near_up)
+    damped, source, own = advected(own, low, near_up)
     near_sources = over_lev(source)
     result = forced(damped, near_up)
-    damped, source = advected(high, far_up)
+    damped, source = advected(own, high, far_up)
     far_sources = over_lev(source)
     result = forced(damped, far_up, result)
     charnock = pl.pallas_call(

time: 56 us -> 49.2 us (0.88)
  Pallas kernels: 22.7 us -> 16.7 us
  starting transfers between devices: 17.2 us -> 13.2 us
  waiting for transfers between devices: 8.67 us -> 11.8 us
    pallas_call x2, Pallas kernels: 14.3 us -> 8.28 us  [advected(): pl.pallas_call(functools.partial(advect_kernel, directions), out_shape=[h...]
    ppermute x1, starting transfers between devices: 3.56 us -> 0.09 us  [on_device_(): low = lax.ppermute(low, 'band', [(i, i ^ 1) for i in range(bands)])]
    ppermute x7, waiting for transfers between devices: 8.67 us -> 11.8 us  [swapped(): lax.ppermute(block, axis, [(i, i ^ 1 << apart) for i in range(count)])]
    unnamed x15 -> x17, local copies, waits for them, and re-layouts: 2.3 us -> 2.3 us
  transfers between devices with their start and end apart: 9 -> 9, of which waited for: 3 -> 3; matrix products, arithmetic and copies ran while one was open for 3% -> 4% of each run, Pallas kernels for 40% -> 33%
where the time goes in v2:
time: 49.2 us; the launch traced here: 48.9 us
  Pallas kernels  16.7 us (34%)
  starting transfers between devices  13.2 us (27%)
  waiting for transfers between devices  11.8 us (24%)
  local copies, waits for them, and re-layouts  2.54 us (5%)
  other arithmetic  1.97 us (4%)
  between operations  1.47 us (3%)
  matrix products  1.17 us (2%)
    ppermute x7, waiting for transfers between devices, swapped(): lax.ppermute(block, axis, [(i, i ^ 1 << apart) for i in range(count)])  11.8 us
    ppermute x7, starting transfers between devices, swapped(): lax.ppermute(block, axis, [(i, i ^ 1 << apart) for i in range(count)])  11.8 us
    pallas_call x2, Pallas kernels, advected(): pl.pallas_call(functools.partial(advect_kernel, directions), out_shape=[h...  8.28 us
    pallas_call x2, Pallas kernels, forced(): pl.pallas_call(functools.partial(result_kernel, directions, levs), out_sh...  2.87 us
    unnamed x17, local copies, waits for them, and re-layouts  2.3 us
    pallas_call x1, Pallas kernels, on_device_(): pl.pallas_call(functools.partial(fourier_kernel, lats, share), out_shape=...  1.99 us
    pallas_call x1, Pallas kernels, on_device_(): pl.pallas_call(pack_kernel, out_shape=[half_shape] * 2, in_specs=[SMEM, h...  1.9 us
    ppermute x1, starting transfers between devices, on_device_(): high = lax.ppermute(high, 'band', across + [(j, i) for i, j in across])  1.39 us
  transfers between devices with their start and end apart: 9, of which 3 were waited for; matrix products, arithmetic and copies ran while one was open for 4% of the time, Pallas kernels for 33%

profile of v2, /device:TPU:0, one launch (start us, length us, event | category | flops | bytes accessed | tf_op | source)
XLA Modules:
  0.0 48.9 jit_solution(9826224845258912425)
XLA Ops:
  0.6 0.0 copy-start
  0.7 1.6 %copy.15 = bf16[80,2,1,3,1280]{4,0,3,1,2:T(8,128)(2,1)S(1)} copy(bf16[80,2,1,3,1280]{4,1,3,2,0:T(2,128)(2,1)} %param.10) | data formatting | bytes 2457600 | tf_op args[0]
  2.2 0.7 %copy-done = bf16[80,16,1280]{2,1,0:T(8,128)(2,1)S(1)} copy-done((bf16[80,16,1280]{2,1,0:T(8,128)(2,1)S(1)}, bf16[80,16,1280]{2,1,0:T(8,128)(2,1)}, u32[]{:S(2)}) %copy-start) | copy-done | bytes 3276824
  2.9 1.2 %fusion.2 = bf16[80,6,16]{2,1,0:T(8,128)(2,1)S(1)} fusion(bf16[80,16,1280]{2,1,0:T(8,128)(2,1)S(1)} %copy-done, bf16[80,6,1280]{2,0,1:T(8,128)(2,1)S(1)} %bitcast.14), kind=kOutput, calls=%fused_computation.2 | convolution fusion | flops 19668480 | bytes 4520960 | tf_op jit(solution)/shard_map/dot_general | solution.py:381
  4.1 0.0 copy-start.6
  4.1 0.1 copy.17
  4.3 0.1 copy.18
  4.4 0.1 broadcast_multiply_fusion.refs_0_
  4.4 3.0 %collective-permute-start = (bf16[80,96]{1,0:T(8,128)(2,1)S(1)}, bf16[80,96]{1,0:T(8,128)(2,1)S(1)}, u32[]{:S(2)}, u32[]{:S(2)}) collective-permute-start(bf16[80,96]{1,0:T(8,128)(2,1)S(1)} %broadcast_multiply_fusion.refs_0_), channel_id=1, source_target_pairs={{0,2},{2,0},{4,6},{6,4},{8,10},{10,8},{12,14},{14,12},{16,18},{18,... | collective-permute-start | bytes 46088 | tf_op jit(solution)/shard_map/ppermute | solution.py:24
  7.4 1.9 %pack.1 = (bf16[18,18,4,128]{3,2,1,0:T(4,128)(2,1)}, bf16[18,18,4,128]{3,2,1,0:T(4,128)(2,1)}) custom-call(s32[1]{0:T(128)} %bitcast.band, bf16[18,36,4,128]{3,2,1,0:T(4,128)(2,1)} %spectra.1), custom_call_target="tpu_custom_call" | custom-call | tf_op jit(solution)/shard_map/pack/pallas_call | solution.py:364
  9.3 0.1 collective-permute-start.4
  9.4 1.4 %collective-permute-start.5 = (bf16[18,18,4,128]{3,2,1,0:T(4,128)(2,1)}, bf16[18,18,4,128]{3,2,1,0:T(4,128)(2,1)}, u32[]{:S(2)}, u32[]{:S(2)}) collective-permute-start(bf16[18,18,4,128]{3,2,1,0:T(4,128)(2,1)} %get-tuple-element.23), channel_id=1, source_target_pairs={{2,4},{6,8},{10,12},{14,16},{18,20},{22,24},{26,28},{4,2},{8,6},{1... | collective-permute-start | bytes 995336 | tf_op jit(solution)/shard_map/ppermute | solution.py:378
  10.8 0.0 collective-permute-done.refs_1_
  10.8 6.0 %collective-permute-start.1 = (bf16[160,96]{1,0:T(8,128)(2,1)S(1)}, bf16[160,96]{1,0:T(8,128)(2,1)S(1)}, u32[]{:S(2)}, u32[]{:S(2)}) collective-permute-start(bf16[160,96]{1,0:T(8,128)(2,1)S(1)} %pad_maximum_fusion.2), channel_id=1, source_target_pairs={{0,16},{2,18},{4,20},{6,22},{8,24},{10,26},{12,28},{14,30},{16,0},... | collective-permute-start | bytes 92168 | tf_op jit(solution)/shard_map/ppermute | solution.py:24
  16.9 8.4 %collective-permute-done.1.refs_2_ = bf16[160,96]{1,0:T(8,128)(2,1)S(1)} collective-permute-done((bf16[160,96]{1,0:T(8,128)(2,1)S(1)}, bf16[160,96]{1,0:T(8,128)(2,1)S(1)}, u32[]{:S(2)}, u32[]{:S(2)}) %collective-permute-start.1) | collective-permute-done | bytes 30752 | tf_op jit(solution)/shard_map/ppermute | solution.py:24
  25.3 2.1 %collective-permute-start.2 = (bf16[320,96]{1,0:T(8,128)(2,1)S(1)}, bf16[320,96]{1,0:T(8,128)(2,1)S(1)}, u32[]{:S(2)}, u32[]{:S(2)}) collective-permute-start(bf16[320,96]{1,0:T(8,128)(2,1)S(1)} %pad_maximum_fusion.1), channel_id=1, source_target_pairs={{0,8},{2,10},{4,12},{6,14},{8,0},{10,2},{12,4},{14,6},{16,24},{18,... | collective-permute-start | bytes 184328 | tf_op jit(solution)/shard_map/ppermute | solution.py:24
  27.4 0.1 pad_add_fusion
  27.5 2.3 %collective-permute-done.2.refs_3_ = bf16[320,96]{1,0:T(8,128)(2,1)S(1)} collective-permute-done((bf16[320,96]{1,0:T(8,128)(2,1)S(1)}, bf16[320,96]{1,0:T(8,128)(2,1)S(1)}, u32[]{:S(2)}, u32[]{:S(2)}) %collective-permute-start.2) | collective-permute-done | bytes 61472 | tf_op jit(solution)/shard_map/ppermute | solution.py:24
  29.8 0.7 %pad_maximum_fusion = bf16[640,96]{1,0:T(8,128)(2,1)} fusion(bf16[320,96]{1,0:T(8,128)(2,1)S(1)} %collective-permute-done.2.refs_3_, bf16[160,96]{1,0:T(8,128)(2,1)S(1)} %collective-permute-done.1.refs_2_, bf16[80,96]{1,0:T(8,128)(2,1)S(1)} %collective-permute-done.refs_1_, bf16[80,96]{1,0:T(8,128)(2,1)S(1)} %broadcast_multiply_fusion.refs_0_), kind=kLoop, calls=%fused_computation.3 | loop fusion | flops 491520 | bytes 245760 | tf_op jit(solution)/shard_map/concatenate | solution.py:391
  30.5 1.0 %fusion.9 = (f32[26,512]{1,0:T(8,128)S(1)}, f32[26,512]{1,0:T(8,128)}) fusion(s32[26]{0:T(128)S(1)} %pad_add_fusion), kind=kLoop, calls=%fused_computation.11 | loop fusion | flops 119808 | bytes 106600 | tf_op jit(solution)/shard_map/sin | solution.py:339
  31.5 4.6 %shard_map.121 = (f32[18,9,8,128]{3,2,1,0:T(8,128)S(1)}, f32[9,8,128]{2,1,0:T(8,128)S(1)}, bf16[18,9,8,128]{3,2,1,0:T(8,128)(2,1)S(1)}) custom-call(s32[1]{0:T(128)} %bitcast.6.lev, s32[1]{0:T(128)} %bitcast.7.up, f32[18]{0:T(128)S(1)} %copy-done.5, f32[18]{0:T(128)S(1)} %copy-done.3, f32[18]{0:T(128)S(1)} %copy-done.6, bf16[18,18,8,128]{3,2,1,0:T(8,128)(2,1)} %bitcast.16, ...), custom_call_target="tpu_custom_call" | custom-call | tf_op jit(solution)/shard_map/pallas_call | solution.py:463
  36.1 3.7 %shard_map.122 = (f32[18,9,8,128]{3,2,1,0:T(8,128)S(1)}, f32[9,8,128]{2,1,0:T(8,128)S(1)}) custom-call(s32[1]{0:T(128)} %bitcast.6.lev, s32[1]{0:T(128)} %bitcast.5.up, f32[18]{0:T(128)S(1)} %copy-done.5, f32[18]{0:T(128)S(1)} %copy-done.3, f32[18]{0:T(128)S(1)} %copy-done.6, bf16[18,9,8,128]{3,2,1,0:T(8,128)(2,1)S(1)} %get-tuple-element.22.spectra, ...), custom_call_target="tpu_custom_call" | custom-call | tf_op jit(solution)/shard_map/pallas_call | solution.py:463
  39.8 0.1 collective-permute-start.8
  39.9 0.5 %collective-permute-start.7 = (f32[9,8,128]{2,1,0:T(8,128)S(1)}, f32[9,8,128]{2,1,0:T(8,128)S(1)}, u32[]{:S(2)}, u32[]{:S(2)}) collective-permute-start(f32[9,8,128]{2,1,0:T(8,128)S(1)} %get-tuple-element.27.refs_2_), channel_id=1, source_target_pairs={{0,1},{1,0},{2,3},{3,2},{4,5},{5,4},{6,7},{7,6},{8,9},{9,8},{10,11... | collective-permute-start | bytes 110600 | tf_op jit(solution)/shard_map/ppermute | solution.py:24
  40.4 0.1 fusion.14
  41.2 1.0 %first.1 = (f32[48,512]{1,0:T(8,128)S(1)}, bf16[640,512]{1,0:T(8,128)(2,1)S(1)}, bf16[640,512]{1,0:T(8,128)(2,1)S(1)}, bf16[512,512]{1,0:T(8,128)(2,1)S(1)}) custom-call(f32[26,512]{1,0:T(8,128)S(1)} %copy-done.1, f32[26,512]{1,0:T(8,128)S(1)} %get-tuple-element.35.sines, s32[4,128]{1,0:T(4,128)S(1)} %copy-done.4, ...), custom_call_target="tpu_custom_call" | custom-call | tf_op jit(solution)/shard_map/first/pallas_call | solution.py:412
  42.2 2.0 %fourier.1 = (f32[3,1,512]{2,1,0:T(1,128)}, f32[2,4,128]{2,1,0:T(4,128)S(1)}) custom-call(s32[1]{0:T(128)} %bitcast.band, f32[1]{0:T(128)S(6)} %copy.25.level, f32[48,512]{1,0:T(8,128)S(1)} %get-tuple-element.16.early, bf16[640,96]{1,0:T(8,128)(2,1)} %collective-permute-done.3.last, f32[1,512]{1,0:T(1,128)S(1)} %get-tuple-element.38.phase_cos, ...), custom_call_target="tpu_custom_call" | custom-call | tf_op jit(solution)/shard_map/fourier/pallas_call | solution.py:436
  44.2 0.1 collective-permute-start.6
  44.3 1.1 %collective-permute-done.6.refs_1_ = f32[2,4,128]{2,1,0:T(4,128)S(1)} collective-permute-done((f32[2,4,128]{2,1,0:T(4,128)S(1)}, f32[2,4,128]{2,1,0:T(4,128)S(1)}, u32[]{:S(2)}, u32[]{:S(2)}) %collective-permute-start.6) | collective-permute-done | bytes 4128 | tf_op jit(solution)/shard_map/ppermute | solution.py:24
  45.4 1.4 %shard_map.123.refs_2_ = f32[18,18,8,128]{3,2,1,0:T(8,128)} custom-call(s32[1]{0:T(128)} %bitcast.7.up, f32[18]{0:T(128)S(1)} %copy-done.3, f32[18,9,8,128]{3,2,1,0:T(8,128)S(1)} %get-tuple-element.26.damped, f32[2,4,128]{2,1,0:T(4,128)S(1)} %get-tuple-element.25.refs_0_, f32[2,4,128]{2,1,0:T(4,128)S(1)} %collective-permute-done.6.refs_1_), custom_call_target="tpu_custom_call" | custom-call | tf_op jit(solution)/shard_map/pallas_call | solution.py:491
  46.8 1.4 %shard_map.124 = f32[18,18,8,128]{3,2,1,0:T(8,128)} custom-call(s32[1]{0:T(128)} %bitcast.5.up, f32[18]{0:T(128)S(1)} %copy-done.3, f32[18,9,8,128]{3,2,1,0:T(8,128)S(1)} %get-tuple-element.24.damped, f32[2,4,128]{2,1,0:T(4,128)S(1)} %get-tuple-element.25.refs_0_, f32[2,4,128]{2,1,0:T(4,128)S(1)} %collective-permute-done.6.refs_1_, ...), custom_call_target="tpu_custom_call", output_to_operand_aliasing={{}: (5, {})} | custom-call | tf_op jit(solution)/shard_map/pallas_call | solution.py:491
  48.3 0.6 %charnock.1 = f32[4,128]{1,0:T(4,128)} custom-call(s32[1]{0:T(128)} %bitcast.7.up, s32[4,128]{1,0:T(4,128)S(1)} %copy-done.2, f32[2,4,128]{2,1,0:T(4,128)S(1)} %get-tuple-element.25.refs_0_, f32[2,4,128]{2,1,0:T(4,128)S(1)} %collective-permute-done.6.refs_1_, f32[9,8,128]{2,1,0:T(8,128)S(1)} %get-tuple-element.27.refs_2_, ...), custom_call_target="tpu_custom_call" | custom-call | tf_op jit(solution)/shard_map/charnock/pallas_call | solution.py:512
  (25 shorter events, 0.1 us)
Async XLA Ops:
  0.6 2.3 %copy-start = (bf16[80,16,1280]{2,1,0:T(8,128)(2,1)S(1)}, bf16[80,16,1280]{2,1,0:T(8,128)(2,1)}, u32[]{:S(2)}) copy-start(bf16[80,16,1280]{2,1,0:T(8,128)(2,1)} %param.11) | copy-start | bytes 9830404
  2.9 7.9 %copy-start.7 = (s32[8]{0:T(128)S(1)}, s32[8]{0:T(128)}, u32[]{:S(2)}) copy-start(s32[8]{0:T(128)} %constant.60.clone) | copy-start | bytes 100
  4.1 27.4 %copy-start.2 = (s32[4,128]{1,0:T(4,128)S(1)}, s32[4,128]{1,0:T(4,128)}, u32[]{:S(2)}) copy-start(s32[4,128]{1,0:T(4,128)} %land.5) | copy-start | bytes 6148
  4.1 27.4 %copy-start.3 = (f32[18]{0:T(128)S(1)}, f32[18]{0:T(128)}, u32[]{:S(2)}) copy-start(f32[18]{0:T(128)} %rate.7) | copy-start | bytes 220
  4.1 27.4 %copy-start.5 = (f32[18]{0:T(128)S(1)}, f32[18]{0:T(128)}, u32[]{:S(2)}) copy-start(f32[18]{0:T(128)} %courant.3) | copy-start | bytes 220
  4.1 27.4 %copy-start.6 = (f32[18]{0:T(128)S(1)}, f32[18]{0:T(128)}, u32[]{:S(2)}) copy-start(f32[18]{0:T(128)} %breaking.3) | copy-start | bytes 220
  4.3 36.9 %copy-start.4 = (s32[4,128]{1,0:T(4,128)S(1)}, s32[4,128]{1,0:T(4,128)}, u32[]{:S(2)}) copy-start(s32[4,128]{1,0:T(4,128)} %coupling.3) | copy-start | bytes 6148
  4.4 6.4 %collective-permute-start = (bf16[80,96]{1,0:T(8,128)(2,1)S(1)}, bf16[80,96]{1,0:T(8,128)(2,1)S(1)}, u32[]{:S(2)}, u32[]{:S(2)}) collective-permute-start(bf16[80,96]{1,0:T(8,128)(2,1)S(1)} %broadcast_multiply_fusion.refs_0_), channel_id=1, source_target_pairs={{0,2},{2,0},{4,6},{6,4},{8,10},{10,8},{12,14},{14,12},{16,18},{18,... | collective-permute-start | bytes 46088 | tf_op jit(solution)/shard_map/ppermute | solution.py:24
  9.3 22.2 %collective-permute-start.4 = (bf16[18,18,4,128]{3,2,1,0:T(4,128)(2,1)}, bf16[18,18,4,128]{3,2,1,0:T(4,128)(2,1)}, u32[]{:S(2)}, u32[]{:S(2)}) collective-permute-start(bf16[18,18,4,128]{3,2,1,0:T(4,128)(2,1)} %get-tuple-element.21), channel_id=1, source_target_pairs={{0,2},{2,0},{4,6},{6,4},{8,10},{10,8},{12,14},{14,12},{16,18},{18,... | collective-permute-start | bytes 995336 | tf_op jit(solution)/shard_map/ppermute | solution.py:376
  9.4 26.7 %collective-permute-start.5 = (bf16[18,18,4,128]{3,2,1,0:T(4,128)(2,1)}, bf16[18,18,4,128]{3,2,1,0:T(4,128)(2,1)}, u32[]{:S(2)}, u32[]{:S(2)}) collective-permute-start(bf16[18,18,4,128]{3,2,1,0:T(4,128)(2,1)} %get-tuple-element.23), channel_id=1, source_target_pairs={{2,4},{6,8},{10,12},{14,16},{18,20},{22,24},{26,28},{4,2},{8,6},{1... | collective-permute-start | bytes 995336 | tf_op jit(solution)/shard_map/ppermute | solution.py:378
  10.8 14.4 %collective-permute-start.1 = (bf16[160,96]{1,0:T(8,128)(2,1)S(1)}, bf16[160,96]{1,0:T(8,128)(2,1)S(1)}, u32[]{:S(2)}, u32[]{:S(2)}) collective-permute-start(bf16[160,96]{1,0:T(8,128)(2,1)S(1)} %pad_maximum_fusion.2), channel_id=1, source_target_pairs={{0,16},{2,18},{4,20},{6,22},{8,24},{10,26},{12,28},{14,30},{16,0},... | collective-permute-start | bytes 92168 | tf_op jit(solution)/shard_map/ppermute | solution.py:24
  25.3 4.5 %collective-permute-start.2 = (bf16[320,96]{1,0:T(8,128)(2,1)S(1)}, bf16[320,96]{1,0:T(8,128)(2,1)S(1)}, u32[]{:S(2)}, u32[]{:S(2)}) collective-permute-start(bf16[320,96]{1,0:T(8,128)(2,1)S(1)} %pad_maximum_fusion.1), channel_id=1, source_target_pairs={{0,8},{2,10},{4,12},{6,14},{8,0},{10,2},{12,4},{14,6},{16,24},{18,... | collective-permute-start | bytes 184328 | tf_op jit(solution)/shard_map/ppermute | solution.py:24
  30.5 11.7 %collective-permute-start.3 = (bf16[640,96]{1,0:T(8,128)(2,1)}, bf16[640,96]{1,0:T(8,128)(2,1)}, u32[]{:S(2)}, u32[]{:S(2)}) collective-permute-start(bf16[640,96]{1,0:T(8,128)(2,1)} %pad_maximum_fusion), channel_id=1, source_target_pairs={{0,4},{2,6},{4,0},{6,2},{8,12},{10,14},{12,8},{14,10},{16,20},{18,... | collective-permute-start | bytes 368648 | tf_op jit(solution)/shard_map/ppermute | solution.py:24
  31.5 9.7 %copy-start.1 = (f32[26,512]{1,0:T(8,128)S(1)}, f32[26,512]{1,0:T(8,128)}, u32[]{:S(2)}) copy-start(f32[26,512]{1,0:T(8,128)} %get-tuple-element.36.cosines) | copy-start | bytes 159748
  39.8 8.4 %collective-permute-start.8 = (f32[9,8,128]{2,1,0:T(8,128)S(1)}, f32[9,8,128]{2,1,0:T(8,128)S(1)}, u32[]{:S(2)}, u32[]{:S(2)}) collective-permute-start(f32[9,8,128]{2,1,0:T(8,128)S(1)} %get-tuple-element.28.refs_4_), channel_id=1, source_target_pairs={{0,1},{1,0},{2,3},{3,2},{4,5},{5,4},{6,7},{7,6},{8,9},{9,8},{10,11... | collective-permute-start | bytes 110600 | tf_op jit(solution)/shard_map/ppermute | solution.py:24
  39.9 8.4 %collective-permute-start.7 = (f32[9,8,128]{2,1,0:T(8,128)S(1)}, f32[9,8,128]{2,1,0:T(8,128)S(1)}, u32[]{:S(2)}, u32[]{:S(2)}) collective-permute-start(f32[9,8,128]{2,1,0:T(8,128)S(1)} %get-tuple-element.27.refs_2_), channel_id=1, source_target_pairs={{0,1},{1,0},{2,3},{3,2},{4,5},{5,4},{6,7},{7,6},{8,9},{9,8},{10,11... | collective-permute-start | bytes 110600 | tf_op jit(solution)/shard_map/ppermute | solution.py:24
  44.2 1.2 %collective-permute-start.6 = (f32[2,4,128]{2,1,0:T(4,128)S(1)}, f32[2,4,128]{2,1,0:T(4,128)S(1)}, u32[]{:S(2)}, u32[]{:S(2)}) collective-permute-start(f32[2,4,128]{2,1,0:T(4,128)S(1)} %get-tuple-element.25.refs_0_), channel_id=1, source_target_pairs={{0,1},{1,0},{2,3},{3,2},{4,5},{5,4},{6,7},{7,6},{8,9},{9,8},{10,11... | collective-permute-start | bytes 12296 | tf_op jit(solution)/shard_map/ppermute | solution.py:24

commit v3 on v2

--- a/solution.py
+++ b/solution.py
@@ -295,22 +295,26 @@
     return (2 * up - 1).astype(jnp.float32)
 
 
-def result_kernel(directions, parts, up, rate, damped, *refs):
+def result_kernel(directions, parts, up, rate, near, far, *refs):
     winds = refs[:parts]
     result, stage, sems = refs[-3:]
     half = directions // 4
     chunks = sems.shape[0]
     span = rate.shape[0] // chunks
-    pushes, _, _ = pushes_of(directions, winds, sign_of(up[0]))
+    sign = sign_of(up[0])
+    sides = [
+        (near, (1 - up[0]) * half, pushes_of(directions, winds, sign)[0]),
+        (far, up[0] * half, pushes_of(directions, winds, -sign)[0]),
+    ]
     copies = []
     for chunk in range(chunks):
         for f in range(chunk * span, (chunk + 1) * span):
-            for j in range(half):
-                value = damped[f, j]
-                stage[f, j] = value + value * (rate[f] * pushes[j])
+            for damped, first, pushes in sides:
+                for j in range(half):
+                    value = damped[f, j]
+                    stage[f, first + j] = value + value * (rate[f] * pushes[j])
         rows = pl.ds(chunk * span, span)
-        there = result.at[rows, pl.ds((1 - up[0]) * half, half)]
-        copies.append(pltpu.make_async_copy(stage.at[rows], there, sems.at[chunk]))
+        copies.append(pltpu.make_async_copy(stage.at[rows], result.at[rows], sems.at[chunk]))
         copies[-1].start()
     for copy in copies:
         copy.wait()
@@ -487,28 +491,24 @@
             bit += 1
         return parts
 
-    def forced(damped, up, *earlier):
-        return pl.pallas_call(
-            functools.partial(result_kernel, directions, levs),
-            out_shape=pltpu.MemorySpace.HBM((freqs, pairs, 8, 128), jnp.float32),
-            in_specs=[SMEM] * 2 + [VMEM] * (1 + levs) + [hbm] * len(earlier),
-            out_specs=hbm,
-            scratch_shapes=[
-                pltpu.VMEM((freqs, quarter, 8, 128), jnp.float32),
-                pltpu.SemaphoreType.DMA((chunks,)),
-            ],
-            input_output_aliases={3 + levs: 0} if earlier else {},
-            compiler_params=params(4),
-        )(up, growth_rate, damped, *winds, *earlier)
-
     near_up, far_up = odd.reshape(1), (1 - odd).reshape(1)
     winds = over_lev(wind)
-    damped, source, own = advected(own, low, near_up)
+    near_damped, source, own = advected(own, low, near_up)
     near_sources = over_lev(source)
-    result = forced(damped, near_up)
-    damped, source = advected(own, high, far_up)
+    far_damped, source = advected(own, high, far_up)
     far_sources = over_lev(source)
-    result = forced(damped, far_up, result)
+    result = pl.pallas_call(
+        functools.partial(result_kernel, directions, levs),
+        out_shape=pltpu.MemorySpace.HBM((freqs, pairs, 8, 128), jnp.float32),
+        in_specs=[SMEM] * 2 + [VMEM] * (2 + levs),
+        out_specs=hbm,
+        scratch_shapes=[
+            pltpu.VMEM((freqs, pairs, 8, 128), jnp.float32),
+            pltpu.SemaphoreType.DMA((chunks,)),
+        ],
+        compiler_params=params(6),
+        name="result",
+    )(near_up, growth_rate, near_damped, far_damped, *winds)
     charnock = pl.pallas_call(
         functools.partial(charnock_kernel, directions, levs),
         out_shape=jax.ShapeDtypeStruct((tile_rows, tile_cols), jnp.float32),

time: 49.2 us -> 48.1 us (0.978)
  Pallas kernels: 16.7 us -> 15.6 us
    pallas_call x2 -> x1, Pallas kernels: 2.87 us -> 1.79 us  [on_device_(): pl.pallas_call(functools.partial(result_kernel, directions, levs), out_sh...]
  transfers between devices with their start and end apart: 9 -> 9, of which waited for: 3 -> 3; matrix products, arithmetic and copies ran while one was open for 4% -> 4% of each run, Pallas kernels for 33% -> 31%
where the time goes in v3:
time: 48.1 us; the launch traced here: 47.8 us
  Pallas kernels  15.6 us (32%)
  starting transfers between devices  13.2 us (27%)
  waiting for transfers between devices  11.8 us (25%)
  local copies, waits for them, and re-layouts  2.54 us (5%)
  other arithmetic  1.97 us (4%)
  between operations  1.47 us (3%)
  matrix products  1.17 us (2%)
    ppermute x7, waiting for transfers between devices, swapped(): lax.ppermute(block, axis, [(i, i ^ 1 << apart) for i in range(count)])  11.8 us
    ppermute x7, starting transfers between devices, swapped(): lax.ppermute(block, axis, [(i, i ^ 1 << apart) for i in range(count)])  11.8 us
    pallas_call x2, Pallas kernels, advected(): pl.pallas_call(functools.partial(advect_kernel, directions), out_shape=[h...  8.28 us
    unnamed x17, local copies, waits for them, and re-layouts  2.3 us
    pallas_call x1, Pallas kernels, on_device_(): pl.pallas_call(functools.partial(fourier_kernel, lats, share), out_shape=...  1.99 us
    pallas_call x1, Pallas kernels, on_device_(): pl.pallas_call(pack_kernel, out_shape=[half_shape] * 2, in_specs=[SMEM, h...  1.9 us
    pallas_call x1, Pallas kernels, on_device_(): pl.pallas_call(functools.partial(result_kernel, directions, levs), out_sh...  1.79 us
    ppermute x1, starting transfers between devices, on_device_(): high = lax.ppermute(high, 'band', across + [(j, i) for i, j in across])  1.39 us
  transfers between devices with their start and end apart: 9, of which 3 were waited for; matrix products, arithmetic and copies ran while one was open for 4% of the time, Pallas kernels for 31%

profile of v3, /device:TPU:0, one launch (start us, length us, event | category | flops | bytes accessed | tf_op | source)
XLA Modules:
  0.0 47.8 jit_solution(2585860166400811871)
XLA Ops:
  0.6 0.0 copy-start
  0.7 1.6 %copy.14 = bf16[80,2,1,3,1280]{4,0,3,1,2:T(8,128)(2,1)S(1)} copy(bf16[80,2,1,3,1280]{4,1,3,2,0:T(2,128)(2,1)} %param.10) | data formatting | bytes 2457600 | tf_op args[0]
  2.2 0.7 %copy-done = bf16[80,16,1280]{2,1,0:T(8,128)(2,1)S(1)} copy-done((bf16[80,16,1280]{2,1,0:T(8,128)(2,1)S(1)}, bf16[80,16,1280]{2,1,0:T(8,128)(2,1)}, u32[]{:S(2)}) %copy-start) | copy-done | bytes 3276824
  2.9 1.2 %fusion.2 = bf16[80,6,16]{2,1,0:T(8,128)(2,1)S(1)} fusion(bf16[80,16,1280]{2,1,0:T(8,128)(2,1)S(1)} %copy-done, bf16[80,6,1280]{2,0,1:T(8,128)(2,1)S(1)} %bitcast.14), kind=kOutput, calls=%fused_computation.2 | convolution fusion | flops 19668480 | bytes 4520960 | tf_op jit(solution)/shard_map/dot_general | solution.py:385
  4.1 0.0 copy-start.6
  4.1 0.1 copy.16
  4.3 0.1 copy.17
  4.4 0.1 broadcast_multiply_fusion.refs_0_
  4.4 3.0 %collective-permute-start = (bf16[80,96]{1,0:T(8,128)(2,1)S(1)}, bf16[80,96]{1,0:T(8,128)(2,1)S(1)}, u32[]{:S(2)}, u32[]{:S(2)}) collective-permute-start(bf16[80,96]{1,0:T(8,128)(2,1)S(1)} %broadcast_multiply_fusion.refs_0_), channel_id=1, source_target_pairs={{0,2},{2,0},{4,6},{6,4},{8,10},{10,8},{12,14},{14,12},{16,18},{18,... | collective-permute-start | bytes 46088 | tf_op jit(solution)/shard_map/ppermute | solution.py:24
  7.4 1.9 %pack.1 = (bf16[18,18,4,128]{3,2,1,0:T(4,128)(2,1)}, bf16[18,18,4,128]{3,2,1,0:T(4,128)(2,1)}) custom-call(s32[1]{0:T(128)} %bitcast.band, bf16[18,36,4,128]{3,2,1,0:T(4,128)(2,1)} %spectra.1), custom_call_target="tpu_custom_call" | custom-call | tf_op jit(solution)/shard_map/pack/pallas_call | solution.py:368
  9.3 0.1 collective-permute-start.4
  9.4 1.4 %collective-permute-start.5 = (bf16[18,18,4,128]{3,2,1,0:T(4,128)(2,1)}, bf16[18,18,4,128]{3,2,1,0:T(4,128)(2,1)}, u32[]{:S(2)}, u32[]{:S(2)}) collective-permute-start(bf16[18,18,4,128]{3,2,1,0:T(4,128)(2,1)} %get-tuple-element.24), channel_id=1, source_target_pairs={{2,4},{6,8},{10,12},{14,16},{18,20},{22,24},{26,28},{4,2},{8,6},{1... | collective-permute-start | bytes 995336 | tf_op jit(solution)/shard_map/ppermute | solution.py:382
  10.8 0.0 collective-permute-done.refs_1_
  10.8 6.0 %collective-permute-start.1 = (bf16[160,96]{1,0:T(8,128)(2,1)S(1)}, bf16[160,96]{1,0:T(8,128)(2,1)S(1)}, u32[]{:S(2)}, u32[]{:S(2)}) collective-permute-start(bf16[160,96]{1,0:T(8,128)(2,1)S(1)} %pad_maximum_fusion.2), channel_id=1, source_target_pairs={{0,16},{2,18},{4,20},{6,22},{8,24},{10,26},{12,28},{14,30},{16,0},... | collective-permute-start | bytes 92168 | tf_op jit(solution)/shard_map/ppermute | solution.py:24
  16.9 8.4 %collective-permute-done.1.refs_2_ = bf16[160,96]{1,0:T(8,128)(2,1)S(1)} collective-permute-done((bf16[160,96]{1,0:T(8,128)(2,1)S(1)}, bf16[160,96]{1,0:T(8,128)(2,1)S(1)}, u32[]{:S(2)}, u32[]{:S(2)}) %collective-permute-start.1) | collective-permute-done | bytes 30752 | tf_op jit(solution)/shard_map/ppermute | solution.py:24
  25.3 2.1 %collective-permute-start.2 = (bf16[320,96]{1,0:T(8,128)(2,1)S(1)}, bf16[320,96]{1,0:T(8,128)(2,1)S(1)}, u32[]{:S(2)}, u32[]{:S(2)}) collective-permute-start(bf16[320,96]{1,0:T(8,128)(2,1)S(1)} %pad_maximum_fusion.1), channel_id=1, source_target_pairs={{0,8},{2,10},{4,12},{6,14},{8,0},{10,2},{12,4},{14,6},{16,24},{18,... | collective-permute-start | bytes 184328 | tf_op jit(solution)/shard_map/ppermute | solution.py:24
  27.4 0.1 pad_add_fusion
  27.5 2.3 %collective-permute-done.2.refs_3_ = bf16[320,96]{1,0:T(8,128)(2,1)S(1)} collective-permute-done((bf16[320,96]{1,0:T(8,128)(2,1)S(1)}, bf16[320,96]{1,0:T(8,128)(2,1)S(1)}, u32[]{:S(2)}, u32[]{:S(2)}) %collective-permute-start.2) | collective-permute-done | bytes 61472 | tf_op jit(solution)/shard_map/ppermute | solution.py:24
  29.8 0.7 %pad_maximum_fusion = bf16[640,96]{1,0:T(8,128)(2,1)} fusion(bf16[320,96]{1,0:T(8,128)(2,1)S(1)} %collective-permute-done.2.refs_3_, bf16[160,96]{1,0:T(8,128)(2,1)S(1)} %collective-permute-done.1.refs_2_, bf16[80,96]{1,0:T(8,128)(2,1)S(1)} %collective-permute-done.refs_1_, bf16[80,96]{1,0:T(8,128)(2,1)S(1)} %broadcast_multiply_fusion.refs_0_), kind=kLoop, calls=%fused_computation.3 | loop fusion | flops 491520 | bytes 245760 | tf_op jit(solution)/shard_map/concatenate | solution.py:395
  30.5 1.0 %fusion.9 = (f32[26,512]{1,0:T(8,128)S(1)}, f32[26,512]{1,0:T(8,128)}) fusion(s32[26]{0:T(128)S(1)} %pad_add_fusion), kind=kLoop, calls=%fused_computation.11 | loop fusion | flops 119808 | bytes 106600 | tf_op jit(solution)/shard_map/sin | solution.py:343
  31.5 4.6 %shard_map.121 = (f32[18,9,8,128]{3,2,1,0:T(8,128)S(1)}, f32[9,8,128]{2,1,0:T(8,128)S(1)}, bf16[18,9,8,128]{3,2,1,0:T(8,128)(2,1)S(1)}) custom-call(s32[1]{0:T(128)} %bitcast.6.lev, s32[1]{0:T(128)} %bitcast.5.up, f32[18]{0:T(128)S(1)} %copy-done.5, f32[18]{0:T(128)S(1)} %copy-done.4, f32[18]{0:T(128)S(1)} %copy-done.6, bf16[18,18,8,128]{3,2,1,0:T(8,128)(2,1)} %bitcast.15, ...), custom_call_target="tpu_custom_call" | custom-call | tf_op jit(solution)/shard_map/pallas_call | solution.py:467
  36.1 3.7 %shard_map.122 = (f32[18,9,8,128]{3,2,1,0:T(8,128)S(1)}, f32[9,8,128]{2,1,0:T(8,128)S(1)}) custom-call(s32[1]{0:T(128)} %bitcast.6.lev, s32[1]{0:T(128)} %bitcast.9.up, f32[18]{0:T(128)S(1)} %copy-done.5, f32[18]{0:T(128)S(1)} %copy-done.4, f32[18]{0:T(128)S(1)} %copy-done.6, bf16[18,9,8,128]{3,2,1,0:T(8,128)(2,1)S(1)} %get-tuple-element.23.spectra, ...), custom_call_target="tpu_custom_call" | custom-call | tf_op jit(solution)/shard_map/pallas_call | solution.py:467
  39.8 0.1 collective-permute-start.8
  39.9 0.5 %collective-permute-start.7 = (f32[9,8,128]{2,1,0:T(8,128)S(1)}, f32[9,8,128]{2,1,0:T(8,128)S(1)}, u32[]{:S(2)}, u32[]{:S(2)}) collective-permute-start(f32[9,8,128]{2,1,0:T(8,128)S(1)} %get-tuple-element.27.refs_2_), channel_id=1, source_target_pairs={{0,1},{1,0},{2,3},{3,2},{4,5},{5,4},{6,7},{7,6},{8,9},{9,8},{10,11... | collective-permute-start | bytes 110600 | tf_op jit(solution)/shard_map/ppermute | solution.py:24
  40.4 0.1 fusion.14
  41.2 1.0 %first.1 = (f32[48,512]{1,0:T(8,128)S(1)}, bf16[640,512]{1,0:T(8,128)(2,1)S(1)}, bf16[640,512]{1,0:T(8,128)(2,1)S(1)}, bf16[512,512]{1,0:T(8,128)(2,1)S(1)}) custom-call(f32[26,512]{1,0:T(8,128)S(1)} %copy-done.1, f32[26,512]{1,0:T(8,128)S(1)} %get-tuple-element.35.sines, s32[4,128]{1,0:T(4,128)S(1)} %copy-done.3, ...), custom_call_target="tpu_custom_call" | custom-call | tf_op jit(solution)/shard_map/first/pallas_call | solution.py:416
  42.2 2.0 %fourier.1 = (f32[3,1,512]{2,1,0:T(1,128)}, f32[2,4,128]{2,1,0:T(4,128)S(1)}) custom-call(s32[1]{0:T(128)} %bitcast.band, f32[1]{0:T(128)S(6)} %copy.23.level, f32[48,512]{1,0:T(8,128)S(1)} %get-tuple-element.16.early, bf16[640,96]{1,0:T(8,128)(2,1)} %collective-permute-done.3.last, f32[1,512]{1,0:T(1,128)S(1)} %get-tuple-element.38.phase_cos, ...), custom_call_target="tpu_custom_call" | custom-call | tf_op jit(solution)/shard_map/fourier/pallas_call | solution.py:440
  44.2 0.1 collective-permute-start.6
  44.3 1.1 %collective-permute-done.6.refs_1_ = f32[2,4,128]{2,1,0:T(4,128)S(1)} collective-permute-done((f32[2,4,128]{2,1,0:T(4,128)S(1)}, f32[2,4,128]{2,1,0:T(4,128)S(1)}, u32[]{:S(2)}, u32[]{:S(2)}) %collective-permute-start.6) | collective-permute-done | bytes 4128 | tf_op jit(solution)/shard_map/ppermute | solution.py:24
  45.4 1.8 %result.1 = f32[18,18,8,128]{3,2,1,0:T(8,128)} custom-call(s32[1]{0:T(128)} %bitcast.5.up, f32[18]{0:T(128)S(1)} %copy-done.4, f32[18,9,8,128]{3,2,1,0:T(8,128)S(1)} %get-tuple-element.22.near, f32[18,9,8,128]{3,2,1,0:T(8,128)S(1)} %get-tuple-element.25.far, f32[2,4,128]{2,1,0:T(4,128)S(1)} %get-tuple-element.26.refs_0_, ...), custom_call_target="tpu_custom_call" | custom-call | tf_op jit(solution)/shard_map/result/pallas_call | solution.py:500
  47.2 0.0 collective-permute-done.7.refs_3_
  47.2 0.6 %charnock.1 = f32[4,128]{1,0:T(4,128)} custom-call(s32[1]{0:T(128)} %bitcast.5.up, s32[4,128]{1,0:T(4,128)S(1)} %copy-done.2, f32[2,4,128]{2,1,0:T(4,128)S(1)} %get-tuple-element.26.refs_0_, f32[2,4,128]{2,1,0:T(4,128)S(1)} %collective-permute-done.6.refs_1_, f32[9,8,128]{2,1,0:T(8,128)S(1)} %get-tuple-element.27.refs_2_, ...), custom_call_target="tpu_custom_call" | custom-call | tf_op jit(solution)/shard_map/charnock/pallas_call | solution.py:512
  (24 shorter events, 0.1 us)
Async XLA Ops:
  0.6 2.3 %copy-start = (bf16[80,16,1280]{2,1,0:T(8,128)(2,1)S(1)}, bf16[80,16,1280]{2,1,0:T(8,128)(2,1)}, u32[]{:S(2)}) copy-start(bf16[80,16,1280]{2,1,0:T(8,128)(2,1)} %param.11) | copy-start | bytes 9830404
  2.9 7.9 %copy-start.7 = (s32[8]{0:T(128)S(1)}, s32[8]{0:T(128)}, u32[]{:S(2)}) copy-start(s32[8]{0:T(128)} %constant.60.clone) | copy-start | bytes 100
  4.1 27.4 %copy-start.2 = (s32[4,128]{1,0:T(4,128)S(1)}, s32[4,128]{1,0:T(4,128)}, u32[]{:S(2)}) copy-start(s32[4,128]{1,0:T(4,128)} %land.5) | copy-start | bytes 6148
  4.1 27.4 %copy-start.4 = (f32[18]{0:T(128)S(1)}, f32[18]{0:T(128)}, u32[]{:S(2)}) copy-start(f32[18]{0:T(128)} %rate.5) | copy-start | bytes 220
  4.1 27.4 %copy-start.5 = (f32[18]{0:T(128)S(1)}, f32[18]{0:T(128)}, u32[]{:S(2)}) copy-start(f32[18]{0:T(128)} %courant.3) | copy-start | bytes 220
  4.1 27.4 %copy-start.6 = (f32[18]{0:T(128)S(1)}, f32[18]{0:T(128)}, u32[]{:S(2)}) copy-start(f32[18]{0:T(128)} %breaking.3) | copy-start | bytes 220
  4.3 36.9 %copy-start.3 = (s32[4,128]{1,0:T(4,128)S(1)}, s32[4,128]{1,0:T(4,128)}, u32[]{:S(2)}) copy-start(s32[4,128]{1,0:T(4,128)} %coupling.3) | copy-start | bytes 6148
  4.4 6.4 %collective-permute-start = (bf16[80,96]{1,0:T(8,128)(2,1)S(1)}, bf16[80,96]{1,0:T(8,128)(2,1)S(1)}, u32[]{:S(2)}, u32[]{:S(2)}) collective-permute-start(bf16[80,96]{1,0:T(8,128)(2,1)S(1)} %broadcast_multiply_fusion.refs_0_), channel_id=1, source_target_pairs={{0,2},{2,0},{4,6},{6,4},{8,10},{10,8},{12,14},{14,12},{16,18},{18,... | collective-permute-start | bytes 46088 | tf_op jit(solution)/shard_map/ppermute | solution.py:24
  9.3 22.2 %collective-permute-start.4 = (bf16[18,18,4,128]{3,2,1,0:T(4,128)(2,1)}, bf16[18,18,4,128]{3,2,1,0:T(4,128)(2,1)}, u32[]{:S(2)}, u32[]{:S(2)}) collective-permute-start(bf16[18,18,4,128]{3,2,1,0:T(4,128)(2,1)} %get-tuple-element.21), channel_id=1, source_target_pairs={{0,2},{2,0},{4,6},{6,4},{8,10},{10,8},{12,14},{14,12},{16,18},{18,... | collective-permute-start | bytes 995336 | tf_op jit(solution)/shard_map/ppermute | solution.py:380
  9.4 26.7 %collective-permute-start.5 = (bf16[18,18,4,128]{3,2,1,0:T(4,128)(2,1)}, bf16[18,18,4,128]{3,2,1,0:T(4,128)(2,1)}, u32[]{:S(2)}, u32[]{:S(2)}) collective-permute-start(bf16[18,18,4,128]{3,2,1,0:T(4,128)(2,1)} %get-tuple-element.24), channel_id=1, source_target_pairs={{2,4},{6,8},{10,12},{14,16},{18,20},{22,24},{26,28},{4,2},{8,6},{1... | collective-permute-start | bytes 995336 | tf_op jit(solution)/shard_map/ppermute | solution.py:382
  10.8 14.4 %collective-permute-start.1 = (bf16[160,96]{1,0:T(8,128)(2,1)S(1)}, bf16[160,96]{1,0:T(8,128)(2,1)S(1)}, u32[]{:S(2)}, u32[]{:S(2)}) collective-permute-start(bf16[160,96]{1,0:T(8,128)(2,1)S(1)} %pad_maximum_fusion.2), channel_id=1, source_target_pairs={{0,16},{2,18},{4,20},{6,22},{8,24},{10,26},{12,28},{14,30},{16,0},... | collective-permute-start | bytes 92168 | tf_op jit(solution)/shard_map/ppermute | solution.py:24
  25.3 4.5 %collective-permute-start.2 = (bf16[320,96]{1,0:T(8,128)(2,1)S(1)}, bf16[320,96]{1,0:T(8,128)(2,1)S(1)}, u32[]{:S(2)}, u32[]{:S(2)}) collective-permute-start(bf16[320,96]{1,0:T(8,128)(2,1)S(1)} %pad_maximum_fusion.1), channel_id=1, source_target_pairs={{0,8},{2,10},{4,12},{6,14},{8,0},{10,2},{12,4},{14,6},{16,24},{18,... | collective-permute-start | bytes 184328 | tf_op jit(solution)/shard_map/ppermute | solution.py:24
  30.5 11.7 %collective-permute-start.3 = (bf16[640,96]{1,0:T(8,128)(2,1)}, bf16[640,96]{1,0:T(8,128)(2,1)}, u32[]{:S(2)}, u32[]{:S(2)}) collective-permute-start(bf16[640,96]{1,0:T(8,128)(2,1)} %pad_maximum_fusion), channel_id=1, source_target_pairs={{0,4},{2,6},{4,0},{6,2},{8,12},{10,14},{12,8},{14,10},{16,20},{18,... | collective-permute-start | bytes 368648 | tf_op jit(solution)/shard_map/ppermute | solution.py:24
  31.5 9.7 %copy-start.1 = (f32[26,512]{1,0:T(8,128)S(1)}, f32[26,512]{1,0:T(8,128)}, u32[]{:S(2)}) copy-start(f32[26,512]{1,0:T(8,128)} %get-tuple-element.36.cosines) | copy-start | bytes 159748
  39.8 7.3 %collective-permute-start.8 = (f32[9,8,128]{2,1,0:T(8,128)S(1)}, f32[9,8,128]{2,1,0:T(8,128)S(1)}, u32[]{:S(2)}, u32[]{:S(2)}) collective-permute-start(f32[9,8,128]{2,1,0:T(8,128)S(1)} %get-tuple-element.28.refs_4_), channel_id=1, source_target_pairs={{0,1},{1,0},{2,3},{3,2},{4,5},{5,4},{6,7},{7,6},{8,9},{9,8},{10,11... | collective-permute-start | bytes 110600 | tf_op jit(solution)/shard_map/ppermute | solution.py:24
  39.9 7.3 %collective-permute-start.7 = (f32[9,8,128]{2,1,0:T(8,128)S(1)}, f32[9,8,128]{2,1,0:T(8,128)S(1)}, u32[]{:S(2)}, u32[]{:S(2)}) collective-permute-start(f32[9,8,128]{2,1,0:T(8,128)S(1)} %get-tuple-element.27.refs_2_), channel_id=1, source_target_pairs={{0,1},{1,0},{2,3},{3,2},{4,5},{5,4},{6,7},{7,6},{8,9},{9,8},{10,11... | collective-permute-start | bytes 110600 | tf_op jit(solution)/shard_map/ppermute | solution.py:24
  44.2 1.2 %collective-permute-start.6 = (f32[2,4,128]{2,1,0:T(4,128)S(1)}, f32[2,4,128]{2,1,0:T(4,128)S(1)}, u32[]{:S(2)}, u32[]{:S(2)}) collective-permute-start(f32[2,4,128]{2,1,0:T(4,128)S(1)} %get-tuple-element.26.refs_0_), channel_id=1, source_target_pairs={{0,1},{1,0},{2,3},{3,2},{4,5},{5,4},{6,7},{7,6},{8,9},{9,8},{10,11... | collective-permute-start | bytes 12296 | tf_op jit(solution)/shard_map/ppermute | solution.py:24

commit v4 on v3

--- a/solution.py
+++ b/solution.py
@@ -42,6 +42,13 @@
 
 def params(mib):
     return pltpu.CompilerParams(vmem_limit_bytes=mib * 2**20)
+
+
+def join_kernel(*refs):
+    at = 0
+    for part in refs[:-1]:
+        refs[-1][at : at + part.shape[0], :] = part[...]
+        at += part.shape[0]
 
 
 def pack_kernel(band, spectra, low, high, buffer, sems):
@@ -183,9 +190,10 @@
     waves = wave_cos.shape[0]
     blocks = cos_table.shape[0] // waves
     tens = waves // 8
+    units = slice(blocks + tens, blocks + tens + 8)
     for j in range(tens):
         ca, sa = cosines[blocks + j : blocks + j + 1, :], sines[blocks + j : blocks + j + 1, :]
-        cb, sb = cosines[blocks + tens :, :], sines[blocks + tens :, :]
+        cb, sb = cosines[units, :], sines[units, :]
         wave_cos[8 * j : 8 * j + 8, :] = ca * cb - sa * sb
         wave_sin[8 * j : 8 * j + 8, :] = sa * cb + ca * sb
 
@@ -206,64 +214,78 @@
 
 
 def one_hot(coupling, pick):
-    longitude = lanes_of(coupling[...]) % LON_W
+    longitude = lanes_of(coupling[...]) % 128
     columns = lax.broadcasted_iota(jnp.int32, pick.shape, 0)
     pick[...] = (columns == longitude).astype(jnp.float32).astype(jnp.bfloat16)
 
 
-def turned(parts, hold):
+def synthesis(groups, phases, cosines, sines, cos_table, sin_table):
+    stacked = jnp.concatenate(groups, axis=0) if len(groups) > 1 else groups[0]
+    by_cos = dot(stacked, cos_table[...])
+    by_sin = dot(stacked, sin_table[...])
+    rows = groups[0].shape[0] // 2
+    result = None
+    for g, phase in enumerate(phases):
+        first, middle, end = 2 * g * rows, (2 * g + 1) * rows, (2 * g + 2) * rows
+        value = by_cos[first:middle] + by_sin[middle:end]
+        if phase:
+            at = cosines.shape[0] - 4 + phase
+            imag = by_cos[middle:end] - by_sin[first:middle]
+            value = cosines[at : at + 1, :] * value - sines[at : at + 1, :] * imag
+        result = value if result is None else result + value
+    return result
+
+
+def first_kernel(count, built, cosines, sines, coupling, *refs):
+    if built:
+        parts, (early, cos_table, sin_table, pick, legs, wave_cos, wave_sin) = (
+            refs[:count], refs[count:],
+        )
+        build_basis(cosines, sines, cos_table, sin_table, wave_cos, wave_sin)
+    else:
+        cos_table, sin_table = refs[:2]
+        parts, (early, pick, legs) = refs[2 : 2 + count], refs[2 + count :]
+    one_hot(coupling, pick)
     at = 0
-    for part in parts:
-        count = part.shape[0]
-        hold[at : at + count, :] = part[...]
-        at += count
-    return hold[...].T
-
-
-def real_sum(legs, cos_table, sin_table):
-    rows = legs.shape[0] // 2
-    return dot(legs[:rows], cos_table[...]) + dot(legs[rows:], sin_table[...])
-
-
-def first_kernel(count, cosines, sines, coupling, *refs):
-    parts = refs[:count]
-    early, cos_table, sin_table, pick, legs, wave_cos, wave_sin = refs[count:]
-    build_basis(cosines, sines, cos_table, sin_table, wave_cos, wave_sin)
-    one_hot(coupling, pick)
-    early[...] = real_sum(turned(parts, legs), cos_table, sin_table)
-
-
-def sum_kernel(count, cos_table, sin_table, coupling, *refs):
-    parts = refs[:count]
-    early, pick, legs = refs[count:]
-    one_hot(coupling, pick)
-    early[...] = real_sum(turned(parts, legs), cos_table, sin_table)
+    for part in parts[:-1]:
+        legs[at : at + part.shape[0], :] = part[...]
+        at += part.shape[0]
+    groups = [legs[...].T, parts[-1][...].T]
+    early[...] = synthesis(groups, (0, 1), cosines, sines, cos_table, sin_table)
 
 
 def fourier_kernel(
-    lats, share, band, level, early, last, phase_cos, phase_sin, cos_table, sin_table, pick, coupling,
+    lats, share, band, level, early, last, cosines, sines, cos_table, sin_table, pick, coupling,
     grid, wind, hold,
 ):
     legs = last[...].T
-    rows = legs.shape[0] // 2
-    by_cos = dot(legs, cos_table[...])
-    by_sin = dot(legs, sin_table[...])
-    real = by_cos[:rows] + by_sin[rows:]
-    imag = by_cos[rows:] - by_sin[:rows]
-    fields = early[...] + (phase_cos[...] * real - phase_sin[...] * imag)
+    middle = legs.shape[1] // 2
+    groups = [legs[:, :middle], legs[:, middle:]]
+    fields = early[...] + synthesis(groups, (2, 3), cosines, sines, cos_table, sin_table)
     hold[...] = fields
     for f in range(FIELDS):
         grid[f] = hold[pl.ds(f * lats + band[0] * share, share), :]
     speed = fields[: 2 * lats] * level[0]
     top = speed.astype(jnp.bfloat16)
     low = (speed - top.astype(jnp.float32)).astype(jnp.bfloat16)
-    found = dot(top, pick[...]) + dot(low, pick[...])
-    latitude = lanes_of(coupling[...]) // LON_W
-    here = lax.broadcasted_iota(jnp.int32, (lats, latitude.shape[1]), 0) == latitude
+    pieces = [part[:, at : at + 128] for part in (top, low) for at in range(0, LON_W, 128)]
+    found = dot(jnp.concatenate(pieces, axis=0), pick[...])
+    where = lanes_of(coupling[...])
+    latitude = where // LON_W
+    group = where % LON_W // 128
+    count = LON_W // 128
+    row = lax.broadcasted_iota(jnp.int32, (lats, where.shape[1]), 0)
+    values = [None, None]
+    for a in range(count):
+        here = (row == latitude) & (group == a)
+        for c in range(2):
+            first = (2 * a + c) * lats
+            second = (2 * (count + a) + c) * lats
+            part = found[first : first + lats] + found[second : second + lats]
+            part = jnp.where(here, part, 0.0)
+            values[c] = part if a == 0 else values[c] + part
     for c in range(2):
-        value = jnp.sum(
-            jnp.where(here, found[c * lats : (c + 1) * lats], 0.0), axis=0, keepdims=True
-        )
+        value = jnp.sum(values[c], axis=0, keepdims=True)
         for r in range(wind.shape[1]):
             wind[c, r : r + 1, :] = value[:, r * 128 : (r + 1) * 128]
 
@@ -391,52 +413,62 @@
 
     order = [0]
     parts = [legs]
-    for bit in bits_of(bands):
-        together = jnp.concatenate(parts, axis=0) if len(parts) > 1 else legs
+    bits = bits_of(bands)
+    small = lats <= 32
+    for bit in bits:
+        if len(parts) == len(bits) and small:
+            rows = sum(part.shape[0] for part in parts)
+            together = pl.pallas_call(
+                join_kernel,
+                out_shape=pltpu.VMEM((rows, legs.shape[1]), jnp.bfloat16),
+                in_specs=[VMEM] * len(parts),
+                out_specs=VMEM,
+                compiler_params=params(2),
+                name="join",
+            )(*parts)
+        else:
+            together = jnp.concatenate(parts, axis=0) if len(parts) > 1 else legs
         parts = parts + [swapped(together, "band", bit)]
-        if len(parts) <= bands.bit_length() - 1:
+        if len(parts) < len(bits):
             order = order + [q ^ (1 << bit) for q in order]
-    blocks = band ^ jnp.asarray(order, dtype=jnp.int32)
+
+    def flipped(bit):
+        return (waves << bit) * (1 - 2 * (jnp.right_shift(band, bit) % 2))
 
     count = len(parts) - 1
-    total = bands * waves // 2
+    total_rows = bands * waves // 4
     points = tile_rows * tile_cols
     columns = 2 * FIELDS * lats
-    last = bits_of(bands)[-1]
-    shift = (waves << last) * (1 - 2 * (jnp.right_shift(band, last) % 2))
-    table = pltpu.VMEM((total, LON_W), jnp.bfloat16)
-    pick_shape = jax.ShapeDtypeStruct((LON_W, points), jnp.bfloat16)
+    table = pltpu.VMEM((total_rows, LON_W), jnp.bfloat16)
+    pick_shape = jax.ShapeDtypeStruct((128, points), jnp.bfloat16)
     fields_shape = jax.ShapeDtypeStruct((FIELDS * lats, LON_W), jnp.float32)
-    legs_scratch = pltpu.VMEM((total, columns), jnp.bfloat16)
-    size = 10 if lats <= 32 else 32
-    if waves % 16 == 0:
-        tens = waves // 8
-        listed = [blocks * waves, 8 * jnp.arange(tens, dtype=jnp.int32)]
-        cos_rows, sin_rows = trig(jnp.concatenate(listed + [jnp.arange(8, dtype=jnp.int32)]))
-        early, cos_table, sin_table, pick = pl.pallas_call(
-            functools.partial(first_kernel, count),
-            out_shape=[fields_shape, table, table, pick_shape],
-            in_specs=[VMEM] * (3 + count),
-            out_specs=[VMEM] * 4,
-            scratch_shapes=[legs_scratch] + [pltpu.VMEM((waves, LON_W), jnp.float32)] * 2,
-            compiler_params=params(size),
-            name="first",
-        )(cos_rows, sin_rows, coupling, *parts[:-1])
-    else:
+    legs_scratch = pltpu.VMEM((total_rows, columns), jnp.bfloat16)
+    size = 10 if small else 36
+    built = waves % 16 == 0
+    blocks = band ^ jnp.asarray(order, dtype=jnp.int32)
+    one, two = flipped(bits[-2]), flipped(bits[-1])
+    listed = [jnp.stack([one, two, one + two])]
+    if built:
+        units = jnp.arange(8, dtype=jnp.int32)
+        listed = [blocks * waves, 8 * jnp.arange(waves // 8, dtype=jnp.int32), units] + listed
+    cos_rows, sin_rows = trig(jnp.concatenate(listed))
+    tables = []
+    if not built:
         cos_table, sin_table = trig(
             (blocks[:, None] * waves + jnp.arange(waves, dtype=jnp.int32)).reshape(-1)
         )
-        cos_table, sin_table = cos_table.astype(jnp.bfloat16), -sin_table.astype(jnp.bfloat16)
-        early, pick = pl.pallas_call(
-            functools.partial(sum_kernel, count),
-            out_shape=[fields_shape, pick_shape],
-            in_specs=[VMEM] * (3 + count),
-            out_specs=[VMEM] * 2,
-            scratch_shapes=[legs_scratch],
-            compiler_params=params(size),
-            name="first",
-        )(cos_table, sin_table, coupling, *parts[:-1])
-    phase_cos, phase_sin = trig(shift.reshape(1))
+        tables = [cos_table.astype(jnp.bfloat16), -sin_table.astype(jnp.bfloat16)]
+    outs = pl.pallas_call(
+        functools.partial(first_kernel, count, built),
+        out_shape=[fields_shape] + [table, table] * built + [pick_shape],
+        in_specs=[VMEM] * (3 + len(tables) + count),
+        out_specs=[VMEM] * (2 + 2 * built),
+        scratch_shapes=[legs_scratch] + [pltpu.VMEM((waves, LON_W), jnp.float32)] * (2 * built),
+        compiler_params=params(size),
+        name="first",
+    )(cos_rows, sin_rows, coupling, *tables, *parts[:-1])
+    early, pick = outs[0], outs[-1]
+    tables = tables or outs[1:3]
     grid, wind = pl.pallas_call(
         functools.partial(fourier_kernel, lats, share),
         out_shape=[
@@ -449,8 +481,7 @@
         compiler_params=params(size),
         name="fourier",
     )(
-        band.reshape(1), level_weights, early, parts[-1], phase_cos, phase_sin, cos_table, sin_table,
-        pick, coupling,
+        band.reshape(1), level_weights, early, in_vmem(parts[-1]) if small else parts[-1], cos_rows, sin_rows, *tables, pick, coupling
     )
     grid = jnp.transpose(grid, (1, 0, 2)).reshape(share, 1, FIELDS, LON_W)
 

time: 48.1 us -> 45.7 us (0.950)
  other arithmetic: 1.97 us -> 0.47 us
  local copies, waits for them, and re-layouts: 2.54 us -> 3.8 us
  Pallas kernels: 15.6 us -> 14.4 us
  waiting for transfers between devices: 11.8 us -> 10.8 us
    ppermute x7, waiting for transfers between devices: 11.8 us -> 10.7 us  [swapped(): lax.ppermute(block, axis, [(i, i ^ 1 << apart) for i in range(count)])]
    pallas_call x1, Pallas kernels: 1.99 us -> 1.07 us  [on_device_(): pl.pallas_call(functools.partial(fourier_kernel, lats, share), out_shape=...]
    concatenate x0 -> x1, local copies, waits for them, and re-layouts: none -> 0.73 us  [on_device_(): cos_rows, sin_rows = trig(jnp.concatenate(listed))]
    concatenate x3 -> x2, other arithmetic: 0.75 us -> 0.03 us  [on_device_(): together = jnp.concatenate(parts, axis=0) if len(parts) > 1 else legs]
    sin x2 -> x1, other arithmetic: 1.06 us -> 0.35 us  [trig(): return (jnp.cos(angles), jnp.sin(angles))]
    iota x1, local copies, waits for them, and re-layouts: 0.01 us -> 0.51 us  [on_device_(): units = jnp.arange(8, dtype=jnp.int32)]
    pallas_call x1 -> x2, Pallas kernels: 1.04 us -> 0.76 us  [the longest x1 0.73 us: on_device_(): pl.pallas_call(functools.partial(first_kernel, count, built), out_shape=[...]
    unnamed x17 -> x15, local copies, waits for them, and re-layouts: 2.3 us -> 2.31 us
  transfers between devices with their start and end apart: 9 -> 9, of which waited for: 3 -> 3; matrix products, arithmetic and copies ran while one was open for 4% -> 4% of each run, Pallas kernels for 31% -> 30%
where the time goes in v4:
time: 45.7 us; the launch traced here: 45.4 us
  Pallas kernels  14.4 us (32%)
  starting transfers between devices  13.3 us (29%)
  waiting for transfers between devices  10.8 us (24%)
  local copies, waits for them, and re-layouts  3.8 us (8%)
  between operations  1.49 us (3%)
  matrix products  1.17 us (3%)
  other arithmetic  0.47 us (1%)
    ppermute x7, starting transfers between devices, swapped(): lax.ppermute(block, axis, [(i, i ^ 1 << apart) for i in range(count)])  11.8 us
    ppermute x7, waiting for transfers between devices, swapped(): lax.ppermute(block, axis, [(i, i ^ 1 << apart) for i in range(count)])  10.7 us
    pallas_call x2, Pallas kernels, advected(): pl.pallas_call(functools.partial(advect_kernel, directions), out_shape=[h...  8.29 us
    unnamed x15, local copies, waits for them, and re-layouts  2.31 us
    pallas_call x1, Pallas kernels, on_device_(): pl.pallas_call(pack_kernel, out_shape=[half_shape] * 2, in_specs=[SMEM, h...  1.91 us
    pallas_call x1, Pallas kernels, on_device_(): pl.pallas_call(functools.partial(result_kernel, directions, levs), out_sh...  1.79 us
    ppermute x1, starting transfers between devices, on_device_(): high = lax.ppermute(high, 'band', across + [(j, i) for i, j in across])  1.4 us
    dot_general x1, matrix products, on_device_(): lax.dot_general(stacked, legendre, (((2,), (2,)), ((0,), (0,))), preferre...  1.17 us
  transfers between devices with their start and end apart: 9, of which 3 were waited for; matrix products, arithmetic and copies ran while one was open for 4% of the time, Pallas kernels for 30%

profile of v4, /device:TPU:0, one launch (start us, length us, event | category | flops | bytes accessed | tf_op | source)
XLA Modules:
  0.0 45.4 jit_solution(3998314058397444444)
XLA Ops:
  0.6 0.0 copy-start
  0.7 1.6 %copy.14 = bf16[80,2,1,3,1280]{4,0,3,1,2:T(8,128)(2,1)S(1)} copy(bf16[80,2,1,3,1280]{4,1,3,2,0:T(2,128)(2,1)} %param.10) | data formatting | bytes 2457600 | tf_op args[0]
  2.2 0.7 %copy-done = bf16[80,16,1280]{2,1,0:T(8,128)(2,1)S(1)} copy-done((bf16[80,16,1280]{2,1,0:T(8,128)(2,1)S(1)}, bf16[80,16,1280]{2,1,0:T(8,128)(2,1)}, u32[]{:S(2)}) %copy-start) | copy-done | bytes 3276824
  2.9 0.0 copy-start.5
  3.0 1.2 %fusion.2 = bf16[80,6,16]{2,1,0:T(8,128)(2,1)S(1)} fusion(bf16[80,16,1280]{2,1,0:T(8,128)(2,1)S(1)} %copy-done, bf16[80,6,1280]{2,0,1:T(8,128)(2,1)S(1)} %bitcast.17), kind=kOutput, calls=%fused_computation.2 | convolution fusion | flops 19668480 | bytes 4520960 | tf_op jit(solution)/shard_map/dot_general | solution.py:407
  4.1 0.1 copy.16
  4.3 0.1 copy.17
  4.4 0.1 broadcast_multiply_fusion.refs_0_
  4.5 3.0 %collective-permute-start = (bf16[80,96]{1,0:T(8,128)(2,1)S(1)}, bf16[80,96]{1,0:T(8,128)(2,1)S(1)}, u32[]{:S(2)}, u32[]{:S(2)}) collective-permute-start(bf16[80,96]{1,0:T(8,128)(2,1)S(1)} %broadcast_multiply_fusion.refs_0_), channel_id=1, source_target_pairs={{0,2},{2,0},{4,6},{6,4},{8,10},{10,8},{12,14},{14,12},{16,18},{18,... | collective-permute-start | bytes 46088 | tf_op jit(solution)/shard_map/ppermute | solution.py:24
  7.4 1.9 %pack.1 = (bf16[18,18,4,128]{3,2,1,0:T(4,128)(2,1)}, bf16[18,18,4,128]{3,2,1,0:T(4,128)(2,1)}) custom-call(s32[1]{0:T(128)} %bitcast.band, bf16[18,36,4,128]{3,2,1,0:T(4,128)(2,1)} %spectra.1), custom_call_target="tpu_custom_call" | custom-call | tf_op jit(solution)/shard_map/pack/pallas_call | solution.py:390
  9.4 0.1 collective-permute-start.4
  9.5 1.4 %collective-permute-start.5 = (bf16[18,18,4,128]{3,2,1,0:T(4,128)(2,1)}, bf16[18,18,4,128]{3,2,1,0:T(4,128)(2,1)}, u32[]{:S(2)}, u32[]{:S(2)}) collective-permute-start(bf16[18,18,4,128]{3,2,1,0:T(4,128)(2,1)} %get-tuple-element.24), channel_id=1, source_target_pairs={{2,4},{6,8},{10,12},{14,16},{18,20},{22,24},{26,28},{4,2},{8,6},{1... | collective-permute-start | bytes 995336 | tf_op jit(solution)/shard_map/ppermute | solution.py:404
  10.9 6.0 %collective-permute-start.1 = (bf16[160,96]{1,0:T(8,128)(2,1)S(1)}, bf16[160,96]{1,0:T(8,128)(2,1)S(1)}, u32[]{:S(2)}, u32[]{:S(2)}) collective-permute-start(bf16[160,96]{1,0:T(8,128)(2,1)S(1)} %pad_maximum_fusion.1), channel_id=1, source_target_pairs={{0,16},{2,18},{4,20},{6,22},{8,24},{10,26},{12,28},{14,30},{16,0},... | collective-permute-start | bytes 92168 | tf_op jit(solution)/shard_map/ppermute | solution.py:24
  16.9 8.4 %collective-permute-done.1.refs_2_ = bf16[160,96]{1,0:T(8,128)(2,1)S(1)} collective-permute-done((bf16[160,96]{1,0:T(8,128)(2,1)S(1)}, bf16[160,96]{1,0:T(8,128)(2,1)S(1)}, u32[]{:S(2)}, u32[]{:S(2)}) %collective-permute-start.1) | collective-permute-done | bytes 30752 | tf_op jit(solution)/shard_map/ppermute | solution.py:24
  25.3 2.1 %collective-permute-start.2 = (bf16[320,96]{1,0:T(8,128)(2,1)S(1)}, bf16[320,96]{1,0:T(8,128)(2,1)S(1)}, u32[]{:S(2)}, u32[]{:S(2)}) collective-permute-start(bf16[320,96]{1,0:T(8,128)(2,1)S(1)} %pad_maximum_fusion), channel_id=1, source_target_pairs={{0,8},{2,10},{4,12},{6,14},{8,0},{10,2},{12,4},{14,6},{16,24},{18,... | collective-permute-start | bytes 184328 | tf_op jit(solution)/shard_map/ppermute | solution.py:24
  27.4 0.5 %iota.16 = s32[8]{0:T(128)} iota(), iota_dimension=0 | iota | bytes 32 | tf_op jit(solution)/shard_map/iota | solution.py:452
  27.9 0.7 %concatenate.9 = s32[25]{0:T(128)S(1)} concatenate(s32[4]{0:T(128)S(1)} %xor_multiply_fusion, s32[10]{0:T(128)S(1)} %iota_multiply_fusion, s32[8]{0:T(128)} %iota.16, s32[1]{0:T(128)} %bitcast.1, s32[1]{0:T(128)} %bitcast.2, s32[1]{0:T(128)} %bitcast.3), dimensions={0} | concatenate | bytes 200 | tf_op jit(solution)/shard_map/concatenate | solution.py:454
  28.6 1.2 %collective-permute-done.2.refs_3_ = bf16[320,96]{1,0:T(8,128)(2,1)S(1)} collective-permute-done((bf16[320,96]{1,0:T(8,128)(2,1)S(1)}, bf16[320,96]{1,0:T(8,128)(2,1)S(1)}, u32[]{:S(2)}, u32[]{:S(2)}) %collective-permute-start.2) | collective-permute-done | bytes 61472 | tf_op jit(solution)/shard_map/ppermute | solution.py:24
  29.9 0.1 collective-permute-start.3
  29.9 0.0 collective-permute-done.4
  30.0 4.6 %shard_map.121 = (f32[18,9,8,128]{3,2,1,0:T(8,128)S(1)}, f32[9,8,128]{2,1,0:T(8,128)S(1)}, bf16[18,9,8,128]{3,2,1,0:T(8,128)(2,1)S(1)}) custom-call(s32[1]{0:T(128)} %bitcast.9.lev, s32[1]{0:T(128)} %bitcast.8.up, f32[18]{0:T(128)S(1)} %copy-done.4, f32[18]{0:T(128)S(1)} %copy-done.3, f32[18]{0:T(128)S(1)} %copy-done.5, bf16[18,18,8,128]{3,2,1,0:T(8,128)(2,1)} %bitcast.18, ...), custom_call_target="tpu_custom_call" | custom-call | tf_op jit(solution)/shard_map/pallas_call | solution.py:498
  34.6 0.1 collective-permute-start.7
  34.6 3.7 %shard_map.122 = (f32[18,9,8,128]{3,2,1,0:T(8,128)S(1)}, f32[9,8,128]{2,1,0:T(8,128)S(1)}) custom-call(s32[1]{0:T(128)} %bitcast.9.lev, s32[1]{0:T(128)} %bitcast.12.up, f32[18]{0:T(128)S(1)} %copy-done.4, f32[18]{0:T(128)S(1)} %copy-done.3, f32[18]{0:T(128)S(1)} %copy-done.5, bf16[18,9,8,128]{3,2,1,0:T(8,128)(2,1)S(1)} %get-tuple-element.23.spectra, ...), custom_call_target="tpu_custom_call" | custom-call | tf_op jit(solution)/shard_map/pallas_call | solution.py:498
  38.4 0.6 %collective-permute-start.8 = (f32[9,8,128]{2,1,0:T(8,128)S(1)}, f32[9,8,128]{2,1,0:T(8,128)S(1)}, u32[]{:S(2)}, u32[]{:S(2)}) collective-permute-start(f32[9,8,128]{2,1,0:T(8,128)S(1)} %get-tuple-element.28.refs_4_), channel_id=1, source_target_pairs={{0,1},{1,0},{2,3},{3,2},{4,5},{5,4},{6,7},{7,6},{8,9},{9,8},{10,11... | collective-permute-start | bytes 110600 | tf_op jit(solution)/shard_map/ppermute | solution.py:24
  38.9 0.3 fusion.9
  39.9 0.7 %first.1 = (f32[48,512]{1,0:T(8,128)S(1)}, bf16[320,512]{1,0:T(8,128)(2,1)S(1)}, bf16[320,512]{1,0:T(8,128)(2,1)S(1)}, bf16[128,512]{1,0:T(8,128)(2,1)S(1)}) custom-call(f32[25,512]{1,0:T(8,128)S(1)} %get-tuple-element.36.cosines, f32[25,512]{1,0:T(8,128)S(1)} %get-tuple-element.35.sines, s32[4,128]{1,0:T(4,128)S(1)} %copy-done.2, ...), custom_call_target="tpu_custom_call" | custom-call | tf_op jit(solution)/shard_map/first/pallas_call | solution.py:461
  40.7 0.0 collective-permute-done.3.last
  40.7 1.1 %fourier.1 = (f32[3,1,512]{2,1,0:T(1,128)}, f32[2,4,128]{2,1,0:T(4,128)S(1)}) custom-call(s32[1]{0:T(128)} %bitcast.band, f32[1]{0:T(128)S(6)} %copy.23.level, f32[48,512]{1,0:T(8,128)S(1)} %get-tuple-element.16.early, bf16[640,96]{1,0:T(8,128)(2,1)S(1)} %collective-permute-done.3.last, f32[25,512]{1,0:T(8,128)S(1)} %get-tuple-element.36.cosines, ...), custom_call_target="tpu_custom_call" | custom-call | tf_op jit(solution)/shard_map/fourier/pallas_call | solution.py:472
  41.8 0.0 collective-permute-start.6
  41.8 1.2 %collective-permute-done.6.refs_1_ = f32[2,4,128]{2,1,0:T(4,128)S(1)} collective-permute-done((f32[2,4,128]{2,1,0:T(4,128)S(1)}, f32[2,4,128]{2,1,0:T(4,128)S(1)}, u32[]{:S(2)}, u32[]{:S(2)}) %collective-permute-start.6) | collective-permute-done | bytes 4128 | tf_op jit(solution)/shard_map/ppermute | solution.py:24
  42.9 1.8 %result.1 = f32[18,18,8,128]{3,2,1,0:T(8,128)} custom-call(s32[1]{0:T(128)} %bitcast.8.up, f32[18]{0:T(128)S(1)} %copy-done.3, f32[18,9,8,128]{3,2,1,0:T(8,128)S(1)} %get-tuple-element.22.near, f32[18,9,8,128]{3,2,1,0:T(8,128)S(1)} %get-tuple-element.25.far, f32[2,4,128]{2,1,0:T(4,128)S(1)} %get-tuple-element.26.refs_0_, ...), custom_call_target="tpu_custom_call" | custom-call | tf_op jit(solution)/shard_map/result/pallas_call | solution.py:531
  44.7 0.6 %charnock.1 = f32[4,128]{1,0:T(4,128)} custom-call(s32[1]{0:T(128)} %bitcast.8.up, s32[4,128]{1,0:T(4,128)S(1)} %copy-done.1, f32[2,4,128]{2,1,0:T(4,128)S(1)} %get-tuple-element.26.refs_0_, f32[2,4,128]{2,1,0:T(4,128)S(1)} %collective-permute-done.6.refs_1_, f32[9,8,128]{2,1,0:T(8,128)S(1)} %get-tuple-element.27.refs_2_, ...), custom_call_target="tpu_custom_call" | custom-call | tf_op jit(solution)/shard_map/charnock/pallas_call | solution.py:543
  (21 shorter events, 0.1 us)
Async XLA Ops:
  0.6 2.3 %copy-start = (bf16[80,16,1280]{2,1,0:T(8,128)(2,1)S(1)}, bf16[80,16,1280]{2,1,0:T(8,128)(2,1)}, u32[]{:S(2)}) copy-start(bf16[80,16,1280]{2,1,0:T(8,128)(2,1)} %param.11) | copy-start | bytes 9830404
  2.9 14.0 %copy-start.6 = (s32[4]{0:T(128)S(1)}, s32[4]{0:T(128)}, u32[]{:S(2)}) copy-start(s32[4]{0:T(128)} %constant.59.clone) | copy-start | bytes 52
  2.9 27.0 %copy-start.1 = (s32[4,128]{1,0:T(4,128)S(1)}, s32[4,128]{1,0:T(4,128)}, u32[]{:S(2)}) copy-start(s32[4,128]{1,0:T(4,128)} %land.5) | copy-start | bytes 6148
  2.9 27.0 %copy-start.3 = (f32[18]{0:T(128)S(1)}, f32[18]{0:T(128)}, u32[]{:S(2)}) copy-start(f32[18]{0:T(128)} %rate.5) | copy-start | bytes 220
  2.9 27.0 %copy-start.4 = (f32[18]{0:T(128)S(1)}, f32[18]{0:T(128)}, u32[]{:S(2)}) copy-start(f32[18]{0:T(128)} %courant.3) | copy-start | bytes 220
  2.9 27.0 %copy-start.5 = (f32[18]{0:T(128)S(1)}, f32[18]{0:T(128)}, u32[]{:S(2)}) copy-start(f32[18]{0:T(128)} %breaking.3) | copy-start | bytes 220
  4.3 35.7 %copy-start.2 = (s32[4,128]{1,0:T(4,128)S(1)}, s32[4,128]{1,0:T(4,128)}, u32[]{:S(2)}) copy-start(s32[4,128]{1,0:T(4,128)} %coupling.3) | copy-start | bytes 6148
  4.5 6.4 %collective-permute-start = (bf16[80,96]{1,0:T(8,128)(2,1)S(1)}, bf16[80,96]{1,0:T(8,128)(2,1)S(1)}, u32[]{:S(2)}, u32[]{:S(2)}) collective-permute-start(bf16[80,96]{1,0:T(8,128)(2,1)S(1)} %broadcast_multiply_fusion.refs_0_), channel_id=1, source_target_pairs={{0,2},{2,0},{4,6},{6,4},{8,10},{10,8},{12,14},{14,12},{16,18},{18,... | collective-permute-start | bytes 46088 | tf_op jit(solution)/shard_map/ppermute | solution.py:24
  9.4 20.6 %collective-permute-start.4 = (bf16[18,18,4,128]{3,2,1,0:T(4,128)(2,1)}, bf16[18,18,4,128]{3,2,1,0:T(4,128)(2,1)}, u32[]{:S(2)}, u32[]{:S(2)}) collective-permute-start(bf16[18,18,4,128]{3,2,1,0:T(4,128)(2,1)} %get-tuple-element.21), channel_id=1, source_target_pairs={{0,2},{2,0},{4,6},{6,4},{8,10},{10,8},{12,14},{14,12},{16,18},{18,... | collective-permute-start | bytes 995336 | tf_op jit(solution)/shard_map/ppermute | solution.py:402
  9.5 25.2 %collective-permute-start.5 = (bf16[18,18,4,128]{3,2,1,0:T(4,128)(2,1)}, bf16[18,18,4,128]{3,2,1,0:T(4,128)(2,1)}, u32[]{:S(2)}, u32[]{:S(2)}) collective-permute-start(bf16[18,18,4,128]{3,2,1,0:T(4,128)(2,1)} %get-tuple-element.24), channel_id=1, source_target_pairs={{2,4},{6,8},{10,12},{14,16},{18,20},{22,24},{26,28},{4,2},{8,6},{1... | collective-permute-start | bytes 995336 | tf_op jit(solution)/shard_map/ppermute | solution.py:404
  10.9 14.4 %collective-permute-start.1 = (bf16[160,96]{1,0:T(8,128)(2,1)S(1)}, bf16[160,96]{1,0:T(8,128)(2,1)S(1)}, u32[]{:S(2)}, u32[]{:S(2)}) collective-permute-start(bf16[160,96]{1,0:T(8,128)(2,1)S(1)} %pad_maximum_fusion.1), channel_id=1, source_target_pairs={{0,16},{2,18},{4,20},{6,22},{8,24},{10,26},{12,28},{14,30},{16,0},... | collective-permute-start | bytes 92168 | tf_op jit(solution)/shard_map/ppermute | solution.py:24
  25.3 4.5 %collective-permute-start.2 = (bf16[320,96]{1,0:T(8,128)(2,1)S(1)}, bf16[320,96]{1,0:T(8,128)(2,1)S(1)}, u32[]{:S(2)}, u32[]{:S(2)}) collective-permute-start(bf16[320,96]{1,0:T(8,128)(2,1)S(1)} %pad_maximum_fusion), channel_id=1, source_target_pairs={{0,8},{2,10},{4,12},{6,14},{8,0},{10,2},{12,4},{14,6},{16,24},{18,... | collective-permute-start | bytes 184328 | tf_op jit(solution)/shard_map/ppermute | solution.py:24
  29.9 10.8 %collective-permute-start.3 = (bf16[640,96]{1,0:T(8,128)(2,1)S(1)}, bf16[640,96]{1,0:T(8,128)(2,1)S(1)}, u32[]{:S(2)}, u32[]{:S(2)}) collective-permute-start(bf16[640,96]{1,0:T(8,128)(2,1)S(1)} %join.1), channel_id=1, source_target_pairs={{0,4},{2,6},{4,0},{6,2},{8,12},{10,14},{12,8},{14,10},{16,20},{18,... | collective-permute-start | bytes 368648 | tf_op jit(solution)/shard_map/ppermute | solution.py:24
  34.6 10.2 %collective-permute-start.7 = (f32[9,8,128]{2,1,0:T(8,128)S(1)}, f32[9,8,128]{2,1,0:T(8,128)S(1)}, u32[]{:S(2)}, u32[]{:S(2)}) collective-permute-start(f32[9,8,128]{2,1,0:T(8,128)S(1)} %get-tuple-element.27.refs_2_), channel_id=1, source_target_pairs={{0,1},{1,0},{2,3},{3,2},{4,5},{5,4},{6,7},{7,6},{8,9},{9,8},{10,11... | collective-permute-start | bytes 110600 | tf_op jit(solution)/shard_map/ppermute | solution.py:24
  38.4 6.4 %collective-permute-start.8 = (f32[9,8,128]{2,1,0:T(8,128)S(1)}, f32[9,8,128]{2,1,0:T(8,128)S(1)}, u32[]{:S(2)}, u32[]{:S(2)}) collective-permute-start(f32[9,8,128]{2,1,0:T(8,128)S(1)} %get-tuple-element.28.refs_4_), channel_id=1, source_target_pairs={{0,1},{1,0},{2,3},{3,2},{4,5},{5,4},{6,7},{7,6},{8,9},{9,8},{10,11... | collective-permute-start | bytes 110600 | tf_op jit(solution)/shard_map/ppermute | solution.py:24
  41.8 1.2 %collective-permute-start.6 = (f32[2,4,128]{2,1,0:T(4,128)S(1)}, f32[2,4,128]{2,1,0:T(4,128)S(1)}, u32[]{:S(2)}, u32[]{:S(2)}) collective-permute-start(f32[2,4,128]{2,1,0:T(4,128)S(1)} %get-tuple-element.26.refs_0_), channel_id=1, source_target_pairs={{0,1},{1,0},{2,3},{3,2},{4,5},{5,4},{6,7},{7,6},{8,9},{9,8},{10,11... | collective-permute-start | bytes 12296 | tf_op jit(solution)/shard_map/ppermute | solution.py:24

commit v5 on v4

--- a/solution.py
+++ b/solution.py
@@ -3,6 +3,7 @@
 
 import jax
 import jax.numpy as jnp
+import numpy as np
 from jax import lax
 from jax.experimental import pallas as pl
 from jax.experimental.pallas import tpu as pltpu
@@ -51,9 +52,9 @@
         at += part.shape[0]
 
 
-def pack_kernel(band, spectra, low, high, buffer, sems):
+def pack_kernel(band, lev, spectra, low, high, buffer, sems):
     freqs, half = low.shape[:2]
-    odd = band[0] % 2
+    odd = band[0] & 1
     chunks = buffer.shape[1]
     span = freqs // chunks
     reads, writes = [], []
@@ -75,33 +76,36 @@
         copy.wait()
 
 
-def advect_kernel(directions, lev, up, courant, rate, breaking, spectra, halo, land, *refs):
+def shift_matrix():
+    table = np.zeros((STEPS * 128, 256), np.float32)
+    x = np.arange(128)
+    for i in range(STEPS):
+        table[128 * i + (x - i - 1) % 128, x] = 1.0
+        table[128 * i + (x + i + 1) % 128, 128 + x] = 1.0
+    return jnp.asarray(table, jnp.bfloat16)
+
+
+def advect_kernel(
+    directions, flip, lev, band, courant, rate, breaking, spectra, halo, land, shift_table, *refs
+):
     whole = spectra.shape[1] > halo.shape[1]
     if whole:
         damped, source, other, own, terms, moved, kept, shifts, sems = refs
     else:
-        damped, source, terms, moved, kept, shifts = refs
+        damped, source, terms, moved, kept, shifts, sems = refs
         own = spectra
+    up = (band[0] & 1) ^ flip
     freqs = courant.shape[0]
     half = directions // 4
     tiles = -(-half // 2)
     theta = angles_of(directions)
+    shift_copy = pltpu.make_async_copy(shift_table, shifts, sems.at[0])
+    shift_copy.start()
     if whole:
         copies = []
-        for k, (first, dst) in enumerate((((1 - up[0]) * half, own), (up[0] * half, other))):
-            copies.append(pltpu.make_async_copy(spectra.at[:, pl.ds(first, half)], dst, sems.at[k]))
+        for k, (first, dst) in enumerate((((1 - up) * half, own), (up * half, other))):
+            copies.append(pltpu.make_async_copy(spectra.at[:, pl.ds(first, half)], dst, sems.at[1 + k]))
             copies[-1].start()
-
-    sign = 2 * up[0] - 1
-    row = lax.broadcasted_iota(jnp.int32, (128, 128), 0)
-    column = lax.broadcasted_iota(jnp.int32, (128, 128), 1)
-    for i in range(STEPS):
-        for k in range(2):
-            move = (1 - 2 * k) * sign * (i + 1)
-            hit = (row - column + move + 256) % 128 == 0
-            shifts[128 * i : 128 * i + 128, 128 * k : 128 * k + 128] = hit.astype(
-                jnp.float32
-            ).astype(jnp.bfloat16)
 
     row = lax.broadcasted_iota(jnp.int32, (8, 128), 0)
     row_low = row < 4
@@ -153,20 +157,23 @@
                 ]
             )
             if j % 2 or j == half - 1:
-                first = held[-2] if j % 2 else held[-1]
+                lower = held[-2] if j % 2 else held[-1]
                 at = pl.ds(pl.multiple_of(f * (16 * tiles) + 16 * (j // 2), 16), 16)
                 for i in range(STEPS):
-                    tile = jnp.concatenate([first[i], held[-1][i]], axis=0)
+                    tile = jnp.concatenate([lower[i], held[-1][i]], axis=0)
                     terms[at, 128 * i : 128 * i + 128] = tile.astype(jnp.bfloat16)
         return carry
 
     for rising in (True, False):
 
-        @pl.when(up[0] == int(rising))
+        @pl.when(up == int(rising))
         def _(rising=rising):
             lax.fori_loop(0, freqs, functools.partial(powers, rising=rising), 0)
 
+    shift_copy.wait()
     moved[...] = dot(terms[...], shifts[...])
+
+    first = pl.multiple_of((1 - up) * 128, 128)
 
     def finish(f, carry):
         damp = breaking[f]
@@ -174,10 +181,8 @@
         for j in range(half):
             at = pl.ds(pl.multiple_of(f * (16 * tiles) + 8 * j, 8), 8)
             east = [math.cos(theta[2 * j + k]) > 0 for k in range(2)]
-            if east[0] == east[1]:
-                shifted = moved[at, 0:128] if east[0] else moved[at, 128:256]
-            else:
-                shifted = halves(row_low, moved[at, 0:128], moved[at, 128:256])
+            sides = [moved[at, pl.ds(first if way else 128 - first, 128)] for way in east]
+            shifted = sides[0] if east[0] == east[1] else halves(row_low, *sides)
             state = kept[f, j] + shifted
             damped[f, j] = mask * state / (1.0 + damp * state)
             source[j] = source[j] + gain * state
@@ -313,20 +318,17 @@
     return pushes, east4, north4
 
 
-def sign_of(up):
-    return (2 * up - 1).astype(jnp.float32)
-
-
-def result_kernel(directions, parts, up, rate, near, far, *refs):
+def result_kernel(directions, parts, band, rate, near, far, *refs):
     winds = refs[:parts]
     result, stage, sems = refs[-3:]
     half = directions // 4
     chunks = sems.shape[0]
     span = rate.shape[0] // chunks
-    sign = sign_of(up[0])
+    up = band[0] & 1
+    sign = (2 * up - 1).astype(jnp.float32)
     sides = [
-        (near, (1 - up[0]) * half, pushes_of(directions, winds, sign)[0]),
-        (far, up[0] * half, pushes_of(directions, winds, -sign)[0]),
+        (near, (1 - up) * half, pushes_of(directions, winds, sign)[0]),
+        (far, up * half, pushes_of(directions, winds, -sign)[0]),
     ]
     copies = []
     for chunk in range(chunks):
@@ -342,11 +344,12 @@
         copy.wait()
 
 
-def charnock_kernel(directions, parts, up, land, *refs):
+def charnock_kernel(directions, parts, band, land, *refs):
     winds, first, second, charnock = (
         refs[:parts], refs[parts : 2 * parts], refs[2 * parts : 3 * parts], refs[3 * parts],
     )
-    sign = sign_of(up[0])
+    up = band[0] & 1
+    sign = (2 * up - 1).astype(jnp.float32)
     stress = jnp.zeros((8, 128), jnp.float32)
     for sources, way in ((first, sign), (second, -sign)):
         pushes, east, north = pushes_of(directions, winds, way)
@@ -390,7 +393,7 @@
     low, high = pl.pallas_call(
         pack_kernel,
         out_shape=[half_shape] * 2,
-        in_specs=[SMEM, hbm],
+        in_specs=[SMEM, SMEM, hbm],
         out_specs=[hbm] * 2,
         scratch_shapes=[
             pltpu.VMEM((2, chunks, freqs // chunks, half, tile_rows, tile_cols), jnp.bfloat16),
@@ -398,7 +401,7 @@
         ],
         compiler_params=params(4),
         name="pack",
-    )(band.reshape(1), in_hbm(spectra))
+    )(band.reshape(1), lev.reshape(1), in_hbm(spectra))
     low = lax.ppermute(low, "band", [(i, i ^ 1) for i in range(bands)])
     across = [(i, i + 1) for i in range(1, bands - 1, 2)]
     high = lax.ppermute(high, "band", across + [(j, i) for i, j in across])
@@ -433,7 +436,7 @@
             order = order + [q ^ (1 << bit) for q in order]
 
     def flipped(bit):
-        return (waves << bit) * (1 - 2 * (jnp.right_shift(band, bit) % 2))
+        return (waves << bit) * (1 - 2 * (jnp.right_shift(band, bit) & 1))
 
     count = len(parts) - 1
     total_rows = bands * waves // 4
@@ -486,32 +489,33 @@
     grid = jnp.transpose(grid, (1, 0, 2)).reshape(share, 1, FIELDS, LON_W)
 
     quarter = pairs // 2
-    odd = band % 2
-    levels = lev.reshape(1)
+    levels, here = lev.reshape(1), band.reshape(1)
     own = in_hbm(spectra.reshape(freqs, pairs, 8, 128))
     half_state = pltpu.VMEM((freqs, quarter, 8, 128), jnp.float32)
 
-    def advected(spectra_of, halo, up):
+    shifts = in_hbm(shift_matrix())
+
+    def advected(spectra_of, halo, flip):
         whole = spectra_of.shape[1] == pairs
         part = pltpu.VMEM((freqs, quarter, 8, 128), jnp.bfloat16)
         tall = 16 * -(-quarter // 2) * freqs
         return pl.pallas_call(
-            functools.partial(advect_kernel, directions),
+            functools.partial(advect_kernel, directions, flip),
             out_shape=[half_state, pltpu.VMEM((quarter, 8, 128), jnp.float32)] + [part] * whole,
-            in_specs=[SMEM] * 5 + [hbm if whole else VMEM, VMEM, VMEM],
+            in_specs=[SMEM] * 5 + [hbm if whole else VMEM] + [VMEM] * 2 + [hbm],
             out_specs=[VMEM] * (2 + whole),
             scratch_shapes=[part] * whole
             + [
                 pltpu.VMEM((tall, STEPS * 128), jnp.bfloat16),
                 pltpu.VMEM((tall, 256), jnp.float32),
                 pltpu.VMEM((freqs, quarter, 8, 128), jnp.float32),
-                pltpu.VMEM((STEPS * 128, 256), jnp.bfloat16),
-            ]
-            + [pltpu.SemaphoreType.DMA((2,))] * whole,
+                pltpu.VMEM(shifts.shape, shifts.dtype),
+                pltpu.SemaphoreType.DMA((3,)),
+            ],
             compiler_params=params(12),
         )(
-            levels, up, courant, growth_rate, breaking, spectra_of,
-            in_vmem(halo.reshape(freqs, quarter, 8, 128)), land_sea,
+            levels, here, courant, growth_rate, breaking, spectra_of,
+            in_vmem(halo.reshape(freqs, quarter, 8, 128)), land_sea, shifts,
         )
 
     def over_lev(value):
@@ -522,11 +526,10 @@
             bit += 1
         return parts
 
-    near_up, far_up = odd.reshape(1), (1 - odd).reshape(1)
     winds = over_lev(wind)
-    near_damped, source, own = advected(own, low, near_up)
+    near_damped, source, own = advected(own, low, 0)
     near_sources = over_lev(source)
-    far_damped, source = advected(own, high, far_up)
+    far_damped, source = advected(own, high, 1)
     far_sources = over_lev(source)
     result = pl.pallas_call(
         functools.partial(result_kernel, directions, levs),
@@ -539,7 +542,7 @@
         ],
         compiler_params=params(6),
         name="result",
-    )(near_up, growth_rate, near_damped, far_damped, *winds)
+    )(here, growth_rate, near_damped, far_damped, *winds)
     charnock = pl.pallas_call(
         functools.partial(charnock_kernel, directions, levs),
         out_shape=jax.ShapeDtypeStruct((tile_rows, tile_cols), jnp.float32),
@@ -547,7 +550,7 @@
         out_specs=VMEM,
         compiler_params=params(2),
         name="charnock",
-    )(near_up, land_sea, *winds, *near_sources, *far_sources)
+    )(here, land_sea, *winds, *near_sources, *far_sources)
     return grid, result.reshape(freqs, directions, tile_rows, tile_cols), charnock
 
 

time: 45.7 us -> 45.5 us (level)
  no operation moved by 1% of the time
where the time goes in v5:
time: 45.5 us; the launch traced here: 45.2 us
  Pallas kernels  14.3 us (31%)
  starting transfers between devices  13.3 us (29%)
  waiting for transfers between devices  10.7 us (24%)
  local copies, waits for them, and re-layouts  3.79 us (8%)
  between operations  1.49 us (3%)
  matrix products  1.17 us (3%)
  other arithmetic  0.47 us (1%)
    ppermute x7, starting transfers between devices, swapped(): lax.ppermute(block, axis, [(i, i ^ 1 << apart) for i in range(count)])  11.8 us
    ppermute x7, waiting for transfers between devices, swapped(): lax.ppermute(block, axis, [(i, i ^ 1 << apart) for i in range(count)])  10.7 us
    pallas_call x2, Pallas kernels, advected(): pl.pallas_call(functools.partial(advect_kernel, directions, flip), out_sh...  8.31 us
    unnamed x15, local copies, waits for them, and re-layouts  2.3 us
    pallas_call x1, Pallas kernels, on_device_(): pl.pallas_call(pack_kernel, out_shape=[half_shape] * 2, in_specs=[SMEM, S...  1.91 us
    pallas_call x1, Pallas kernels, on_device_(): pl.pallas_call(functools.partial(result_kernel, directions, levs), out_sh...  1.68 us
    ppermute x1, starting transfers between devices, on_device_(): high = lax.ppermute(high, 'band', across + [(j, i) for i, j in across])  1.4 us
    dot_general x1, matrix products, on_device_(): lax.dot_general(stacked, legendre, (((2,), (2,)), ((0,), (0,))), preferre...  1.17 us
  transfers between devices with their start and end apart: 9, of which 3 were waited for; matrix products, arithmetic and copies ran while one was open for 4% of the time, Pallas kernels for 30%

profile of v5, /device:TPU:0, one launch (start us, length us, event | category | flops | bytes accessed | tf_op | source)
XLA Modules:
  0.0 45.2 jit_solution(6374207590585305836)
XLA Ops:
  0.6 0.0 copy-start
  0.7 1.6 %copy.15 = bf16[80,2,1,3,1280]{4,0,3,1,2:T(8,128)(2,1)S(1)} copy(bf16[80,2,1,3,1280]{4,1,3,2,0:T(2,128)(2,1)} %param.11) | data formatting | bytes 2457600 | tf_op args[0]
  2.2 0.7 %copy-done = bf16[80,16,1280]{2,1,0:T(8,128)(2,1)S(1)} copy-done((bf16[80,16,1280]{2,1,0:T(8,128)(2,1)S(1)}, bf16[80,16,1280]{2,1,0:T(8,128)(2,1)}, u32[]{:S(2)}) %copy-start) | copy-done | bytes 3276824
  2.9 0.0 copy-start.5
  3.0 1.2 %fusion.2 = bf16[80,6,16]{2,1,0:T(8,128)(2,1)S(1)} fusion(bf16[80,16,1280]{2,1,0:T(8,128)(2,1)S(1)} %copy-done, bf16[80,6,1280]{2,0,1:T(8,128)(2,1)S(1)} %bitcast.15), kind=kOutput, calls=%fused_computation.2 | convolution fusion | flops 19668480 | bytes 4520960 | tf_op jit(solution)/shard_map/dot_general | solution.py:410
  4.1 0.1 copy.17
  4.3 0.1 copy.18
  4.4 0.1 broadcast_multiply_fusion.refs_0_
  4.4 3.0 %collective-permute-start = (bf16[80,96]{1,0:T(8,128)(2,1)S(1)}, bf16[80,96]{1,0:T(8,128)(2,1)S(1)}, u32[]{:S(2)}, u32[]{:S(2)}) collective-permute-start(bf16[80,96]{1,0:T(8,128)(2,1)S(1)} %broadcast_multiply_fusion.refs_0_), channel_id=1, source_target_pairs={{0,2},{2,0},{4,6},{6,4},{8,10},{10,8},{12,14},{14,12},{16,18},{18,... | collective-permute-start | bytes 46088 | tf_op jit(solution)/shard_map/ppermute | solution.py:25
  7.4 1.9 %pack.1 = (bf16[18,18,4,128]{3,2,1,0:T(4,128)(2,1)}, bf16[18,18,4,128]{3,2,1,0:T(4,128)(2,1)}) custom-call(s32[1]{0:T(128)} %bitcast.band, s32[1]{0:T(128)} %bitcast.8.lev, bf16[18,36,4,128]{3,2,1,0:T(4,128)(2,1)} %spectra.1), custom_call_target="tpu_custom_call" | custom-call | tf_op jit(solution)/shard_map/pack/pallas_call | solution.py:393
  9.4 0.0 copy-start.2
  9.4 0.1 collective-permute-start.4
  9.5 1.4 %collective-permute-start.5 = (bf16[18,18,4,128]{3,2,1,0:T(4,128)(2,1)}, bf16[18,18,4,128]{3,2,1,0:T(4,128)(2,1)}, u32[]{:S(2)}, u32[]{:S(2)}) collective-permute-start(bf16[18,18,4,128]{3,2,1,0:T(4,128)(2,1)} %get-tuple-element.24), channel_id=1, source_target_pairs={{2,4},{6,8},{10,12},{14,16},{18,20},{22,24},{26,28},{4,2},{8,6},{1... | collective-permute-start | bytes 995336 | tf_op jit(solution)/shard_map/ppermute | solution.py:407
  10.9 6.0 %collective-permute-start.1 = (bf16[160,96]{1,0:T(8,128)(2,1)S(1)}, bf16[160,96]{1,0:T(8,128)(2,1)S(1)}, u32[]{:S(2)}, u32[]{:S(2)}) collective-permute-start(bf16[160,96]{1,0:T(8,128)(2,1)S(1)} %pad_maximum_fusion.1), channel_id=1, source_target_pairs={{0,16},{2,18},{4,20},{6,22},{8,24},{10,26},{12,28},{14,30},{16,0},... | collective-permute-start | bytes 92168 | tf_op jit(solution)/shard_map/ppermute | solution.py:25
  16.9 8.4 %collective-permute-done.1.refs_2_ = bf16[160,96]{1,0:T(8,128)(2,1)S(1)} collective-permute-done((bf16[160,96]{1,0:T(8,128)(2,1)S(1)}, bf16[160,96]{1,0:T(8,128)(2,1)S(1)}, u32[]{:S(2)}, u32[]{:S(2)}) %collective-permute-start.1) | collective-permute-done | bytes 30752 | tf_op jit(solution)/shard_map/ppermute | solution.py:25
  25.3 2.1 %collective-permute-start.2 = (bf16[320,96]{1,0:T(8,128)(2,1)S(1)}, bf16[320,96]{1,0:T(8,128)(2,1)S(1)}, u32[]{:S(2)}, u32[]{:S(2)}) collective-permute-start(bf16[320,96]{1,0:T(8,128)(2,1)S(1)} %pad_maximum_fusion), channel_id=1, source_target_pairs={{0,8},{2,10},{4,12},{6,14},{8,0},{10,2},{12,4},{14,6},{16,24},{18,... | collective-permute-start | bytes 184328 | tf_op jit(solution)/shard_map/ppermute | solution.py:25
  27.4 0.5 %iota.16 = s32[8]{0:T(128)} iota(), iota_dimension=0 | iota | bytes 32 | tf_op jit(solution)/shard_map/iota | solution.py:455
  27.9 0.7 %concatenate.9 = s32[25]{0:T(128)S(1)} concatenate(s32[4]{0:T(128)S(1)} %xor_multiply_fusion, s32[10]{0:T(128)S(1)} %iota_multiply_fusion, s32[8]{0:T(128)} %iota.16, s32[1]{0:T(128)} %bitcast.1, s32[1]{0:T(128)} %bitcast.2, s32[1]{0:T(128)} %bitcast.3), dimensions={0} | concatenate | bytes 200 | tf_op jit(solution)/shard_map/concatenate | solution.py:457
  28.6 1.2 %collective-permute-done.2.refs_3_ = bf16[320,96]{1,0:T(8,128)(2,1)S(1)} collective-permute-done((bf16[320,96]{1,0:T(8,128)(2,1)S(1)}, bf16[320,96]{1,0:T(8,128)(2,1)S(1)}, u32[]{:S(2)}, u32[]{:S(2)}) %collective-permute-start.2) | collective-permute-done | bytes 61472 | tf_op jit(solution)/shard_map/ppermute | solution.py:25
  29.9 0.1 collective-permute-start.3
  29.9 0.0 collective-permute-done.4
  30.0 4.7 %shard_map.130 = (f32[18,9,8,128]{3,2,1,0:T(8,128)S(1)}, f32[9,8,128]{2,1,0:T(8,128)S(1)}, bf16[18,9,8,128]{3,2,1,0:T(8,128)(2,1)S(1)}) custom-call(s32[1]{0:T(128)} %bitcast.8.lev, s32[1]{0:T(128)} %bitcast.band, f32[18]{0:T(128)S(1)} %copy-done.4, f32[18]{0:T(128)S(1)} %copy-done.3, f32[18]{0:T(128)S(1)} %copy-done.5, bf16[18,18,8,128]{3,2,1,0:T(8,128)(2,1)} %bitcast.16, ...), custom_call_target="tpu_custom_call" | custom-call | tf_op jit(solution)/shard_map/pallas_call | solution.py:502
  34.7 3.6 %shard_map.131 = (f32[18,9,8,128]{3,2,1,0:T(8,128)S(1)}, f32[9,8,128]{2,1,0:T(8,128)S(1)}) custom-call(s32[1]{0:T(128)} %bitcast.8.lev, s32[1]{0:T(128)} %bitcast.band, f32[18]{0:T(128)S(1)} %copy-done.4, f32[18]{0:T(128)S(1)} %copy-done.3, f32[18]{0:T(128)S(1)} %copy-done.5, bf16[18,9,8,128]{3,2,1,0:T(8,128)(2,1)S(1)} %get-tuple-element.23.spectra, ...), custom_call_target="tpu_custom_call" | custom-call | tf_op jit(solution)/shard_map/pallas_call | solution.py:502
  38.3 0.1 collective-permute-start.8
  38.4 0.5 %collective-permute-start.7 = (f32[9,8,128]{2,1,0:T(8,128)S(1)}, f32[9,8,128]{2,1,0:T(8,128)S(1)}, u32[]{:S(2)}, u32[]{:S(2)}) collective-permute-start(f32[9,8,128]{2,1,0:T(8,128)S(1)} %get-tuple-element.27.refs_2_), channel_id=1, source_target_pairs={{0,1},{1,0},{2,3},{3,2},{4,5},{5,4},{6,7},{7,6},{8,9},{9,8},{10,11... | collective-permute-start | bytes 110600 | tf_op jit(solution)/shard_map/ppermute | solution.py:25
  38.9 0.3 fusion.9
  39.9 0.7 %first.1 = (f32[48,512]{1,0:T(8,128)S(1)}, bf16[320,512]{1,0:T(8,128)(2,1)S(1)}, bf16[320,512]{1,0:T(8,128)(2,1)S(1)}, bf16[128,512]{1,0:T(8,128)(2,1)S(1)}) custom-call(f32[25,512]{1,0:T(8,128)S(1)} %get-tuple-element.36.cosines, f32[25,512]{1,0:T(8,128)S(1)} %get-tuple-element.35.sines, s32[4,128]{1,0:T(4,128)S(1)} %copy-done.2, ...), custom_call_target="tpu_custom_call" | custom-call | tf_op jit(solution)/shard_map/first/pallas_call | solution.py:464
  40.6 1.1 %fourier.1 = (f32[3,1,512]{2,1,0:T(1,128)}, f32[2,4,128]{2,1,0:T(4,128)S(1)}) custom-call(s32[1]{0:T(128)} %bitcast.band, f32[1]{0:T(128)S(6)} %copy.24.level, f32[48,512]{1,0:T(8,128)S(1)} %get-tuple-element.16.early, bf16[640,96]{1,0:T(8,128)(2,1)S(1)} %collective-permute-done.3.last, f32[25,512]{1,0:T(8,128)S(1)} %get-tuple-element.36.cosines, ...), custom_call_target="tpu_custom_call" | custom-call | tf_op jit(solution)/shard_map/fourier/pallas_call | solution.py:475
  41.7 0.1 collective-permute-start.6
  41.8 1.1 %collective-permute-done.6.refs_1_ = f32[2,4,128]{2,1,0:T(4,128)S(1)} collective-permute-done((f32[2,4,128]{2,1,0:T(4,128)S(1)}, f32[2,4,128]{2,1,0:T(4,128)S(1)}, u32[]{:S(2)}, u32[]{:S(2)}) %collective-permute-start.6) | collective-permute-done | bytes 4128 | tf_op jit(solution)/shard_map/ppermute | solution.py:25
  42.9 1.7 %result.1 = f32[18,18,8,128]{3,2,1,0:T(8,128)} custom-call(s32[1]{0:T(128)} %bitcast.band, f32[18]{0:T(128)S(1)} %copy-done.3, f32[18,9,8,128]{3,2,1,0:T(8,128)S(1)} %get-tuple-element.22.near, f32[18,9,8,128]{3,2,1,0:T(8,128)S(1)} %get-tuple-element.25.far, f32[2,4,128]{2,1,0:T(4,128)S(1)} %get-tuple-element.26.refs_0_, ...), custom_call_target="tpu_custom_call" | custom-call | tf_op jit(solution)/shard_map/result/pallas_call | solution.py:534
  44.6 0.6 %charnock.1 = f32[4,128]{1,0:T(4,128)} custom-call(s32[1]{0:T(128)} %bitcast.band, s32[4,128]{1,0:T(4,128)S(1)} %copy-done.1, f32[2,4,128]{2,1,0:T(4,128)S(1)} %get-tuple-element.26.refs_0_, f32[2,4,128]{2,1,0:T(4,128)S(1)} %collective-permute-done.6.refs_1_, f32[9,8,128]{2,1,0:T(8,128)S(1)} %get-tuple-element.27.refs_2_, ...), custom_call_target="tpu_custom_call" | custom-call | tf_op jit(solution)/shard_map/charnock/pallas_call | solution.py:546
  (21 shorter events, 0.1 us)
Async XLA Ops:
  0.6 2.3 %copy-start = (bf16[80,16,1280]{2,1,0:T(8,128)(2,1)S(1)}, bf16[80,16,1280]{2,1,0:T(8,128)(2,1)}, u32[]{:S(2)}) copy-start(bf16[80,16,1280]{2,1,0:T(8,128)(2,1)} %param.12) | copy-start | bytes 9830404
  2.9 14.0 %copy-start.6 = (s32[4]{0:T(128)S(1)}, s32[4]{0:T(128)}, u32[]{:S(2)}) copy-start(s32[4]{0:T(128)} %constant.44.clone) | copy-start | bytes 52
  2.9 27.0 %copy-start.1 = (s32[4,128]{1,0:T(4,128)S(1)}, s32[4,128]{1,0:T(4,128)}, u32[]{:S(2)}) copy-start(s32[4,128]{1,0:T(4,128)} %land.5) | copy-start | bytes 6148
  2.9 27.0 %copy-start.3 = (f32[18]{0:T(128)S(1)}, f32[18]{0:T(128)}, u32[]{:S(2)}) copy-start(f32[18]{0:T(128)} %rate.5) | copy-start | bytes 220
  2.9 27.0 %copy-start.4 = (f32[18]{0:T(128)S(1)}, f32[18]{0:T(128)}, u32[]{:S(2)}) copy-start(f32[18]{0:T(128)} %courant.3) | copy-start | bytes 220
  2.9 27.0 %copy-start.5 = (f32[18]{0:T(128)S(1)}, f32[18]{0:T(128)}, u32[]{:S(2)}) copy-start(f32[18]{0:T(128)} %breaking.3) | copy-start | bytes 220
  4.4 6.4 %collective-permute-start = (bf16[80,96]{1,0:T(8,128)(2,1)S(1)}, bf16[80,96]{1,0:T(8,128)(2,1)S(1)}, u32[]{:S(2)}, u32[]{:S(2)}) collective-permute-start(bf16[80,96]{1,0:T(8,128)(2,1)S(1)} %broadcast_multiply_fusion.refs_0_), channel_id=1, source_target_pairs={{0,2},{2,0},{4,6},{6,4},{8,10},{10,8},{12,14},{14,12},{16,18},{18,... | collective-permute-start | bytes 46088 | tf_op jit(solution)/shard_map/ppermute | solution.py:25
  9.4 30.5 %copy-start.2 = (s32[4,128]{1,0:T(4,128)S(1)}, s32[4,128]{1,0:T(4,128)}, u32[]{:S(2)}) copy-start(s32[4,128]{1,0:T(4,128)} %coupling.3) | copy-start | bytes 6148
  9.4 20.6 %collective-permute-start.4 = (bf16[18,18,4,128]{3,2,1,0:T(4,128)(2,1)}, bf16[18,18,4,128]{3,2,1,0:T(4,128)(2,1)}, u32[]{:S(2)}, u32[]{:S(2)}) collective-permute-start(bf16[18,18,4,128]{3,2,1,0:T(4,128)(2,1)} %get-tuple-element.21), channel_id=1, source_target_pairs={{0,2},{2,0},{4,6},{6,4},{8,10},{10,8},{12,14},{14,12},{16,18},{18,... | collective-permute-start | bytes 995336 | tf_op jit(solution)/shard_map/ppermute | solution.py:405
  9.5 25.3 %collective-permute-start.5 = (bf16[18,18,4,128]{3,2,1,0:T(4,128)(2,1)}, bf16[18,18,4,128]{3,2,1,0:T(4,128)(2,1)}, u32[]{:S(2)}, u32[]{:S(2)}) collective-permute-start(bf16[18,18,4,128]{3,2,1,0:T(4,128)(2,1)} %get-tuple-element.24), channel_id=1, source_target_pairs={{2,4},{6,8},{10,12},{14,16},{18,20},{22,24},{26,28},{4,2},{8,6},{1... | collective-permute-start | bytes 995336 | tf_op jit(solution)/shard_map/ppermute | solution.py:407
  10.9 14.4 %collective-permute-start.1 = (bf16[160,96]{1,0:T(8,128)(2,1)S(1)}, bf16[160,96]{1,0:T(8,128)(2,1)S(1)}, u32[]{:S(2)}, u32[]{:S(2)}) collective-permute-start(bf16[160,96]{1,0:T(8,128)(2,1)S(1)} %pad_maximum_fusion.1), channel_id=1, source_target_pairs={{0,16},{2,18},{4,20},{6,22},{8,24},{10,26},{12,28},{14,30},{16,0},... | collective-permute-start | bytes 92168 | tf_op jit(solution)/shard_map/ppermute | solution.py:25
  25.3 4.5 %collective-permute-start.2 = (bf16[320,96]{1,0:T(8,128)(2,1)S(1)}, bf16[320,96]{1,0:T(8,128)(2,1)S(1)}, u32[]{:S(2)}, u32[]{:S(2)}) collective-permute-start(bf16[320,96]{1,0:T(8,128)(2,1)S(1)} %pad_maximum_fusion), channel_id=1, source_target_pairs={{0,8},{2,10},{4,12},{6,14},{8,0},{10,2},{12,4},{14,6},{16,24},{18,... | collective-permute-start | bytes 184328 | tf_op jit(solution)/shard_map/ppermute | solution.py:25
  29.9 10.8 %collective-permute-start.3 = (bf16[640,96]{1,0:T(8,128)(2,1)S(1)}, bf16[640,96]{1,0:T(8,128)(2,1)S(1)}, u32[]{:S(2)}, u32[]{:S(2)}) collective-permute-start(bf16[640,96]{1,0:T(8,128)(2,1)S(1)} %join.1), channel_id=1, source_target_pairs={{0,4},{2,6},{4,0},{6,2},{8,12},{10,14},{12,8},{14,10},{16,20},{18,... | collective-permute-start | bytes 368648 | tf_op jit(solution)/shard_map/ppermute | solution.py:25
  38.3 6.3 %collective-permute-start.8 = (f32[9,8,128]{2,1,0:T(8,128)S(1)}, f32[9,8,128]{2,1,0:T(8,128)S(1)}, u32[]{:S(2)}, u32[]{:S(2)}) collective-permute-start(f32[9,8,128]{2,1,0:T(8,128)S(1)} %get-tuple-element.28.refs_4_), channel_id=1, source_target_pairs={{0,1},{1,0},{2,3},{3,2},{4,5},{5,4},{6,7},{7,6},{8,9},{9,8},{10,11... | collective-permute-start | bytes 110600 | tf_op jit(solution)/shard_map/ppermute | solution.py:25
  38.4 6.2 %collective-permute-start.7 = (f32[9,8,128]{2,1,0:T(8,128)S(1)}, f32[9,8,128]{2,1,0:T(8,128)S(1)}, u32[]{:S(2)}, u32[]{:S(2)}) collective-permute-start(f32[9,8,128]{2,1,0:T(8,128)S(1)} %get-tuple-element.27.refs_2_), channel_id=1, source_target_pairs={{0,1},{1,0},{2,3},{3,2},{4,5},{5,4},{6,7},{7,6},{8,9},{9,8},{10,11... | collective-permute-start | bytes 110600 | tf_op jit(solution)/shard_map/ppermute | solution.py:25
  41.7 1.2 %collective-permute-start.6 = (f32[2,4,128]{2,1,0:T(4,128)S(1)}, f32[2,4,128]{2,1,0:T(4,128)S(1)}, u32[]{:S(2)}, u32[]{:S(2)}) collective-permute-start(f32[2,4,128]{2,1,0:T(4,128)S(1)} %get-tuple-element.26.refs_0_), channel_id=1, source_target_pairs={{0,1},{1,0},{2,3},{3,2},{4,5},{5,4},{6,7},{7,6},{8,9},{9,8},{10,11... | collective-permute-start | bytes 12296 | tf_op jit(solution)/shard_map/ppermute | solution.py:25

commit v6 on v5

--- a/solution.py
+++ b/solution.py
@@ -45,28 +45,20 @@
     return pltpu.CompilerParams(vmem_limit_bytes=mib * 2**20)
 
 
-def join_kernel(*refs):
-    at = 0
-    for part in refs[:-1]:
-        refs[-1][at : at + part.shape[0], :] = part[...]
-        at += part.shape[0]
-
-
 def pack_kernel(band, lev, spectra, low, high, buffer, sems):
     freqs, half = low.shape[:2]
     odd = band[0] & 1
-    chunks = buffer.shape[1]
+    chunks = sems.shape[2]
     span = freqs // chunks
     reads, writes = [], []
     for k, out in enumerate((low, high)):
+        held = buffer.at[k]
         first = (odd if k == 0 else 1 - odd) * half
         for c in range(chunks):
             rows = pl.ds(c * span, span)
-            held = buffer.at[k, c]
-            reads.append(
-                pltpu.make_async_copy(spectra.at[rows, pl.ds(first, half)], held, sems.at[0, k, c])
-            )
-            writes.append(pltpu.make_async_copy(held, out.at[rows], sems.at[1, k, c]))
+            inside = spectra.at[rows, pl.ds(first, half)]
+            reads.append(pltpu.make_async_copy(inside, held.at[rows], sems.at[0, k, c]))
+            writes.append(pltpu.make_async_copy(held.at[rows], out.at[rows], sems.at[1, k, c]))
     for copy in reads:
         copy.start()
     for read, write in zip(reads, writes):
@@ -86,14 +78,9 @@
 
 
 def advect_kernel(
-    directions, flip, lev, band, courant, rate, breaking, spectra, halo, land, shift_table, *refs
+    directions, flip, lev, band, courant, rate, breaking, own, halo, land, shift_table,
+    damped, source, terms, moved, kept, shifts, sems,
 ):
-    whole = spectra.shape[1] > halo.shape[1]
-    if whole:
-        damped, source, other, own, terms, moved, kept, shifts, sems = refs
-    else:
-        damped, source, terms, moved, kept, shifts, sems = refs
-        own = spectra
     up = (band[0] & 1) ^ flip
     freqs = courant.shape[0]
     half = directions // 4
@@ -101,21 +88,12 @@
     theta = angles_of(directions)
     shift_copy = pltpu.make_async_copy(shift_table, shifts, sems.at[0])
     shift_copy.start()
-    if whole:
-        copies = []
-        for k, (first, dst) in enumerate((((1 - up) * half, own), (up * half, other))):
-            copies.append(pltpu.make_async_copy(spectra.at[:, pl.ds(first, half)], dst, sems.at[1 + k]))
-            copies[-1].start()
-
     row = lax.broadcasted_iota(jnp.int32, (8, 128), 0)
     row_low = row < 4
     inner_row = row % 4
     land4 = land[...].astype(jnp.float32)
     mask = jnp.concatenate([land4, land4], axis=0)
     source[...] = jnp.zeros_like(source)
-    if whole:
-        for copy in copies:
-            copy.wait()
 
     def powers(f, carry, rising):
         speed = courant[f]
@@ -191,7 +169,7 @@
     lax.fori_loop(0, freqs, finish, 0)
 
 
-def build_basis(cosines, sines, cos_table, sin_table, wave_cos, wave_sin):
+def basis_kernel(cosines, sines, coupling, cos_table, sin_table, pick, wave_cos, wave_sin):
     waves = wave_cos.shape[0]
     blocks = cos_table.shape[0] // waves
     tens = waves // 8
@@ -212,6 +190,7 @@
         return carry
 
     lax.fori_loop(0, blocks, body, 0)
+    one_hot(coupling, pick)
 
 
 def lanes_of(cells):
@@ -234,43 +213,39 @@
         first, middle, end = 2 * g * rows, (2 * g + 1) * rows, (2 * g + 2) * rows
         value = by_cos[first:middle] + by_sin[middle:end]
         if phase:
-            at = cosines.shape[0] - 4 + phase
+            at = cosines.shape[0] - 1
             imag = by_cos[middle:end] - by_sin[first:middle]
             value = cosines[at : at + 1, :] * value - sines[at : at + 1, :] * imag
         result = value if result is None else result + value
     return result
 
 
-def first_kernel(count, built, cosines, sines, coupling, *refs):
-    if built:
-        parts, (early, cos_table, sin_table, pick, legs, wave_cos, wave_sin) = (
-            refs[:count], refs[count:],
-        )
-        build_basis(cosines, sines, cos_table, sin_table, wave_cos, wave_sin)
-    else:
-        cos_table, sin_table = refs[:2]
-        parts, (early, pick, legs) = refs[2 : 2 + count], refs[2 + count :]
-    one_hot(coupling, pick)
+def first_kernel(
+    count, lats, share, last, band, cosines, sines, cos_table, sin_table, *refs
+):
+    parts, (early, outgoing, legs) = refs[:count], refs[count:]
     at = 0
     for part in parts[:-1]:
         legs[at : at + part.shape[0], :] = part[...]
         at += part.shape[0]
     groups = [legs[...].T, parts[-1][...].T]
     early[...] = synthesis(groups, (0, 1), cosines, sines, cos_table, sin_table)
+    outgoing[: 2 * lats, :] = early[: 2 * lats, :]
+    theirs = (band[0] ^ (1 << last)) * share
+    outgoing[2 * lats :, :] = jnp.zeros_like(outgoing[2 * lats :, :])
+    outgoing[2 * lats : 2 * lats + share, :] = early[pl.ds(2 * lats + theirs, share), :]
 
 
 def fourier_kernel(
-    lats, share, band, level, early, last, cosines, sines, cos_table, sin_table, pick, coupling,
-    grid, wind, hold,
+    lats, share, band, level, early, incoming, pick, coupling, grid, wind, hold
 ):
-    legs = last[...].T
-    middle = legs.shape[1] // 2
-    groups = [legs[:, :middle], legs[:, middle:]]
-    fields = early[...] + synthesis(groups, (2, 3), cosines, sines, cos_table, sin_table)
+    fields = early[: 2 * lats, :] + incoming[: 2 * lats, :]
+    mine = band[0] * share
+    grid[2] = early[pl.ds(2 * lats + mine, share), :] + incoming[2 * lats : 2 * lats + share, :]
     hold[...] = fields
-    for f in range(FIELDS):
-        grid[f] = hold[pl.ds(f * lats + band[0] * share, share), :]
-    speed = fields[: 2 * lats] * level[0]
+    for f in range(2):
+        grid[f] = hold[pl.ds(f * lats + mine, share), :]
+    speed = fields * level[0]
     top = speed.astype(jnp.bfloat16)
     low = (speed - top.astype(jnp.float32)).astype(jnp.bfloat16)
     pieces = [part[:, at : at + 128] for part in (top, low) for at in range(0, LON_W, 128)]
@@ -385,26 +360,23 @@
     in_hbm = functools.partial(
         pltpu.with_memory_space_constraint, memory_space=pltpu.MemorySpace.HBM
     )
-    in_vmem = functools.partial(
-        pltpu.with_memory_space_constraint, memory_space=pltpu.MemorySpace.VMEM
-    )
     half_shape = pltpu.MemorySpace.HBM((freqs, half, tile_rows, tile_cols), jnp.bfloat16)
     chunks = 3
-    low, high = pl.pallas_call(
+    far_own, near_own = pl.pallas_call(
         pack_kernel,
         out_shape=[half_shape] * 2,
         in_specs=[SMEM, SMEM, hbm],
         out_specs=[hbm] * 2,
         scratch_shapes=[
-            pltpu.VMEM((2, chunks, freqs // chunks, half, tile_rows, tile_cols), jnp.bfloat16),
+            pltpu.VMEM((2, freqs, half, tile_rows, tile_cols), jnp.bfloat16),
             pltpu.SemaphoreType.DMA((2, 2, chunks)),
         ],
         compiler_params=params(4),
         name="pack",
     )(band.reshape(1), lev.reshape(1), in_hbm(spectra))
-    low = lax.ppermute(low, "band", [(i, i ^ 1) for i in range(bands)])
+    low = lax.ppermute(far_own, "band", [(i, i ^ 1) for i in range(bands)])
     across = [(i, i + 1) for i in range(1, bands - 1, 2)]
-    high = lax.ppermute(high, "band", across + [(j, i) for i, j in across])
+    high = lax.ppermute(near_own, "band", across + [(j, i) for i, j in across])
 
     stacked = spectral.reshape(waves, 2 * FIELDS, n_total)
     legs = lax.dot_general(
@@ -417,105 +389,95 @@
     order = [0]
     parts = [legs]
     bits = bits_of(bands)
-    small = lats <= 32
-    for bit in bits:
-        if len(parts) == len(bits) and small:
-            rows = sum(part.shape[0] for part in parts)
-            together = pl.pallas_call(
-                join_kernel,
-                out_shape=pltpu.VMEM((rows, legs.shape[1]), jnp.bfloat16),
-                in_specs=[VMEM] * len(parts),
-                out_specs=VMEM,
-                compiler_params=params(2),
-                name="join",
-            )(*parts)
-        else:
-            together = jnp.concatenate(parts, axis=0) if len(parts) > 1 else legs
+    for bit in bits[:-1]:
+        together = jnp.concatenate(parts, axis=0) if len(parts) > 1 else legs
         parts = parts + [swapped(together, "band", bit)]
         if len(parts) < len(bits):
             order = order + [q ^ (1 << bit) for q in order]
 
-    def flipped(bit):
-        return (waves << bit) * (1 - 2 * (jnp.right_shift(band, bit) & 1))
-
-    count = len(parts) - 1
+    count = len(parts)
     total_rows = bands * waves // 4
     points = tile_rows * tile_cols
     columns = 2 * FIELDS * lats
     table = pltpu.VMEM((total_rows, LON_W), jnp.bfloat16)
-    pick_shape = jax.ShapeDtypeStruct((128, points), jnp.bfloat16)
-    fields_shape = jax.ShapeDtypeStruct((FIELDS * lats, LON_W), jnp.float32)
-    legs_scratch = pltpu.VMEM((total_rows, columns), jnp.bfloat16)
-    size = 10 if small else 36
-    built = waves % 16 == 0
+    pick_shape = pltpu.VMEM((128, points), jnp.bfloat16)
+    size = 10 if lats <= 32 else 36
     blocks = band ^ jnp.asarray(order, dtype=jnp.int32)
-    one, two = flipped(bits[-2]), flipped(bits[-1])
-    listed = [jnp.stack([one, two, one + two])]
-    if built:
+    listed = [((waves << bits[-2]) * (1 - 2 * (jnp.right_shift(band, bits[-2]) & 1))).reshape(1)]
+    if waves % 16 == 0:
         units = jnp.arange(8, dtype=jnp.int32)
         listed = [blocks * waves, 8 * jnp.arange(waves // 8, dtype=jnp.int32), units] + listed
     cos_rows, sin_rows = trig(jnp.concatenate(listed))
-    tables = []
-    if not built:
+    if waves % 16 == 0:
+        cos_table, sin_table, pick = pl.pallas_call(
+            basis_kernel,
+            out_shape=[table, table, pick_shape],
+            in_specs=[VMEM] * 3,
+            out_specs=[VMEM] * 3,
+            scratch_shapes=[pltpu.VMEM((waves, LON_W), jnp.float32)] * 2,
+            compiler_params=params(4),
+            name="basis",
+        )(cos_rows, sin_rows, coupling)
+    else:
         cos_table, sin_table = trig(
             (blocks[:, None] * waves + jnp.arange(waves, dtype=jnp.int32)).reshape(-1)
         )
-        tables = [cos_table.astype(jnp.bfloat16), -sin_table.astype(jnp.bfloat16)]
-    outs = pl.pallas_call(
-        functools.partial(first_kernel, count, built),
-        out_shape=[fields_shape] + [table, table] * built + [pick_shape],
-        in_specs=[VMEM] * (3 + len(tables) + count),
-        out_specs=[VMEM] * (2 + 2 * built),
-        scratch_shapes=[legs_scratch] + [pltpu.VMEM((waves, LON_W), jnp.float32)] * (2 * built),
+        cos_table, sin_table = cos_table.astype(jnp.bfloat16), -sin_table.astype(jnp.bfloat16)
+        pick = pl.pallas_call(
+            one_hot, out_shape=pick_shape, in_specs=[VMEM], out_specs=VMEM, name="pick"
+        )(coupling)
+    sent = -(-(2 * lats + share) // 8) * 8
+    early, outgoing = pl.pallas_call(
+        functools.partial(first_kernel, count, lats, share, bits[-1]),
+        out_shape=[
+            pltpu.VMEM((FIELDS * lats, LON_W), jnp.float32),
+            pltpu.VMEM((sent, LON_W), jnp.float32),
+        ],
+        in_specs=[SMEM] + [VMEM] * (4 + count),
+        out_specs=[VMEM] * 2,
+        scratch_shapes=[pltpu.VMEM((total_rows, columns), jnp.bfloat16)],
         compiler_params=params(size),
         name="first",
-    )(cos_rows, sin_rows, coupling, *tables, *parts[:-1])
-    early, pick = outs[0], outs[-1]
-    tables = tables or outs[1:3]
+    )(band.reshape(1), cos_rows, sin_rows, cos_table, sin_table, *parts)
+    incoming = swapped(outgoing, "band", bits[-1])
     grid, wind = pl.pallas_call(
         functools.partial(fourier_kernel, lats, share),
         out_shape=[
             jax.ShapeDtypeStruct((FIELDS, share, LON_W), jnp.float32),
             jax.ShapeDtypeStruct((2, tile_rows, tile_cols), jnp.float32),
         ],
-        in_specs=[SMEM, SMEM] + [VMEM] * 8,
+        in_specs=[SMEM, SMEM] + [VMEM] * 4,
         out_specs=[VMEM] * 2,
-        scratch_shapes=[pltpu.VMEM((FIELDS * lats, LON_W), jnp.float32)],
+        scratch_shapes=[pltpu.VMEM((2 * lats, LON_W), jnp.float32)],
         compiler_params=params(size),
         name="fourier",
-    )(
-        band.reshape(1), level_weights, early, in_vmem(parts[-1]) if small else parts[-1], cos_rows, sin_rows, *tables, pick, coupling
-    )
+    )(band.reshape(1), level_weights, early, incoming, pick, coupling)
     grid = jnp.transpose(grid, (1, 0, 2)).reshape(share, 1, FIELDS, LON_W)
 
     quarter = pairs // 2
     levels, here = lev.reshape(1), band.reshape(1)
-    own = in_hbm(spectra.reshape(freqs, pairs, 8, 128))
     half_state = pltpu.VMEM((freqs, quarter, 8, 128), jnp.float32)
-
     shifts = in_hbm(shift_matrix())
 
-    def advected(spectra_of, halo, flip):
-        whole = spectra_of.shape[1] == pairs
-        part = pltpu.VMEM((freqs, quarter, 8, 128), jnp.bfloat16)
+    def advected(own, halo, flip):
         tall = 16 * -(-quarter // 2) * freqs
         return pl.pallas_call(
             functools.partial(advect_kernel, directions, flip),
-            out_shape=[half_state, pltpu.VMEM((quarter, 8, 128), jnp.float32)] + [part] * whole,
-            in_specs=[SMEM] * 5 + [hbm if whole else VMEM] + [VMEM] * 2 + [hbm],
-            out_specs=[VMEM] * (2 + whole),
-            scratch_shapes=[part] * whole
-            + [
+            out_shape=[half_state, pltpu.VMEM((quarter, 8, 128), jnp.float32)],
+            in_specs=[SMEM] * 5 + [VMEM] * 3 + [hbm],
+            out_specs=[VMEM] * 2,
+            scratch_shapes=[
                 pltpu.VMEM((tall, STEPS * 128), jnp.bfloat16),
                 pltpu.VMEM((tall, 256), jnp.float32),
                 pltpu.VMEM((freqs, quarter, 8, 128), jnp.float32),
                 pltpu.VMEM(shifts.shape, shifts.dtype),
-                pltpu.SemaphoreType.DMA((3,)),
+                pltpu.SemaphoreType.DMA((1,)),
             ],
             compiler_params=params(12),
         )(
-            levels, here, courant, growth_rate, breaking, spectra_of,
-            in_vmem(halo.reshape(freqs, quarter, 8, 128)), land_sea, shifts,
+            levels, here, courant, growth_rate, breaking,
+            own.reshape(freqs, quarter, 8, 128), halo.reshape(freqs, quarter, 8, 128),
+            land_sea, shifts,
         )
 
     def over_lev(value):
@@ -527,9 +489,9 @@
         return parts
 
     winds = over_lev(wind)
-    near_damped, source, own = advected(own, low, 0)
+    near_damped, source = advected(near_own, low, 0)
     near_sources = over_lev(source)
-    far_damped, source = advected(own, high, 1)
+    far_damped, source = advected(far_own, high, 1)
     far_sources = over_lev(source)
     result = pl.pallas_call(
         functools.partial(result_kernel, directions, levs),

time: 45.5 us -> 44.2 us (0.971)
  Pallas kernels: 14.3 us -> 12.7 us
  waiting for transfers between devices: 10.7 us -> 11.2 us
    pallas_call x2, Pallas kernels: 8.31 us -> 7.11 us  [advected(): pl.pallas_call(functools.partial(advect_kernel, directions, flip), out_sh...]
    unnamed x15 -> x19, local copies, waits for them, and re-layouts: 2.3 us -> 3.27 us
    concatenate x1 -> x0, local copies, waits for them, and re-layouts: 0.73 us -> none  [on_device_(): cos_rows, sin_rows = trig(jnp.concatenate(listed))]
    ppermute x7, waiting for transfers between devices: 10.7 us -> 11.2 us  [swapped(): lax.ppermute(block, axis, [(i, i ^ 1 << apart) for i in range(count)])]
    iota x1, local copies, waits for them, and re-layouts: 0.51 us -> 0.01 us  [on_device_(): units = jnp.arange(8, dtype=jnp.int32)]
  transfers between devices with their start and end apart: 9 -> 9, of which waited for: 3 -> 3; matrix products, arithmetic and copies ran while one was open for 4% -> 1% of each run, Pallas kernels for 30% -> 27%
where the time goes in v6:
time: 44.2 us; the launch traced here: 43.9 us
  starting transfers between devices  13.3 us (30%)
  Pallas kernels  12.7 us (29%)
  waiting for transfers between devices  11.2 us (25%)
  local copies, waits for them, and re-layouts  3.51 us (8%)
  between operations  1.51 us (3%)
  matrix products  1.17 us (3%)
  other arithmetic  0.48 us (1%)
    ppermute x7, starting transfers between devices, swapped(): lax.ppermute(block, axis, [(i, i ^ 1 << apart) for i in range(count)])  11.8 us
    ppermute x7, waiting for transfers between devices, swapped(): lax.ppermute(block, axis, [(i, i ^ 1 << apart) for i in range(count)])  11.2 us
    pallas_call x2, Pallas kernels, advected(): pl.pallas_call(functools.partial(advect_kernel, directions, flip), out_sh...  7.11 us
    unnamed x19, local copies, waits for them, and re-layouts  3.27 us
    pallas_call x1, Pallas kernels, on_device_(): pl.pallas_call(pack_kernel, out_shape=[half_shape] * 2, in_specs=[SMEM, S...  1.91 us
    pallas_call x1, Pallas kernels, on_device_(): pl.pallas_call(functools.partial(result_kernel, directions, levs), out_sh...  1.68 us
    ppermute x1, starting transfers between devices, on_device_(): high = lax.ppermute(near_own, 'band', across + [(j, i) for i, j in across])  1.38 us
    dot_general x1, matrix products, on_device_(): lax.dot_general(stacked, legendre, (((2,), (2,)), ((0,), (0,))), preferre...  1.17 us
  transfers between devices with their start and end apart: 9, of which 3 were waited for; matrix products, arithmetic and copies ran while one was open for 1% of the time, Pallas kernels for 27%

profile of v6, /device:TPU:0, one launch (start us, length us, event | category | flops | bytes accessed | tf_op | source)
XLA Modules:
  0.0 43.9 jit_solution(13051452014803572852)
XLA Ops:
  0.6 0.0 copy-start
  0.7 1.6 %copy.15 = bf16[80,2,1,3,1280]{4,0,3,1,2:T(8,128)(2,1)S(1)} copy(bf16[80,2,1,3,1280]{4,1,3,2,0:T(2,128)(2,1)} %param.11) | data formatting | bytes 2457600 | tf_op args[0]
  2.2 0.7 %copy-done = bf16[80,16,1280]{2,1,0:T(8,128)(2,1)S(1)} copy-done((bf16[80,16,1280]{2,1,0:T(8,128)(2,1)S(1)}, bf16[80,16,1280]{2,1,0:T(8,128)(2,1)}, u32[]{:S(2)}) %copy-start) | copy-done | bytes 3276824
  2.9 1.2 %fusion.2 = bf16[80,6,16]{2,1,0:T(8,128)(2,1)S(1)} fusion(bf16[80,16,1280]{2,1,0:T(8,128)(2,1)S(1)} %copy-done, bf16[80,6,1280]{2,0,1:T(8,128)(2,1)S(1)} %bitcast.16), kind=kOutput, calls=%fused_computation.2 | convolution fusion | flops 19668480 | bytes 4520960 | tf_op jit(solution)/shard_map/dot_general | solution.py:382
  4.1 0.0 copy-start.7
  4.1 0.1 copy.17
  4.3 0.1 copy.18
  4.4 0.1 broadcast_multiply_fusion.refs_0_
  4.4 3.0 %collective-permute-start = (bf16[80,96]{1,0:T(8,128)(2,1)S(1)}, bf16[80,96]{1,0:T(8,128)(2,1)S(1)}, u32[]{:S(2)}, u32[]{:S(2)}) collective-permute-start(bf16[80,96]{1,0:T(8,128)(2,1)S(1)} %broadcast_multiply_fusion.refs_0_), channel_id=1, source_target_pairs={{0,2},{2,0},{4,6},{6,4},{8,10},{10,8},{12,14},{14,12},{16,18},{18,... | collective-permute-start | bytes 46088 | tf_op jit(solution)/shard_map/ppermute | solution.py:25
  7.4 1.9 %pack.1 = (bf16[18,18,4,128]{3,2,1,0:T(4,128)(2,1)}, bf16[18,18,4,128]{3,2,1,0:T(4,128)(2,1)}) custom-call(s32[1]{0:T(128)} %bitcast.band, s32[1]{0:T(128)} %bitcast.6.lev, bf16[18,36,4,128]{3,2,1,0:T(4,128)(2,1)} %spectra.1), custom_call_target="tpu_custom_call" | custom-call | tf_op jit(solution)/shard_map/pack/pallas_call | solution.py:365
  9.3 0.1 collective-permute-start.4
  9.4 1.4 %collective-permute-start.5 = (bf16[18,18,4,128]{3,2,1,0:T(4,128)(2,1)}, bf16[18,18,4,128]{3,2,1,0:T(4,128)(2,1)}, u32[]{:S(2)}, u32[]{:S(2)}) collective-permute-start(bf16[18,18,4,128]{3,2,1,0:T(4,128)(2,1)} %get-tuple-element.22), channel_id=1, source_target_pairs={{2,4},{6,8},{10,12},{14,16},{18,20},{22,24},{26,28},{4,2},{8,6},{1... | collective-permute-start | bytes 995336 | tf_op jit(solution)/shard_map/ppermute | solution.py:379
  10.8 0.0 collective-permute-done.refs_1_
  10.9 6.1 %collective-permute-start.1 = (bf16[160,96]{1,0:T(8,128)(2,1)S(1)}, bf16[160,96]{1,0:T(8,128)(2,1)S(1)}, u32[]{:S(2)}, u32[]{:S(2)}) collective-permute-start(bf16[160,96]{1,0:T(8,128)(2,1)S(1)} %pad_maximum_fusion.1), channel_id=1, source_target_pairs={{0,16},{2,18},{4,20},{6,22},{8,24},{10,26},{12,28},{14,30},{16,0},... | collective-permute-start | bytes 92168 | tf_op jit(solution)/shard_map/ppermute | solution.py:25
  16.9 0.1 pad_add_fusion
  17.0 8.3 %collective-permute-done.1.refs_2_ = bf16[160,96]{1,0:T(8,128)(2,1)S(1)} collective-permute-done((bf16[160,96]{1,0:T(8,128)(2,1)S(1)}, bf16[160,96]{1,0:T(8,128)(2,1)S(1)}, u32[]{:S(2)}, u32[]{:S(2)}) %collective-permute-start.1) | collective-permute-done | bytes 30752 | tf_op jit(solution)/shard_map/ppermute | solution.py:25
  25.3 2.1 %collective-permute-start.2 = (bf16[320,96]{1,0:T(8,128)(2,1)S(1)}, bf16[320,96]{1,0:T(8,128)(2,1)S(1)}, u32[]{:S(2)}, u32[]{:S(2)}) collective-permute-start(bf16[320,96]{1,0:T(8,128)(2,1)S(1)} %pad_maximum_fusion), channel_id=1, source_target_pairs={{0,8},{2,10},{4,12},{6,14},{8,0},{10,2},{12,4},{14,6},{16,24},{18,... | collective-permute-start | bytes 184328 | tf_op jit(solution)/shard_map/ppermute | solution.py:25
  27.4 0.3 fusion.9
  27.7 0.3 basis.1
  28.0 1.8 %collective-permute-done.2.refs_3_ = bf16[320,96]{1,0:T(8,128)(2,1)S(1)} collective-permute-done((bf16[320,96]{1,0:T(8,128)(2,1)S(1)}, bf16[320,96]{1,0:T(8,128)(2,1)S(1)}, u32[]{:S(2)}, u32[]{:S(2)}) %collective-permute-start.2) | collective-permute-done | bytes 61472 | tf_op jit(solution)/shard_map/ppermute | solution.py:25
  29.8 0.4 first.1
  30.2 0.1 collective-permute-start.3
  30.4 1.0 %copy-done.2 = bf16[18,18,4,128]{3,2,1,0:T(4,128)(2,1)S(1)} copy-done((bf16[18,18,4,128]{3,2,1,0:T(4,128)(2,1)S(1)}, bf16[18,18,4,128]{3,2,1,0:T(4,128)(2,1)}, u32[]{:S(2)}) %copy-start.2) | copy-done | bytes 331800
  31.3 3.6 %shard_map.130 = (f32[18,9,8,128]{3,2,1,0:T(8,128)S(1)}, f32[9,8,128]{2,1,0:T(8,128)S(1)}) custom-call(s32[1]{0:T(128)} %bitcast.6.lev, s32[1]{0:T(128)} %bitcast.band, f32[18]{0:T(128)S(1)} %copy-done.6, f32[18]{0:T(128)S(1)} %copy-done.5, f32[18]{0:T(128)S(1)} %copy-done.7, bf16[18,9,8,128]{3,2,1,0:T(8,128)(2,1)S(1)} %bitcast.15, ...), custom_call_target="tpu_custom_call" | custom-call | tf_op jit(solution)/shard_map/pallas_call | solution.py:464
  34.9 0.1 collective-permute-start.7
  35.0 3.6 %shard_map.131 = (f32[18,9,8,128]{3,2,1,0:T(8,128)S(1)}, f32[9,8,128]{2,1,0:T(8,128)S(1)}) custom-call(s32[1]{0:T(128)} %bitcast.6.lev, s32[1]{0:T(128)} %bitcast.band, f32[18]{0:T(128)S(1)} %copy-done.6, f32[18]{0:T(128)S(1)} %copy-done.5, f32[18]{0:T(128)S(1)} %copy-done.7, bf16[18,9,8,128]{3,2,1,0:T(8,128)(2,1)S(1)} %bitcast.14, ...), custom_call_target="tpu_custom_call" | custom-call | tf_op jit(solution)/shard_map/pallas_call | solution.py:464
  38.6 0.5 %collective-permute-start.8 = (f32[9,8,128]{2,1,0:T(8,128)S(1)}, f32[9,8,128]{2,1,0:T(8,128)S(1)}, u32[]{:S(2)}, u32[]{:S(2)}) collective-permute-start(f32[9,8,128]{2,1,0:T(8,128)S(1)} %get-tuple-element.28.refs_4_), channel_id=1, source_target_pairs={{0,1},{1,0},{2,3},{3,2},{4,5},{5,4},{6,7},{7,6},{8,9},{9,8},{10,11... | collective-permute-start | bytes 110600 | tf_op jit(solution)/shard_map/ppermute | solution.py:25
  39.8 0.6 %fourier.1 = (f32[3,1,512]{2,1,0:T(1,128)}, f32[2,4,128]{2,1,0:T(4,128)S(1)}) custom-call(s32[1]{0:T(128)} %bitcast.band, f32[1]{0:T(128)S(6)} %copy.24.level, f32[48,512]{1,0:T(8,128)S(1)} %get-tuple-element.18.early, f32[40,512]{1,0:T(8,128)S(1)} %collective-permute-done.3.incoming, bf16[128,512]{1,0:T(8,128)(2,1)S(1)} %get-tuple-element.20.pick, ...), custom_call_target="tpu_custom_call" | custom-call | tf_op jit(solution)/shard_map/fourier/pallas_call | solution.py:443
  40.4 0.0 collective-permute-start.6
  40.4 1.1 %collective-permute-done.6.refs_1_ = f32[2,4,128]{2,1,0:T(4,128)S(1)} collective-permute-done((f32[2,4,128]{2,1,0:T(4,128)S(1)}, f32[2,4,128]{2,1,0:T(4,128)S(1)}, u32[]{:S(2)}, u32[]{:S(2)}) %collective-permute-start.6) | collective-permute-done | bytes 4128 | tf_op jit(solution)/shard_map/ppermute | solution.py:25
  41.5 1.7 %result.1 = f32[18,18,8,128]{3,2,1,0:T(8,128)} custom-call(s32[1]{0:T(128)} %bitcast.band, f32[18]{0:T(128)S(1)} %copy-done.5, f32[18,9,8,128]{3,2,1,0:T(8,128)S(1)} %get-tuple-element.24.near, f32[18,9,8,128]{3,2,1,0:T(8,128)S(1)} %get-tuple-element.25.far, f32[2,4,128]{2,1,0:T(4,128)S(1)} %get-tuple-element.26.refs_0_, ...), custom_call_target="tpu_custom_call" | custom-call | tf_op jit(solution)/shard_map/result/pallas_call | solution.py:496
  43.3 0.6 %charnock.1 = f32[4,128]{1,0:T(4,128)} custom-call(s32[1]{0:T(128)} %bitcast.band, s32[4,128]{1,0:T(4,128)S(1)} %copy-done.3, f32[2,4,128]{2,1,0:T(4,128)S(1)} %get-tuple-element.26.refs_0_, f32[2,4,128]{2,1,0:T(4,128)S(1)} %collective-permute-done.6.refs_1_, f32[9,8,128]{2,1,0:T(8,128)S(1)} %get-tuple-element.27.refs_2_, ...), custom_call_target="tpu_custom_call" | custom-call | tf_op jit(solution)/shard_map/charnock/pallas_call | solution.py:508
  (25 shorter events, 0.1 us)
Async XLA Ops:
  0.6 2.3 %copy-start = (bf16[80,16,1280]{2,1,0:T(8,128)(2,1)S(1)}, bf16[80,16,1280]{2,1,0:T(8,128)(2,1)}, u32[]{:S(2)}) copy-start(bf16[80,16,1280]{2,1,0:T(8,128)(2,1)} %param.12) | copy-start | bytes 9830404
  2.9 7.9 %copy-start.8 = (s32[4]{0:T(128)S(1)}, s32[4]{0:T(128)}, u32[]{:S(2)}) copy-start(s32[4]{0:T(128)} %constant.42.clone) | copy-start | bytes 52
  2.9 24.7 %copy-start.4 = (s32[4,128]{1,0:T(4,128)S(1)}, s32[4,128]{1,0:T(4,128)}, u32[]{:S(2)}) copy-start(s32[4,128]{1,0:T(4,128)} %coupling.3) | copy-start | bytes 6148
  4.1 26.2 %copy-start.3 = (s32[4,128]{1,0:T(4,128)S(1)}, s32[4,128]{1,0:T(4,128)}, u32[]{:S(2)}) copy-start(s32[4,128]{1,0:T(4,128)} %land.5) | copy-start | bytes 6148
  4.1 26.2 %copy-start.5 = (f32[18]{0:T(128)S(1)}, f32[18]{0:T(128)}, u32[]{:S(2)}) copy-start(f32[18]{0:T(128)} %rate.5) | copy-start | bytes 220
  4.1 26.2 %copy-start.6 = (f32[18]{0:T(128)S(1)}, f32[18]{0:T(128)}, u32[]{:S(2)}) copy-start(f32[18]{0:T(128)} %courant.3) | copy-start | bytes 220
  4.1 26.2 %copy-start.7 = (f32[18]{0:T(128)S(1)}, f32[18]{0:T(128)}, u32[]{:S(2)}) copy-start(f32[18]{0:T(128)} %breaking.3) | copy-start | bytes 220
  4.4 6.4 %collective-permute-start = (bf16[80,96]{1,0:T(8,128)(2,1)S(1)}, bf16[80,96]{1,0:T(8,128)(2,1)S(1)}, u32[]{:S(2)}, u32[]{:S(2)}) collective-permute-start(bf16[80,96]{1,0:T(8,128)(2,1)S(1)} %broadcast_multiply_fusion.refs_0_), channel_id=1, source_target_pairs={{0,2},{2,0},{4,6},{6,4},{8,10},{10,8},{12,14},{14,12},{16,18},{18,... | collective-permute-start | bytes 46088 | tf_op jit(solution)/shard_map/ppermute | solution.py:25
  9.3 21.0 %collective-permute-start.4 = (bf16[18,18,4,128]{3,2,1,0:T(4,128)(2,1)}, bf16[18,18,4,128]{3,2,1,0:T(4,128)(2,1)}, u32[]{:S(2)}, u32[]{:S(2)}) collective-permute-start(bf16[18,18,4,128]{3,2,1,0:T(4,128)(2,1)} %get-tuple-element.23), channel_id=1, source_target_pairs={{0,2},{2,0},{4,6},{6,4},{8,10},{10,8},{12,14},{14,12},{16,18},{18,... | collective-permute-start | bytes 995336 | tf_op jit(solution)/shard_map/ppermute | solution.py:377
  9.4 25.5 %collective-permute-start.5 = (bf16[18,18,4,128]{3,2,1,0:T(4,128)(2,1)}, bf16[18,18,4,128]{3,2,1,0:T(4,128)(2,1)}, u32[]{:S(2)}, u32[]{:S(2)}) collective-permute-start(bf16[18,18,4,128]{3,2,1,0:T(4,128)(2,1)} %get-tuple-element.22), channel_id=1, source_target_pairs={{2,4},{6,8},{10,12},{14,16},{18,20},{22,24},{26,28},{4,2},{8,6},{1... | collective-permute-start | bytes 995336 | tf_op jit(solution)/shard_map/ppermute | solution.py:379
  10.8 24.2 %copy-start.1 = (bf16[18,18,4,128]{3,2,1,0:T(4,128)(2,1)S(1)}, bf16[18,18,4,128]{3,2,1,0:T(4,128)(2,1)}, u32[]{:S(2)}) copy-start(bf16[18,18,4,128]{3,2,1,0:T(4,128)(2,1)} %get-tuple-element.23) | copy-start | bytes 995332
  10.9 14.4 %collective-permute-start.1 = (bf16[160,96]{1,0:T(8,128)(2,1)S(1)}, bf16[160,96]{1,0:T(8,128)(2,1)S(1)}, u32[]{:S(2)}, u32[]{:S(2)}) collective-permute-start(bf16[160,96]{1,0:T(8,128)(2,1)S(1)} %pad_maximum_fusion.1), channel_id=1, source_target_pairs={{0,16},{2,18},{4,20},{6,22},{8,24},{10,26},{12,28},{14,30},{16,0},... | collective-permute-start | bytes 92168 | tf_op jit(solution)/shard_map/ppermute | solution.py:25
  25.3 4.5 %collective-permute-start.2 = (bf16[320,96]{1,0:T(8,128)(2,1)S(1)}, bf16[320,96]{1,0:T(8,128)(2,1)S(1)}, u32[]{:S(2)}, u32[]{:S(2)}) collective-permute-start(bf16[320,96]{1,0:T(8,128)(2,1)S(1)} %pad_maximum_fusion), channel_id=1, source_target_pairs={{0,8},{2,10},{4,12},{6,14},{8,0},{10,2},{12,4},{14,6},{16,24},{18,... | collective-permute-start | bytes 184328 | tf_op jit(solution)/shard_map/ppermute | solution.py:25
  30.2 9.5 %collective-permute-start.3 = (f32[40,512]{1,0:T(8,128)S(1)}, f32[40,512]{1,0:T(8,128)S(1)}, u32[]{:S(2)}, u32[]{:S(2)}) collective-permute-start(f32[40,512]{1,0:T(8,128)S(1)} %get-tuple-element.19), channel_id=1, source_target_pairs={{0,4},{2,6},{4,0},{6,2},{8,12},{10,14},{12,8},{14,10},{16,20},{18,... | collective-permute-start | bytes 245768 | tf_op jit(solution)/shard_map/ppermute | solution.py:25
  30.4 1.0 %copy-start.2 = (bf16[18,18,4,128]{3,2,1,0:T(4,128)(2,1)S(1)}, bf16[18,18,4,128]{3,2,1,0:T(4,128)(2,1)}, u32[]{:S(2)}) copy-start(bf16[18,18,4,128]{3,2,1,0:T(4,128)(2,1)} %get-tuple-element.22) | copy-start | bytes 995332
  34.9 8.4 %collective-permute-start.7 = (f32[9,8,128]{2,1,0:T(8,128)S(1)}, f32[9,8,128]{2,1,0:T(8,128)S(1)}, u32[]{:S(2)}, u32[]{:S(2)}) collective-permute-start(f32[9,8,128]{2,1,0:T(8,128)S(1)} %get-tuple-element.27.refs_2_), channel_id=1, source_target_pairs={{0,1},{1,0},{2,3},{3,2},{4,5},{5,4},{6,7},{7,6},{8,9},{9,8},{10,11... | collective-permute-start | bytes 110600 | tf_op jit(solution)/shard_map/ppermute | solution.py:25
  38.6 4.7 %collective-permute-start.8 = (f32[9,8,128]{2,1,0:T(8,128)S(1)}, f32[9,8,128]{2,1,0:T(8,128)S(1)}, u32[]{:S(2)}, u32[]{:S(2)}) collective-permute-start(f32[9,8,128]{2,1,0:T(8,128)S(1)} %get-tuple-element.28.refs_4_), channel_id=1, source_target_pairs={{0,1},{1,0},{2,3},{3,2},{4,5},{5,4},{6,7},{7,6},{8,9},{9,8},{10,11... | collective-permute-start | bytes 110600 | tf_op jit(solution)/shard_map/ppermute | solution.py:25
  40.4 1.2 %collective-permute-start.6 = (f32[2,4,128]{2,1,0:T(4,128)S(1)}, f32[2,4,128]{2,1,0:T(4,128)S(1)}, u32[]{:S(2)}, u32[]{:S(2)}) collective-permute-start(f32[2,4,128]{2,1,0:T(4,128)S(1)} %get-tuple-element.26.refs_0_), channel_id=1, source_target_pairs={{0,1},{1,0},{2,3},{3,2},{4,5},{5,4},{6,7},{7,6},{8,9},{9,8},{10,11... | collective-permute-start | bytes 12296 | tf_op jit(solution)/shard_map/ppermute | solution.py:25
